TPU v7x, 256 devices: a whole 4x4x8 slice. The times are simulated.
256 devices in a mesh: wire: 64 (over z, y, core), col: 4 (over x).
Axes of the slice: x: 4, y: 4, z: 8, core: 2. Of those that a mesh axis runs over, the one named last changes fastest.
Arguments:
- search: float32 [196608, 384], P('wire', 'col')
- block_values: float32 [196608, 256], P('wire'), may hold values from -0.375 to 0.375
- block_cols: int32 [3072, 4], P('wire'), may hold values from 0 to 3071, as said below
- ritz: float32 [384, 128], replicated, may hold values from -0.3125 to 0.3125
Outputs:
- new_modes: float32 [196608, 128], P('wire', 'col')
- residual: float32 [196608, 128], P('wire', 'col')
- theta: float32 [128], P('col')
- gram_stiff: float32 [384, 384], P(None, 'col')
- gram_mass: float32 [384, 384], P(None, 'col')
Inputs may be any that keep to these rules, and one draw needn't show every extreme that they name: Block rows are in groups of 48, b in group g = b // 48. block_cols[b, 0] = b. Column 1 names a block row of group g. For even b, column 2 names a block row of group g + 1 and column 3 one of group g + 2; for odd b, groups g - 1 and g - 2; groups counted around the loop of all groups.
All inputs are finite; a program needn't handle non-finite values.
Results may differ from a plain program's by a relative error of at most 0.0003.
Values sent between devices are 32-bit elements; how exact they have to be, the bound alone decides.
No kernel may reach another device: no remote copies, remote signals or barrier semaphores. Data moves between devices by JAX's collectives and lax.ppermute only.
A program may use at most 64 MiB of HBM per device.

v0:
```python
import jax
import jax.numpy as jnp
from jax import lax
from jax.experimental import pallas as pl
from jax.experimental.pallas import tpu as pltpu
from jax.sharding import Mesh, PartitionSpec as P


RING = ("zl", "y", "core")
WIRE = ("zh", "zl", "y", "core")
BLOCK = 64
PARTS = 16
TILES = 5
PAIRS = 4
LANES = 128
F32 = jnp.float32
NN = (((1,), (0,)), ((), ()))
NT = (((1,), (1,)), ((), ()))
VMEM = pl.BlockSpec(memory_space=pltpu.VMEM)
SMEM = pl.BlockSpec(memory_space=pltpu.SMEM)


def shifted(array, axis, by):
    length = lax.axis_size(axis)
    return lax.ppermute(array, axis, [(i, (i + by) % length) for i in range(length)])


def split(x):
    high = x.astype(jnp.bfloat16)
    return high, (x - high.astype(F32)).astype(jnp.bfloat16)


def dot3(a, b, dims):
    (ah, al), (bh, bl) = a, b
    one = lambda x, y: lax.dot_general(x, y, dims, preferred_element_type=F32)
    return one(ah, bh) + (one(ah, bl) + one(al, bh))


def low_half(shape):
    return lax.broadcasted_iota(jnp.int32, shape, 1) < BLOCK


def block_at(ref, index, half):
    tile = ref[:, pl.ds(pl.multiple_of(index // 2 * LANES, LANES), LANES)]
    return jnp.where(index % 2 == half, tile, pltpu.roll(tile, BLOCK, 1))


def pack_kernel(base, prev2, next2, st, to_prev2, to_next2):
    low = low_half((st.shape[0], LANES))

    def step(m, carry):
        for asked, parity, out in ((prev2, 0, to_prev2), (next2, 1, to_next2)):
            first = block_at(st, asked[3, 4 * m + parity] - base[0], 0)
            second = block_at(st, asked[3, 4 * m + 2 + parity] - base[0], 1)
            out[:, pl.ds(pl.multiple_of(m * LANES, LANES), LANES)] = jnp.where(low, first, second)
        return carry

    lax.fori_loop(0, to_prev2.shape[1] // LANES, step, 0)


def image_kernel(base, cols, st, up1, down1, up2, down2, values, image):
    m = pl.program_id(0)
    width = st.shape[0]
    pairs = values.shape[0] // LANES
    low = low_half((width, LANES))
    flip = lambda x: pltpu.roll(x, BLOCK, 1)
    for h in range(pairs):
        tile = m * pairs + h
        row = 2 * tile
        own = st[:, pl.ds(pl.multiple_of(tile * LANES, LANES), LANES)]
        left = []
        for q, (far1, far2, at) in enumerate(((up1, up2, 1), (down1, down2, 2))):
            mine = own if q == 0 else flip(own)
            near = block_at(st, cols[1, row + q] - base[0], 1)
            first = block_at(far1, cols[2, row + q] - base[at], 0)
            second = far2[:, h // 2 * LANES : (h // 2 + 1) * LANES]
            second = flip(second) if h % 2 == 0 else second
            left.append(
                jnp.concatenate([jnp.where(low, mine, near), jnp.where(low, first, second)], axis=1)
            )
        part = dot3(
            split(jnp.concatenate(left, axis=0)),
            split(values[h * LANES : (h + 1) * LANES, :]),
            NT,
        )
        image[:, h * LANES : (h + 1) * LANES] = 4.0 * own + jnp.where(low, part[:width], part[width:])


def both_rows(ritz, c, width):
    mine = ritz[pl.ds(pl.multiple_of(c * width, 8), width), :]
    nothing = jnp.zeros_like(mine)
    return split(
        jnp.concatenate(
            [jnp.concatenate([mine, nothing], axis=1), jnp.concatenate([nothing, mine], axis=1)], axis=0
        )
    )


def quotient_terms(piece, both, ritz, start):
    full = ritz[pl.ds(start, piece.shape[0]), :]
    left = dot3(split(piece), both, NN)
    return jnp.sum(left * jnp.concatenate([full, full], axis=1), axis=0, keepdims=True)


def gram_kernel(col, image, st, before, after, ritz, gram, terms):
    c = col[0]
    width = st.shape[0]
    right = split(jnp.concatenate([image[...], st[...]], axis=0))
    both = both_rows(ritz, c, width)
    total = jnp.zeros(terms.shape, F32)
    for i, (piece, by) in enumerate(((st, 0), (before, 3), (after, 1))):
        block = dot3(split(piece[...]), right, NT)
        gram[i] = block
        total = total + quotient_terms(block, both, ritz, pl.multiple_of((c + by) % 4 * width, 8))
    terms[...] = total


def late_kernel(col, gram3, terms3, opp_a, opp_b, image, st, ritz, payload, terms, gram):
    c = col[0]
    width = st.shape[0]
    right = split(jnp.concatenate([image[...], st[...]], axis=0))
    far = dot3(split(jnp.concatenate([opp_a[...], opp_b[...]], axis=0)), right, NT)
    for piece, by in ((gram3[0], 0), (gram3[1], 3), (gram3[2], 1), (far, 2)):
        gram[pl.ds(pl.multiple_of((c + by) % 4 * width, 8), width), :] = piece
    start = pl.multiple_of((c + 2) % 4 * width, 8)
    sums = terms3[...] + quotient_terms(far, both_rows(ritz, c, width), ritz, start)
    terms[...] = jnp.zeros_like(terms)
    terms[0:1, :] = sums[:, :LANES]
    terms[1:2, :] = sums[:, LANES:]
    turned = gram[...].T
    for t in range(PARTS * TILES):
        k, at = t // TILES, t % TILES * 8
        i, j = t // 3 * 8, t % 3 * LANES
        if i < turned.shape[0]:
            payload[k, at : at + 8, :] = turned[i : i + 8, j : j + LANES]
        else:
            payload[k, at : at + 8, :] = jnp.zeros((8, LANES), F32)


def modes_kernel(own, before, after, opp_a, opp_b, coef, modes):
    opp = jnp.concatenate([opp_a[...], opp_b[...]], axis=0)
    modes[...] = (
        dot3(split(coef[0]), split(own[...]), NN)
        + dot3(split(coef[1]), split(before[...]), NN)
        + dot3(split(coef[2]), split(after[...]), NN)
        + dot3(split(coef[3]), split(opp), NN)
    )


def image_part_kernel(image, coef, own, after, opp, before):
    right = split(image[...])
    for i, out in enumerate((own, after, opp, before)):
        out[...] = dot3(split(coef[i]), right, NN)


def final_kernel(col, parts, modes, own, from_prev, from_next, stiff, mass, theta, residual):
    total = jnp.float32(196608.0)
    terms = parts[0, 8 * TILES :, :]
    for k in range(1, PARTS):
        terms = terms + parts[k, 8 * TILES :, :]
    quotient = terms[0:1, :] / terms[1:2, :]
    shape = (modes.shape[0], LANES)
    here = lax.broadcasted_iota(jnp.int32, shape, 1) == (
        lax.broadcasted_iota(jnp.int32, shape, 0) + col[0] * shape[0]
    )
    column = jnp.sum(jnp.where(here, jnp.broadcast_to(quotient, shape), 0.0), axis=1, keepdims=True)
    theta[...] = column
    residual[...] = own[...] + from_prev[...] + from_next[...] - column * modes[...]
    width = stiff.shape[0]
    for t in range(2 * width // 8 * 3):
        k, at = t // TILES, t % TILES * 8
        i, j = t // 3 * 8, t % 3 * LANES
        out = stiff if i < width else mass
        out[i % width : i % width + 8, j : j + LANES] = parts[k, at : at + 8, :] / total


def call(kernel, shapes, in_specs, **kwargs):
    many = isinstance(shapes, list)
    out = [jax.ShapeDtypeStruct(s, F32) for s in (shapes if many else [shapes])]
    specs = kwargs.pop("out_specs", [VMEM] * len(out))
    return pl.pallas_call(
        kernel,
        out_shape=out if many else out[0],
        in_specs=in_specs,
        out_specs=specs if many else specs[0],
        **kwargs,
    )


def spread_out(part):
    return jnp.broadcast_to(part[None], (PARTS,) + part.shape)


def shards(search, values, block_cols, ritz):
    rows, width = search.shape
    blk = block_cols.shape[0]
    modes = ritz.shape[1] // 4
    half = width // 2
    c = lax.axis_index("col")
    w = lax.axis_index(WIRE)
    groups = lax.axis_size(WIRE)
    col = jnp.reshape(c, (1,)).astype(jnp.int32)
    base = (jnp.stack([w, (w + 1) % groups, (w + groups - 1) % groups]) * blk).astype(jnp.int32)
    st = search.T
    cols = block_cols.T

    prev2 = shifted(cols, WIRE, 2)
    next2 = shifted(cols, WIRE, -2)
    before = shifted(st, "col", 1)
    after = shifted(st, "col", -1)
    up1 = shifted(st, WIRE, -1)
    down1 = shifted(st, WIRE, 1)

    packed = call(pack_kernel, [(width, rows // 2)] * 2, [SMEM] * 3 + [VMEM])(base, prev2, next2, st)
    up2 = shifted(packed[0], WIRE, -2)
    down2 = shifted(packed[1], WIRE, 2)

    opp_a = shifted(before[:half], "col", 1)
    opp_b = shifted(after[half:], "col", -1)

    mine = lax.dynamic_slice_in_dim(ritz, c * modes, modes, 1).T
    coef = jnp.stack(
        [lax.dynamic_slice_in_dim(mine, (c + by) % 4 * width, width, 1) for by in (0, 3, 1, 2)]
    )
    ours = lax.dynamic_slice_in_dim(ritz, c * width, width, 0).T
    send = jnp.stack(
        [lax.dynamic_slice_in_dim(ours, (c + by) % 4 * modes, modes, 0) for by in range(4)]
    )

    tile = lambda n: pl.BlockSpec((width, n), lambda m: (0, m))
    whole = pl.BlockSpec((width, rows), lambda m: (0, 0))
    image = call(
        image_kernel,
        (width, rows),
        [SMEM, SMEM, whole, whole, whole]
        + [tile(PAIRS // 2 * LANES)] * 2
        + [pl.BlockSpec((PAIRS * LANES, values.shape[1]), lambda m: (m, 0))],
        out_specs=[tile(PAIRS * LANES)],
        grid=(rows // (PAIRS * LANES),),
    )(base, cols, st, up1, down1, up2, down2, values)

    gram3, terms3 = call(
        gram_kernel, [(3, width, 2 * width), (1, 2 * LANES)], [SMEM] + [VMEM] * 5
    )(col, image, st, before, after, ritz)

    payload, terms = call(
        late_kernel,
        [(PARTS, 8 * TILES, LANES), (8, LANES)],
        [SMEM] + [VMEM] * 7,
        scratch_shapes=[pltpu.VMEM((4 * width, 2 * width), F32)],
    )(col, gram3, terms3, opp_a, opp_b, image, st, ritz)

    got = lax.all_to_all(payload, RING, 0, 0, tiled=True)
    around = [shifted(terms, "col", by) for by in (1, 2, 3)]
    held, opp_a, opp_b, payload = lax.optimization_barrier((image, opp_a, opp_b, payload))
    part_own, part_after, part_opp, part_before = call(
        image_part_kernel, [(modes, rows)] * 4, [VMEM] * 2
    )(held, send)
    cut = rows // 2
    from_a = shifted(part_opp[:, :cut], "col", 1)
    from_b = shifted(part_opp[:, cut:], "col", -1)
    right = jnp.concatenate([part_after[:, :cut] + from_a, part_after[:, cut:]], axis=1)
    left = jnp.concatenate([part_before[:, :cut], part_before[:, cut:] + from_b], axis=1)
    from_prev = shifted(right, "col", 1)
    from_next = shifted(left, "col", -1)
    new_modes = call(modes_kernel, (modes, rows), [VMEM] * 6)(st, before, after, opp_a, opp_b, coef)

    part = jnp.concatenate(
        [jnp.sum(got, axis=0), terms + around[0] + around[1] + around[2]], axis=0
    )
    part = jnp.broadcast_to(part[None], (4,) + part.shape)
    part = lax.all_to_all(part, "zh", 0, 0, tiled=True)
    part = jnp.sum(part, axis=0)
    parts = lax.all_to_all(spread_out(part), RING, 0, 0, tiled=True)

    stiff, mass, theta, residual = call(
        final_kernel,
        [(width, 4 * width), (width, 4 * width), (modes, 1), (modes, rows)],
        [SMEM] + [VMEM] * 5,
    )(col, parts, new_modes, part_own, from_prev, from_next)
    return (new_modes.T, residual.T, theta[:, 0], stiff.T, mass.T)


def solution(mesh):
    mesh = Mesh(mesh.devices.reshape(4, 2, 4, 2, 4), WIRE + ("col",))
    return jax.shard_map(
        shards,
        mesh=mesh,
        in_specs=(P(WIRE, "col"), P(WIRE, None), P(WIRE, None), P()),
        out_specs=(P(WIRE, "col"), P(WIRE, "col"), P("col"), P(None, "col"), P(None, "col")),
        check_vma=False,
    )
```

profile of v0, /device:TPU:1, one launch (start us, length us, event | category | flops | bytes accessed | tf_op | source)
XLA Modules:
  0.0 134.1 jit_solution(14480021723154611991)
XLA Ops:
  0.6 3.4 %collective-permute-start.1 = (f32[96,3072]{1,0:T(8,128)}, f32[96,3072]{1,0:T(8,128)S(1)}, u32[]{:S(2)}, u32[]{:S(2)}) collective-permute-start(f32[96,3072]{1,0:T(8,128)} %bitcast.34), channel_id=1, source_target_pairs={{0,3},{1,0},{2,1},{3,2},{4,7},{5,4},{6,5},{7,6},{8,11},{9,8},{10,9... | collective-permute-start | bytes 3538952 | tf_op jit(solution)/shard_map/ppermute | solution.py:25
  4.0 8.0 %collective-permute-start.5 = (s32[4,48]{1,0:T(4,128)}, s32[4,48]{1,0:T(4,128)S(1)}, u32[]{:S(2)}, u32[]{:S(2)}) collective-permute-start(s32[4,48]{1,0:T(4,128)} %bitcast.52), channel_id=1, source_target_pairs={{0,248},{4,252},{8,0},{12,4},{16,8},{20,12},{24,16},{28,20},{32,24... | collective-permute-start | bytes 2312 | tf_op jit(solution)/shard_map/ppermute | solution.py:25
  12.0 0.9 collective-permute-done.5.next2
  13.0 1.8 %collective-permute-start.2 = (f32[96,3072]{1,0:T(8,128)}, f32[96,3072]{1,0:T(8,128)}, u32[]{:S(2)}, u32[]{:S(2)}) collective-permute-start(f32[96,3072]{1,0:T(8,128)} %bitcast.37), channel_id=1, source_target_pairs={{0,252},{4,0},{8,4},{12,8},{16,12},{20,16},{24,20},{28,24},{32,28}... | collective-permute-start | bytes 3538952 | tf_op jit(solution)/shard_map/ppermute | solution.py:25
  15.4 2.6 %collective-permute-done.4.prev2 = s32[4,48]{1,0:T(4,128)S(1)} collective-permute-done((s32[4,48]{1,0:T(4,128)}, s32[4,48]{1,0:T(4,128)S(1)}, u32[]{:S(2)}, u32[]{:S(2)}) %collective-permute-start.4) | collective-permute-done | bytes 800 | tf_op jit(solution)/shard_map/ppermute | solution.py:25
  18.6 3.9 %shard_map.83 = (f32[96,1536]{1,0:T(8,128)}, f32[96,1536]{1,0:T(8,128)}) custom-call(s32[3]{0:T(128)} %add_multiply_fusion.base, s32[4,48]{1,0:T(4,128)} %copy-done.12, s32[4,48]{1,0:T(4,128)} %copy-done.11, f32[96,3072]{1,0:T(8,128)} %bitcast.38), custom_call_target="tpu_custom_call" | custom-call | tf_op jit(solution)/shard_map/pallas_call | solution.py:214
  22.5 2.7 %collective-permute-start.6 = (f32[96,1536]{1,0:T(8,128)}, f32[96,1536]{1,0:T(8,128)S(1)}, u32[]{:S(2)}, u32[]{:S(2)}) collective-permute-start(f32[96,1536]{1,0:T(8,128)} %get-tuple-element.22), channel_id=1, source_target_pairs={{0,248},{4,252},{8,0},{12,4},{16,8},{20,12},{24,16},{28,20},{32,24... | collective-permute-start | bytes 1769480 | tf_op jit(solution)/shard_map/ppermute | solution.py:25
  25.2 3.8 %collective-permute-done.1.after = f32[96,3072]{1,0:T(8,128)S(1)} collective-permute-done((f32[96,3072]{1,0:T(8,128)}, f32[96,3072]{1,0:T(8,128)S(1)}, u32[]{:S(2)}, u32[]{:S(2)}) %collective-permute-start.1) | collective-permute-done | bytes 1179680 | tf_op jit(solution)/shard_map/ppermute | solution.py:25
  29.0 1.3 collective-permute-start.7
  31.1 1.0 collective-permute-done.before
  32.1 2.3 %collective-permute-start.9 = (f32[48,3072]{1,0:T(8,128)}, f32[48,3072]{1,0:T(8,128)S(1)}, u32[]{:S(2)}, u32[]{:S(2)}) collective-permute-start(f32[48,3072]{1,0:T(8,128)} %slice.33), channel_id=1, source_target_pairs={{0,3},{1,0},{2,1},{3,2},{4,7},{5,4},{6,5},{7,6},{8,11},{9,8},{10,9... | collective-permute-start | bytes 1769480 | tf_op jit(solution)/shard_map/ppermute | solution.py:25
  35.3 3.3 %collective-permute-done.6.up2 = f32[96,1536]{1,0:T(8,128)S(1)} collective-permute-done((f32[96,1536]{1,0:T(8,128)}, f32[96,1536]{1,0:T(8,128)S(1)}, u32[]{:S(2)}, u32[]{:S(2)}) %collective-permute-start.6) | collective-permute-done | bytes 589856 | tf_op jit(solution)/shard_map/ppermute | solution.py:25
  38.6 0.9 copy-done.6
  41.1 8.4 %collective-permute-done.7.down2 = f32[96,1536]{1,0:T(8,128)} collective-permute-done((f32[96,1536]{1,0:T(8,128)}, f32[96,1536]{1,0:T(8,128)}, u32[]{:S(2)}, u32[]{:S(2)}) %collective-permute-start.7) | collective-permute-done | bytes 589856 | tf_op jit(solution)/shard_map/ppermute | solution.py:25
  49.5 8.3 %shard_map.84.image = f32[96,3072]{1,0:T(8,128)} custom-call(s32[3]{0:T(128)} %add_multiply_fusion.base, s32[4,48]{1,0:T(4,128)} %bitcast.54, f32[96,3072]{1,0:T(8,128)} %bitcast.39, f32[96,3072]{1,0:T(8,128)} %collective-permute-done.2.up1, f32[96,3072]{1,0:T(8,128)} %collective-permute-done.3.down1, f32[96,1536]{1,0:T(8,128)} %copy-done.6, ...), custom_call_target="tpu_custom_call" | custom-call | tf_op jit(solution)/shard_map/pallas_call | solution.py:232
  57.8 8.6 %shard_map.85 = (f32[3,96,192]{2,1,0:T(8,128)}, f32[1,256]{1,0:T(1,128)}) custom-call(s32[1]{0:T(128)} %bitcast.5.col, f32[96,3072]{1,0:T(8,128)} %shard_map.84.image, f32[96,3072]{1,0:T(8,128)} %bitcast.40, f32[96,3072]{1,0:T(8,128)} %copy-done.1, f32[96,3072]{1,0:T(8,128)} %copy-done, f32[384,128]{1,0:T(8,128)} %ritz.3), custom_call_target="tpu_custom_call" | custom-call | tf_op jit(solution)/shard_map/pallas_call | solution.py:242
  67.4 4.3 %shard_map.86 = (f32[16,40,128]{2,1,0:T(8,128)}, f32[8,128]{1,0:T(8,128)}) custom-call(s32[1]{0:T(128)} %bitcast.5.col, f32[3,96,192]{2,1,0:T(8,128)} %get-tuple-element.24.gram3, f32[1,256]{1,0:T(1,128)} %get-tuple-element.25.terms3, f32[48,3072]{1,0:T(8,128)} %copy-done.4, f32[48,3072]{1,0:T(8,128)} %copy-done.3, f32[96,3072]{1,0:T(8,128)} %shard_map.84.image, ...), custom_call_target="tpu_custom_call" | custom-call | tf_op jit(solution)/shard_map/pallas_call | solution.py:246
  71.7 3.3 %collective-permute-start.12 = (f32[8,128]{1,0:T(8,128)}, f32[8,128]{1,0:T(8,128)S(1)}, u32[]{:S(2)}, u32[]{:S(2)}) collective-permute-start(f32[8,128]{1,0:T(8,128)} %get-tuple-element.29), channel_id=1, source_target_pairs={{0,3},{1,0},{2,1},{3,2},{4,7},{5,4},{6,5},{7,6},{8,11},{9,8},{10,9... | collective-permute-start | bytes 12296 | tf_op jit(solution)/shard_map/ppermute | solution.py:25
  75.6 6.0 %all-to-all-start = ((f32[16,40,128]{2,1,0:T(8,128)}), f32[16,40,128]{2,1,0:T(8,128)S(1)}, u32[]{:S(2)}, u32[]{:S(2)}) async-start(f32[16,40,128]{2,1,0:T(8,128)} %get-tuple-element.26), calls=%async_computation | async-start | bytes 655360 | tf_op jit(solution)/shard_map/all_to_all | solution.py:253
  81.6 3.1 %shard_map.88 = (f32[32,3072]{1,0:T(8,128)}, f32[32,3072]{1,0:T(8,128)}, f32[32,3072]{1,0:T(8,128)}, f32[32,3072]{1,0:T(8,128)}) custom-call(f32[96,3072]{1,0:T(8,128)} %shard_map.84.image, f32[4,32,96]{2,1,0:T(8,128)} %pad_maximum_fusion.3.coef), custom_call_target="tpu_custom_call" | custom-call | tf_op jit(solution)/shard_map/pallas_call | solution.py:256
  84.7 1.0 fusion.1
  85.7 2.2 %collective-permute-start.15 = (f32[32,1536]{1,0:T(8,128)S(1)}, f32[32,1536]{1,0:T(8,128)S(1)}, u32[]{:S(2)}, u32[]{:S(2)}) collective-permute-start(f32[32,1536]{1,0:T(8,128)S(1)} %get-tuple-element.41), channel_id=1, source_target_pairs={{0,3},{1,0},{2,1},{3,2},{4,7},{5,4},{6,5},{7,6},{8,11},{9,8},{10,9... | collective-permute-start | bytes 589832 | tf_op jit(solution)/shard_map/ppermute | solution.py:25
  88.3 6.8 %collective-permute-done.13 = f32[32,1536]{1,0:T(8,128)S(1)} collective-permute-done((f32[32,1536]{1,0:T(8,128)S(1)}, f32[32,1536]{1,0:T(8,128)S(1)}, u32[]{:S(2)}, u32[]{:S(2)}) %collective-permute-start.13) | collective-permute-done | bytes 196640 | tf_op jit(solution)/shard_map/ppermute | solution.py:25
  95.1 1.1 slice_add_fusion.1
  97.0 4.9 %all-to-all-start.1 = ((f32[4,48,128]{2,1,0:T(8,128)}), f32[4,48,128]{2,1,0:T(8,128)S(1)}, u32[]{:S(2)}, u32[]{:S(2)}) async-start(f32[4,48,128]{2,1,0:T(8,128)} %broadcast_in_dim.4), calls=%async_computation.1 | async-start | bytes 196608 | tf_op jit(solution)/shard_map/all_to_all | solution.py:272
  102.0 7.4 %all-to-all-done.1 = f32[4,48,128]{2,1,0:T(8,128)S(1)} async-done(((f32[4,48,128]{2,1,0:T(8,128)}), f32[4,48,128]{2,1,0:T(8,128)S(1)}, u32[]{:S(2)}, u32[]{:S(2)}) %all-to-all-start.1) | async-done | bytes 98336 | tf_op jit(solution)/shard_map/all_to_all | solution.py:272
  110.2 8.0 %all-to-all-start.2 = ((f32[16,48,128]{2,1,0:T(8,128)}), f32[16,48,128]{2,1,0:T(8,128)S(1)}, u32[]{:S(2)}, u32[]{:S(2)}) async-start(f32[16,48,128]{2,1,0:T(8,128)} %broadcast_in_dim.5), calls=%async_computation.2 | async-start | bytes 786432 | tf_op jit(solution)/shard_map/all_to_all | solution.py:274
  118.3 2.8 %collective-permute-start.16 = (f32[32,3072]{1,0:T(8,128)S(1)}, f32[32,3072]{1,0:T(8,128)S(1)}, u32[]{:S(2)}, u32[]{:S(2)}) collective-permute-start(f32[32,3072]{1,0:T(8,128)S(1)} %pad_maximum_fusion.1), channel_id=1, source_target_pairs={{0,3},{1,0},{2,1},{3,2},{4,7},{5,4},{6,5},{7,6},{8,11},{9,8},{10,9... | collective-permute-start | bytes 1179656 | tf_op jit(solution)/shard_map/ppermute | solution.py:25
  122.0 4.2 %shard_map.87.modes = f32[32,3072]{1,0:T(8,128)} custom-call(f32[96,3072]{1,0:T(8,128)} %bitcast.42, f32[96,3072]{1,0:T(8,128)} %copy-done.1, f32[96,3072]{1,0:T(8,128)} %copy-done, f32[48,3072]{1,0:T(8,128)} %copy-done.4, f32[48,3072]{1,0:T(8,128)} %copy-done.3, f32[4,32,96]{2,1,0:T(8,128)} %pad_maximum_fusion.2.coef), custom_call_target="tpu_custom_call" | custom-call | tf_op jit(solution)/shard_map/pallas_call | solution.py:266
  126.2 3.2 %collective-permute-done.16.from_next = f32[32,3072]{1,0:T(8,128)S(1)} collective-permute-done((f32[32,3072]{1,0:T(8,128)S(1)}, f32[32,3072]{1,0:T(8,128)S(1)}, u32[]{:S(2)}, u32[]{:S(2)}) %collective-permute-start.16) | collective-permute-done | bytes 393248 | tf_op jit(solution)/shard_map/ppermute | solution.py:25
  130.3 2.4 %shard_map.89 = (f32[96,384]{1,0:T(8,128)}, f32[96,384]{1,0:T(8,128)}, f32[32,1]{1,0:T(8,128)}, f32[32,3072]{1,0:T(8,128)}) custom-call(s32[1]{0:T(128)} %bitcast.5.col, f32[16,48,128]{2,1,0:T(8,128)} %copy-done.5, f32[32,3072]{1,0:T(8,128)} %shard_map.87.modes, f32[32,3072]{1,0:T(8,128)} %get-tuple-element.31.own, f32[32,3072]{1,0:T(8,128)} %copy-done.7, ...), custom_call_target="tpu_custom_call" | custom-call | tf_op jit(solution)/shard_map/pallas_call | solution.py:276
  132.7 1.3 %reduce = f32[32]{0:T(128)} reduce(f32[32,1]{1,0:T(8,128)} %get-tuple-element.36, f32[]{:T(128)} %constant.173), dimensions={1}, to_apply=%get-tuple-element.36.reduce_sub_computation | reduce | bytes 260 | tf_op jit(solution)/shard_map/pallas_call | solution.py:276
  (67 shorter events, 10.0 us)
Async XLA Ops:
  0.6 28.3 %collective-permute-start.1 = (f32[96,3072]{1,0:T(8,128)}, f32[96,3072]{1,0:T(8,128)S(1)}, u32[]{:S(2)}, u32[]{:S(2)}) collective-permute-start(f32[96,3072]{1,0:T(8,128)} %bitcast.34), channel_id=1, source_target_pairs={{0,3},{1,0},{2,1},{3,2},{4,7},{5,4},{6,5},{7,6},{8,11},{9,8},{10,9... | collective-permute-start | bytes 3538952 | tf_op jit(solution)/shard_map/ppermute | solution.py:25
  4.0 28.1 %collective-permute-start = (f32[96,3072]{1,0:T(8,128)}, f32[96,3072]{1,0:T(8,128)S(1)}, u32[]{:S(2)}, u32[]{:S(2)}) collective-permute-start(f32[96,3072]{1,0:T(8,128)} %bitcast.35), channel_id=1, source_target_pairs={{0,1},{1,2},{2,3},{3,0},{4,5},{5,6},{6,7},{7,4},{8,9},{9,10},{10,1... | collective-permute-start | bytes 3538952 | tf_op jit(solution)/shard_map/ppermute | solution.py:25
  4.0 9.0 %collective-permute-start.5 = (s32[4,48]{1,0:T(4,128)}, s32[4,48]{1,0:T(4,128)S(1)}, u32[]{:S(2)}, u32[]{:S(2)}) collective-permute-start(s32[4,48]{1,0:T(4,128)} %bitcast.52), channel_id=1, source_target_pairs={{0,248},{4,252},{8,0},{12,4},{16,8},{20,12},{24,16},{28,20},{32,24... | collective-permute-start | bytes 2312 | tf_op jit(solution)/shard_map/ppermute | solution.py:25
  12.0 6.0 %collective-permute-start.4 = (s32[4,48]{1,0:T(4,128)}, s32[4,48]{1,0:T(4,128)S(1)}, u32[]{:S(2)}, u32[]{:S(2)}) collective-permute-start(s32[4,48]{1,0:T(4,128)} %bitcast.53), channel_id=1, source_target_pairs={{0,8},{4,12},{8,16},{12,20},{16,24},{20,28},{24,32},{28,36},{32,40... | collective-permute-start | bytes 2312 | tf_op jit(solution)/shard_map/ppermute | solution.py:25
  12.0 37.5 %collective-permute-start.3 = (f32[96,3072]{1,0:T(8,128)}, f32[96,3072]{1,0:T(8,128)}, u32[]{:S(2)}, u32[]{:S(2)}) collective-permute-start(f32[96,3072]{1,0:T(8,128)} %bitcast.36), channel_id=1, source_target_pairs={{0,4},{4,8},{8,12},{12,16},{16,20},{20,24},{24,28},{28,32},{32,36}... | collective-permute-start | bytes 3538952 | tf_op jit(solution)/shard_map/ppermute | solution.py:25
  13.0 5.0 %copy-start.11 = (s32[4,48]{1,0:T(4,128)}, s32[4,48]{1,0:T(4,128)S(1)}, u32[]{:S(2)}) copy-start(s32[4,48]{1,0:T(4,128)S(1)} %collective-permute-done.5.next2) | copy-start | bytes 2308
  13.0 36.5 %collective-permute-start.2 = (f32[96,3072]{1,0:T(8,128)}, f32[96,3072]{1,0:T(8,128)}, u32[]{:S(2)}, u32[]{:S(2)}) collective-permute-start(f32[96,3072]{1,0:T(8,128)} %bitcast.37), channel_id=1, source_target_pairs={{0,252},{4,0},{8,4},{12,8},{16,12},{20,16},{24,20},{28,24},{32,28}... | collective-permute-start | bytes 3538952 | tf_op jit(solution)/shard_map/ppermute | solution.py:25
  22.5 16.2 %collective-permute-start.6 = (f32[96,1536]{1,0:T(8,128)}, f32[96,1536]{1,0:T(8,128)S(1)}, u32[]{:S(2)}, u32[]{:S(2)}) collective-permute-start(f32[96,1536]{1,0:T(8,128)} %get-tuple-element.22), channel_id=1, source_target_pairs={{0,248},{4,252},{8,0},{12,4},{16,8},{20,12},{24,16},{28,20},{32,24... | collective-permute-start | bytes 1769480 | tf_op jit(solution)/shard_map/ppermute | solution.py:25
  29.0 6.3 %copy-start = (f32[96,3072]{1,0:T(8,128)}, f32[96,3072]{1,0:T(8,128)S(1)}, u32[]{:S(2)}) copy-start(f32[96,3072]{1,0:T(8,128)S(1)} %collective-permute-done.1.after) | copy-start | bytes 3538948
  29.0 11.0 %copy-start.2 = (f32[384,128]{1,0:T(8,128)S(1)}, f32[384,128]{1,0:T(8,128)}, u32[]{:S(2)}) copy-start(f32[384,128]{1,0:T(8,128)} %ritz.3) | copy-start | bytes 589828
  29.0 20.5 %collective-permute-start.7 = (f32[96,1536]{1,0:T(8,128)}, f32[96,1536]{1,0:T(8,128)}, u32[]{:S(2)}, u32[]{:S(2)}) collective-permute-start(f32[96,1536]{1,0:T(8,128)} %get-tuple-element.23), channel_id=1, source_target_pairs={{0,8},{4,12},{8,16},{12,20},{16,24},{20,28},{24,32},{28,36},{32,40... | collective-permute-start | bytes 1769480 | tf_op jit(solution)/shard_map/ppermute | solution.py:25
  32.1 8.3 %copy-start.1 = (f32[96,3072]{1,0:T(8,128)}, f32[96,3072]{1,0:T(8,128)S(1)}, u32[]{:S(2)}) copy-start(f32[96,3072]{1,0:T(8,128)S(1)} %collective-permute-done.before) | copy-start | bytes 3538948
  32.1 34.3 %collective-permute-start.9 = (f32[48,3072]{1,0:T(8,128)}, f32[48,3072]{1,0:T(8,128)S(1)}, u32[]{:S(2)}, u32[]{:S(2)}) collective-permute-start(f32[48,3072]{1,0:T(8,128)} %slice.33), channel_id=1, source_target_pairs={{0,3},{1,0},{2,1},{3,2},{4,7},{5,4},{6,5},{7,6},{8,11},{9,8},{10,9... | collective-permute-start | bytes 1769480 | tf_op jit(solution)/shard_map/ppermute | solution.py:25
  38.6 0.9 copy-start.6
  39.5 26.9 %collective-permute-start.8 = (f32[48,3072]{1,0:T(8,128)}, f32[48,3072]{1,0:T(8,128)S(1)}, u32[]{:S(2)}, u32[]{:S(2)}) collective-permute-start(f32[48,3072]{1,0:T(8,128)} %slice.32), channel_id=1, source_target_pairs={{0,1},{1,2},{2,3},{3,0},{4,5},{5,6},{6,7},{7,4},{8,9},{9,10},{10,1... | collective-permute-start | bytes 1769480 | tf_op jit(solution)/shard_map/ppermute | solution.py:25
  66.4 0.8 copy-start.3
  66.4 1.0 copy-start.4
  71.7 16.5 %collective-permute-start.12 = (f32[8,128]{1,0:T(8,128)}, f32[8,128]{1,0:T(8,128)S(1)}, u32[]{:S(2)}, u32[]{:S(2)}) collective-permute-start(f32[8,128]{1,0:T(8,128)} %get-tuple-element.29), channel_id=1, source_target_pairs={{0,3},{1,0},{2,1},{3,2},{4,7},{5,4},{6,5},{7,6},{8,11},{9,8},{10,9... | collective-permute-start | bytes 12296 | tf_op jit(solution)/shard_map/ppermute | solution.py:25
  75.0 13.2 %collective-permute-start.11 = (f32[8,128]{1,0:T(8,128)}, f32[8,128]{1,0:T(8,128)S(1)}, u32[]{:S(2)}, u32[]{:S(2)}) collective-permute-start(f32[8,128]{1,0:T(8,128)} %get-tuple-element.29), channel_id=1, source_target_pairs={{0,2},{1,3},{2,0},{3,1},{4,6},{5,7},{6,4},{7,5},{8,10},{9,11},{10,... | collective-permute-start | bytes 12296 | tf_op jit(solution)/shard_map/ppermute | solution.py:25
  75.0 13.2 %collective-permute-start.10 = (f32[8,128]{1,0:T(8,128)}, f32[8,128]{1,0:T(8,128)S(1)}, u32[]{:S(2)}, u32[]{:S(2)}) collective-permute-start(f32[8,128]{1,0:T(8,128)} %get-tuple-element.29), channel_id=1, source_target_pairs={{0,1},{1,2},{2,3},{3,0},{4,5},{5,6},{6,7},{7,4},{8,9},{9,10},{10,1... | collective-permute-start | bytes 12296 | tf_op jit(solution)/shard_map/ppermute | solution.py:25
  75.6 20.7 %all-to-all-start = ((f32[16,40,128]{2,1,0:T(8,128)}), f32[16,40,128]{2,1,0:T(8,128)S(1)}, u32[]{:S(2)}, u32[]{:S(2)}) async-start(f32[16,40,128]{2,1,0:T(8,128)} %get-tuple-element.26), calls=%async_computation | async-start | bytes 655360 | tf_op jit(solution)/shard_map/all_to_all | solution.py:253
  81.6 6.7 %copy-start.10 = (f32[8,128]{1,0:T(8,128)S(1)}, f32[8,128]{1,0:T(8,128)}, u32[]{:S(2)}) copy-start(f32[8,128]{1,0:T(8,128)} %get-tuple-element.29) | copy-start | bytes 12292
  85.7 16.2 %collective-permute-start.15 = (f32[32,1536]{1,0:T(8,128)S(1)}, f32[32,1536]{1,0:T(8,128)S(1)}, u32[]{:S(2)}, u32[]{:S(2)}) collective-permute-start(f32[32,1536]{1,0:T(8,128)S(1)} %get-tuple-element.41), channel_id=1, source_target_pairs={{0,3},{1,0},{2,1},{3,2},{4,7},{5,4},{6,5},{7,6},{8,11},{9,8},{10,9... | collective-permute-start | bytes 589832 | tf_op jit(solution)/shard_map/ppermute | solution.py:25
  87.9 7.2 %collective-permute-start.13 = (f32[32,1536]{1,0:T(8,128)S(1)}, f32[32,1536]{1,0:T(8,128)S(1)}, u32[]{:S(2)}, u32[]{:S(2)}) collective-permute-start(f32[32,1536]{1,0:T(8,128)S(1)} %get-tuple-element.42), channel_id=1, source_target_pairs={{0,1},{1,2},{2,3},{3,0},{4,5},{5,6},{6,7},{7,4},{8,9},{9,10},{10,1... | collective-permute-start | bytes 589832 | tf_op jit(solution)/shard_map/ppermute | solution.py:25
  95.1 6.9 %copy-start.8 = (f32[32,3072]{1,0:T(8,128)S(1)}, f32[32,3072]{1,0:T(8,128)}, u32[]{:S(2)}) copy-start(f32[32,3072]{1,0:T(8,128)} %get-tuple-element.34) | copy-start | bytes 1179652
  96.2 29.9 %collective-permute-start.14 = (f32[32,3072]{1,0:T(8,128)S(1)}, f32[32,3072]{1,0:T(8,128)S(1)}, u32[]{:S(2)}, u32[]{:S(2)}) collective-permute-start(f32[32,3072]{1,0:T(8,128)S(1)} %pad_maximum_fusion), channel_id=1, source_target_pairs={{0,1},{1,2},{2,3},{3,0},{4,5},{5,6},{6,7},{7,4},{8,9},{9,10},{10,1... | collective-permute-start | bytes 1179656 | tf_op jit(solution)/shard_map/ppermute | solution.py:25
  97.0 12.4 %all-to-all-start.1 = ((f32[4,48,128]{2,1,0:T(8,128)}), f32[4,48,128]{2,1,0:T(8,128)S(1)}, u32[]{:S(2)}, u32[]{:S(2)}) async-start(f32[4,48,128]{2,1,0:T(8,128)} %broadcast_in_dim.4), calls=%async_computation.1 | async-start | bytes 196608 | tf_op jit(solution)/shard_map/all_to_all | solution.py:272
  110.2 19.2 %all-to-all-start.2 = ((f32[16,48,128]{2,1,0:T(8,128)}), f32[16,48,128]{2,1,0:T(8,128)S(1)}, u32[]{:S(2)}, u32[]{:S(2)}) async-start(f32[16,48,128]{2,1,0:T(8,128)} %broadcast_in_dim.5), calls=%async_computation.2 | async-start | bytes 786432 | tf_op jit(solution)/shard_map/all_to_all | solution.py:274
  118.3 11.1 %collective-permute-start.16 = (f32[32,3072]{1,0:T(8,128)S(1)}, f32[32,3072]{1,0:T(8,128)S(1)}, u32[]{:S(2)}, u32[]{:S(2)}) collective-permute-start(f32[32,3072]{1,0:T(8,128)S(1)} %pad_maximum_fusion.1), channel_id=1, source_target_pairs={{0,3},{1,0},{2,1},{3,2},{4,7},{5,4},{6,5},{7,6},{8,11},{9,8},{10,9... | collective-permute-start | bytes 1179656 | tf_op jit(solution)/shard_map/ppermute | solution.py:25
  126.2 3.2 %copy-start.7 = (f32[32,3072]{1,0:T(8,128)}, f32[32,3072]{1,0:T(8,128)S(1)}, u32[]{:S(2)}) copy-start(f32[32,3072]{1,0:T(8,128)S(1)} %collective-permute-done.14.from_prev) | copy-start | bytes 1179652
  129.4 0.8 copy-start.9
  129.4 0.9 copy-start.5
  (1 other events, 0.6 us)
where the time goes:
time: 135 us; the launch traced here: 134 us
  starting transfers between devices  48.2 us (36%)
  waiting for transfers between devices  37.5 us (28%)
  Pallas kernels  34.7 us (26%)
  local copies, waits for them, and re-layouts  8.35 us (6%)
  other arithmetic  4.49 us (3%)
    ppermute x17, waiting for transfers between devices, shifted(): lax.ppermute(array, axis, [(i, (i + by) % length) for i in range(length)])  30.1 us
    ppermute x17, starting transfers between devices, shifted(): lax.ppermute(array, axis, [(i, (i + by) % length) for i in range(length)])  29.3 us
    pallas_call x1, Pallas kernels, shards(): call(gram_kernel, [(3, width, 2 * width), (1, 2 * LANES)], [SMEM] + [VMEM...  8.57 us
    pallas_call x1, Pallas kernels, shards(): call(image_kernel, (width, rows), [SMEM, SMEM, whole, whole, whole] + [ti...  8.3 us
    all_to_all x1, starting transfers between devices, shards(): parts = lax.all_to_all(spread_out(part), RING, 0, 0, tiled=True)  8.01 us
    all_to_all x1, waiting for transfers between devices, shards(): part = lax.all_to_all(part, 'zh', 0, 0, tiled=True)  7.44 us
    all_to_all x1, starting transfers between devices, shards(): got = lax.all_to_all(payload, RING, 0, 0, tiled=True)  6 us
    all_to_all x1, starting transfers between devices, shards(): part = lax.all_to_all(part, 'zh', 0, 0, tiled=True)  4.93 us
  transfers between devices with their start and end apart: 20, of which 9 were waited for; matrix products, arithmetic and copies ran while one was open for 6% of the time, Pallas kernels for 21%

commit v1 on v0

v1 whole, which is shorter than its diff:
```python
import jax
import jax.numpy as jnp
from jax import lax
from jax.experimental import pallas as pl
from jax.experimental.pallas import tpu as pltpu
from jax.sharding import Mesh, PartitionSpec as P


RING = ("zl", "y", "core")
WIRE = ("zh", "zl", "y", "core")
BLOCK = 64
PARTS = 16
TILES = 5
PAIRS = 4
LANES = 128
F32 = jnp.float32
NN = (((1,), (0,)), ((), ()))
NT = (((1,), (1,)), ((), ()))
VMEM = pl.BlockSpec(memory_space=pltpu.VMEM)
SMEM = pl.BlockSpec(memory_space=pltpu.SMEM)


def shifted(array, axis, by):
    length = lax.axis_size(axis)
    return lax.ppermute(array, axis, [(i, (i + by) % length) for i in range(length)])


def split(x):
    high = x.astype(jnp.bfloat16)
    return high, (x - high.astype(F32)).astype(jnp.bfloat16)


def dot3(a, b, dims):
    (ah, al), (bh, bl) = a, b
    one = lambda x, y: lax.dot_general(x, y, dims, preferred_element_type=F32)
    rows = ah.shape[0]
    first = one(jnp.concatenate([ah, al], axis=0), bh)
    return first[:rows] + (first[rows:] + one(ah, bl))


def low_half(shape):
    return lax.broadcasted_iota(jnp.int32, shape, 1) < BLOCK


def block_at(ref, index, half):
    tile = ref[:, pl.ds(pl.multiple_of(index // 2 * LANES, LANES), LANES)]
    return jnp.where(index % 2 == half, tile, pltpu.roll(tile, BLOCK, 1))


def pack_kernel(base, prev2, next2, st, to_prev2, to_next2):
    low = low_half((st.shape[0], LANES))

    def step(m, carry):
        for asked, parity, out in ((prev2, 0, to_prev2), (next2, 1, to_next2)):
            first = block_at(st, asked[3, 4 * m + parity] - base[0], 0)
            second = block_at(st, asked[3, 4 * m + 2 + parity] - base[0], 1)
            out[:, pl.ds(pl.multiple_of(m * LANES, LANES), LANES)] = jnp.where(low, first, second)
        return carry

    lax.fori_loop(0, to_prev2.shape[1] // LANES, step, 0, unroll=4)


def image_kernel(base, cols, st, up1, down1, up2, down2, values, high, low):
    m = pl.program_id(0)
    width = st.shape[0]
    pairs = values.shape[0] // LANES
    left_half = low_half((width, LANES))
    flip = lambda x: pltpu.roll(x, BLOCK, 1)
    for h in range(pairs):
        tile = m * pairs + h
        own = st[:, pl.ds(pl.multiple_of(tile * LANES, LANES), LANES)]
        left, right = [], []
        for q, (far1, far2, at) in enumerate(((up1, up2, 1), (down1, down2, 2))):
            row = 2 * tile + q
            near = block_at(st, cols[1, row] - base[0], 1 - q)
            first = jnp.where(left_half, own, near) if q == 0 else jnp.where(left_half, near, own)
            side = h % 2
            other = block_at(far1, cols[2, row] - base[at], 1 - side)
            second = far2[:, h // 2 * LANES : (h // 2 + 1) * LANES]
            second = jnp.where(left_half, second, other) if side == 0 else jnp.where(left_half, other, second)
            left.append(jnp.concatenate([first, second], axis=1))
            coef = values[(2 * h + q) * BLOCK : (2 * h + q + 1) * BLOCK, :]
            one, two = coef[:, :LANES], coef[:, LANES:]
            one = one if q == 0 else flip(one)
            two = flip(two) if side == 0 else two
            right.append(jnp.concatenate([one, two], axis=1))
        part = dot3(
            split(jnp.concatenate(left, axis=0)), split(jnp.concatenate(right, axis=0)), NT
        )
        image = 4.0 * own + jnp.where(left_half, part[:width], part[width:])
        high[:, h * LANES : (h + 1) * LANES], low[:, h * LANES : (h + 1) * LANES] = split(image)


def quotient_terms(piece, mine, ritz, start):
    left = dot3(split(piece), split(mine), NN)
    return jnp.sum(left * ritz[pl.ds(start, piece.shape[0]), :], axis=0, keepdims=True)


def piece_terms(gram, c, ritz, terms):
    width = gram.shape[1]
    at = lambda by: pl.multiple_of((c + by) % 4 * width, 8)
    mine = ritz[pl.ds(at(0), width), :]
    total = quotient_terms(gram[0], mine, ritz, at(0))
    total = total + quotient_terms(gram[1], mine, ritz, at(3))
    terms[...] = total + quotient_terms(gram[2], mine, ritz, at(1))


def mass_kernel(col, st, before, after, ritz, high, low, gram, terms):
    width = st.shape[0]
    for i, piece in enumerate((st, before, after)):
        high[i * width : (i + 1) * width, :], low[i * width : (i + 1) * width, :] = split(piece[...])
    block = dot3((high[...], low[...]), (high[:width, :], low[:width, :]), NT)
    for i in range(3):
        gram[i] = block[i * width : (i + 1) * width]
    piece_terms(gram, col[0], ritz, terms)


def stiff_kernel(col, high, low, image_high, image_low, ritz, gram, terms):
    width = image_high.shape[0]
    block = dot3((high[...], low[...]), (image_high[...], image_low[...]), NT)
    for i in range(3):
        gram[i] = block[i * width : (i + 1) * width]
    piece_terms(gram, col[0], ritz, terms)


def late_kernel(
    col, stiff3, stiff_terms, mass3, mass_terms, opp_a, opp_b, image_high, image_low, st_high, st_low,
    ritz, payload, terms, stiff, mass
):
    c = col[0]
    width = st_high.shape[0]
    far = dot3(
        split(jnp.concatenate([opp_a[...], opp_b[...]], axis=0)),
        (
            jnp.concatenate([image_high[...], st_high[...]], axis=0),
            jnp.concatenate([image_low[...], st_low[...]], axis=0),
        ),
        NT,
    )
    terms[...] = jnp.zeros_like(terms)
    at = lambda by: pl.multiple_of((c + by) % 4 * width, 8)
    mine = ritz[pl.ds(at(0), width), :]
    turned = []
    for i, (block, whole, pieces, sums) in enumerate(
        (
            (far[:, :width], stiff, stiff3, stiff_terms),
            (far[:, width:], mass, mass3, mass_terms),
        )
    ):
        for piece, by in ((pieces[0], 0), (pieces[1], 3), (pieces[2], 1), (block, 2)):
            whole[pl.ds(at(by), width), :] = piece
        terms[i : i + 1, :] = sums[...] + quotient_terms(block, mine, ritz, at(2))
        turned.append(whole[...].T)
    for t in range(PARTS * TILES):
        k, to = t // TILES, t % TILES * 8
        i, j = t // 3 * 8, t % 3 * LANES
        if i < 2 * width:
            payload[k, to : to + 8, :] = turned[i // width][i % width : i % width + 8, j : j + LANES]
        else:
            payload[k, to : to + 8, :] = jnp.zeros((8, LANES), F32)


def modes_kernel(high, low, opp_a, opp_b, coef, modes):
    rest = high.shape[0]
    opp = jnp.concatenate([opp_a[...], opp_b[...]], axis=0)
    modes[...] = dot3(split(coef[:, :rest]), (high[...], low[...]), NN) + dot3(
        split(coef[:, rest:]), split(opp), NN
    )


def image_part_kernel(high, low, coef, own, after, opp, before):
    part = dot3(split(coef[...]), (high[...], low[...]), NN)
    modes = own.shape[0]
    for i, out in enumerate((own, after, opp, before)):
        out[...] = part[i * modes : (i + 1) * modes]


def final_kernel(col, parts, modes, own, from_prev, from_next, from_opp, stiff, mass, theta, residual):
    total = jnp.float32(196608.0)
    terms = parts[0, 8 * TILES :, :]
    for k in range(1, PARTS):
        terms = terms + parts[k, 8 * TILES :, :]
    quotient = terms[0:1, :] / terms[1:2, :]
    shape = (modes.shape[0], LANES)
    here = lax.broadcasted_iota(jnp.int32, shape, 1) == (
        lax.broadcasted_iota(jnp.int32, shape, 0) + col[0] * shape[0]
    )
    column = jnp.sum(jnp.where(here, jnp.broadcast_to(quotient, shape), 0.0), axis=1, keepdims=True)
    theta[...] = pltpu.roll(
        jnp.broadcast_to(quotient, (8, LANES)), (4 - col[0]) % 4 * shape[0], 1
    )[0:1, : shape[0]]
    image = (own[...] + from_opp[...]) + (from_prev[...] + from_next[...])
    residual[...] = image - column * modes[...]
    width = stiff.shape[0]
    for t in range(2 * width // 8 * 3):
        k, at = t // TILES, t % TILES * 8
        i, j = t // 3 * 8, t % 3 * LANES
        out = stiff if i < width else mass
        out[i % width : i % width + 8, j : j + LANES] = parts[k, at : at + 8, :] / total


def call(kernel, shapes, in_specs, dtypes=None, **kwargs):
    dtypes = dtypes or [F32] * len(shapes)
    return pl.pallas_call(
        kernel,
        out_shape=[jax.ShapeDtypeStruct(s, d) for s, d in zip(shapes, dtypes)],
        in_specs=in_specs,
        out_specs=kwargs.pop("out_specs", [VMEM] * len(shapes)),
        **kwargs,
    )


def spread_out(part):
    return jnp.broadcast_to(part[None], (PARTS,) + part.shape)


def shards(search, values, block_cols, ritz):
    rows, width = search.shape
    blk = block_cols.shape[0]
    modes = ritz.shape[1] // 4
    half = width // 2
    c = lax.axis_index("col")
    w = lax.axis_index(WIRE)
    groups = lax.axis_size(WIRE)
    col = jnp.reshape(c, (1,)).astype(jnp.int32)
    base = (jnp.stack([w, (w + 1) % groups, (w + groups - 1) % groups]) * blk).astype(jnp.int32)
    st = search.T
    cols = block_cols.T

    before = shifted(st, "col", 1)
    after = shifted(st, "col", -1)
    prev2 = shifted(cols, WIRE, 2)
    next2 = shifted(cols, WIRE, -2)
    up1 = shifted(st, WIRE, -1)
    down1 = shifted(st, WIRE, 1)

    packed = call(pack_kernel, [(width, rows // 2)] * 2, [SMEM] * 3 + [VMEM])(base, prev2, next2, st)
    up2 = shifted(packed[0], WIRE, -2)
    down2 = shifted(packed[1], WIRE, 2)

    opp_a = shifted(before[:half], "col", 1)
    opp_b = shifted(after[half:], "col", -1)

    mine = lax.dynamic_slice_in_dim(ritz, c * modes, modes, 1).T
    coef = jnp.concatenate(
        [lax.dynamic_slice_in_dim(mine, (c + by) % 4 * width, width, 1) for by in (0, 3, 1, 2)], axis=1
    )
    ours = lax.dynamic_slice_in_dim(ritz, c * width, width, 0).T
    send = jnp.roll(ours, -c * modes, 0)

    high, low, mass3, mass_terms = call(
        mass_kernel,
        [(3 * width, rows), (3 * width, rows), (3, width, width), (1, LANES)],
        [SMEM] + [VMEM] * 4,
        [jnp.bfloat16, jnp.bfloat16, F32, F32],
    )(col, st, before, after, ritz)

    tile = lambda n: pl.BlockSpec((width, n), lambda m: (0, m))
    whole = pl.BlockSpec((width, rows), lambda m: (0, 0))
    image = call(
        image_kernel,
        [(width, rows)] * 2,
        [SMEM, SMEM, whole, whole, whole]
        + [tile(PAIRS // 2 * LANES)] * 2
        + [pl.BlockSpec((PAIRS * LANES, values.shape[1]), lambda m: (m, 0))],
        [jnp.bfloat16] * 2,
        out_specs=[tile(PAIRS * LANES)] * 2,
        grid=(rows // (PAIRS * LANES),),
    )(base, cols, st, up1, down1, up2, down2, values)

    stiff3, stiff_terms = call(
        stiff_kernel, [(3, width, width), (1, LANES)], [SMEM] + [VMEM] * 5
    )(col, high, low, *image, ritz)

    payload, terms = call(
        late_kernel,
        [(PARTS, 8 * TILES, LANES), (8, LANES)],
        [SMEM] + [VMEM] * 8 + [whole] * 2 + [VMEM],
        grid=(1,),
        scratch_shapes=[pltpu.VMEM((4 * width, width), F32)] * 2,
    )(col, stiff3, stiff_terms, mass3, mass_terms, opp_a, opp_b, *image, high, low, ritz)

    got = lax.all_to_all(payload, RING, 0, 0, tiled=True)
    around = [shifted(terms, "col", by) for by in (1, 2, 3)]
    image, stiff3 = lax.optimization_barrier((image, stiff3))
    part_own, part_after, part_opp, part_before = call(image_part_kernel, [(modes, rows)] * 4, [VMEM] * 3)(*image, send)
    from_prev = shifted(part_after, "col", 1)
    from_next = shifted(part_before, "col", -1)
    from_opp = shifted(part_opp, "col", 2)
    new_modes = call(modes_kernel, [(modes, rows)], [VMEM] * 5)(high, low, opp_a, opp_b, coef)[0]

    part = jnp.concatenate(
        [jnp.sum(got, axis=0), terms + around[0] + around[1] + around[2]], axis=0
    )
    part = jnp.broadcast_to(part[None], (4,) + part.shape)
    part = lax.all_to_all(part, "zh", 0, 0, tiled=True)
    part = jnp.sum(part, axis=0)
    parts = lax.all_to_all(spread_out(part), RING, 0, 0, tiled=True)

    stiff, mass, theta, residual = call(
        final_kernel,
        [(width, 4 * width), (width, 4 * width), (1, modes), (modes, rows)],
        [SMEM] + [VMEM] * 6,
    )(col, parts, new_modes, part_own, from_prev, from_next, from_opp)
    return (new_modes.T, residual.T, theta[0], stiff.T, mass.T)


def solution(mesh):
    mesh = Mesh(mesh.devices.reshape(4, 2, 4, 2, 4), WIRE + ("col",))
    return jax.shard_map(
        shards,
        mesh=mesh,
        in_specs=(P(WIRE, "col"), P(WIRE, None), P(WIRE, None), P()),
        out_specs=(P(WIRE, "col"), P(WIRE, "col"), P("col"), P(None, "col"), P(None, "col")),
        check_vma=False,
    )
```

time: 135 us -> 132 us (0.978)
  blocking collectives: 0 us -> 13.1 us
  starting transfers between devices: 48.2 us -> 40.3 us
  waiting for transfers between devices: 37.5 us -> 33.6 us
  local copies, waits for them, and re-layouts: 8.35 us -> 5.86 us
  other arithmetic: 4.49 us -> 2.73 us
    all_to_all x0 -> x1, blocking collectives: none -> 13.1 us  [shards(): part = lax.all_to_all(part, 'zh', 0, 0, tiled=True)]
    all_to_all x1 -> x0, waiting for transfers between devices: 7.44 us -> none  [shards(): part = lax.all_to_all(part, 'zh', 0, 0, tiled=True)]
    all_to_all x1 -> x0, starting transfers between devices: 4.93 us -> none  [shards(): part = lax.all_to_all(part, 'zh', 0, 0, tiled=True)]
    ppermute x17 -> x16, waiting for transfers between devices: 30.1 us -> 33.6 us  [shifted(): lax.ppermute(array, axis, [(i, (i + by) % length) for i in range(length)])]
    ppermute x17 -> x16, starting transfers between devices: 29.3 us -> 26.8 us  [shifted(): lax.ppermute(array, axis, [(i, (i + by) % length) for i in range(length)])]
    concatenate x2, other arithmetic: 0.05 us -> 1.41 us  [the longest x1 0.74 us: shards(): jnp.concatenate([lax.dynamic_slice_in_dim(mine, (c + by) % 4 * width, wid...]
    pallas_call x5 -> x6, Pallas kernels: 26.5 us -> 27.7 us  [the longest x1 8.19 us: shards(): call(image_kernel, [(width, rows)] * 2, [SMEM, SMEM, whole, whole, whole]...]
    unnamed x34 -> x29, local copies, waits for them, and re-layouts: 3.96 us -> 3.15 us
  transfers between devices with their start and end apart: 20 -> 18, of which waited for: 9 -> 9; matrix products, arithmetic and copies ran while one was open for 6% -> 4% of each run, Pallas kernels for 21% -> 22%
where the time goes in v1:
time: 132 us; the launch traced here: 131 us
  starting transfers between devices  40.3 us (31%)
  Pallas kernels  34.8 us (26%)
  waiting for transfers between devices  33.6 us (25%)
  blocking collectives  13.1 us (10%)
  local copies, waits for them, and re-layouts  5.86 us (4%)
  other arithmetic  2.73 us (2%)
    ppermute x16, waiting for transfers between devices, shifted(): lax.ppermute(array, axis, [(i, (i + by) % length) for i in range(length)])  33.6 us
    ppermute x16, starting transfers between devices, shifted(): lax.ppermute(array, axis, [(i, (i + by) % length) for i in range(length)])  26.8 us
    all_to_all x1, blocking collectives, shards(): part = lax.all_to_all(part, 'zh', 0, 0, tiled=True)  13.1 us
    pallas_call x1, Pallas kernels, shards(): call(image_kernel, [(width, rows)] * 2, [SMEM, SMEM, whole, whole, whole]...  8.19 us
    all_to_all x1, starting transfers between devices, shards(): parts = lax.all_to_all(spread_out(part), RING, 0, 0, tiled=True)  8.11 us
    all_to_all x1, starting transfers between devices, shards(): got = lax.all_to_all(payload, RING, 0, 0, tiled=True)  5.46 us
    pallas_call x1, Pallas kernels, shards(): call(mass_kernel, [(3 * width, rows), (3 * width, rows), (3, width, width...  5.02 us
    pallas_call x1, Pallas kernels, shards(): call(stiff_kernel, [(3, width, width), (1, LANES)], [SMEM] + [VMEM] * 5)  4.62 us
  transfers between devices with their start and end apart: 18, of which 9 were waited for; matrix products, arithmetic and copies ran while one was open for 4% of the time, Pallas kernels for 22%

profile of v1, /device:TPU:1, one launch (start us, length us, event | category | flops | bytes accessed | tf_op | source)
XLA Modules:
  0.0 131.2 jit_solution(1888734317537832961)
XLA Ops:
  0.6 3.4 %collective-permute-start.1 = (f32[96,3072]{1,0:T(8,128)}, f32[96,3072]{1,0:T(8,128)S(1)}, u32[]{:S(2)}, u32[]{:S(2)}) collective-permute-start(f32[96,3072]{1,0:T(8,128)} %bitcast.16), channel_id=1, source_target_pairs={{0,3},{1,0},{2,1},{3,2},{4,7},{5,4},{6,5},{7,6},{8,11},{9,8},{10,9... | collective-permute-start | bytes 3538952 | tf_op jit(solution)/shard_map/ppermute | solution.py:25
  4.0 8.0 %collective-permute-start.7 = (s32[4,48]{1,0:T(4,128)}, s32[4,48]{1,0:T(4,128)S(1)}, u32[]{:S(2)}, u32[]{:S(2)}) collective-permute-start(s32[4,48]{1,0:T(4,128)} %bitcast.29), channel_id=1, source_target_pairs={{0,248},{4,252},{8,0},{12,4},{16,8},{20,12},{24,16},{28,20},{32,24... | collective-permute-start | bytes 2312 | tf_op jit(solution)/shard_map/ppermute | solution.py:25
  12.0 0.9 collective-permute-done.7.next2
  13.0 1.8 %collective-permute-start.4 = (f32[96,3072]{1,0:T(8,128)}, f32[96,3072]{1,0:T(8,128)}, u32[]{:S(2)}, u32[]{:S(2)}) collective-permute-start(f32[96,3072]{1,0:T(8,128)} %bitcast.19), channel_id=1, source_target_pairs={{0,252},{4,0},{8,4},{12,8},{16,12},{20,16},{24,20},{28,24},{32,28}... | collective-permute-start | bytes 3538952 | tf_op jit(solution)/shard_map/ppermute | solution.py:25
  15.4 2.6 %collective-permute-done.6.prev2 = s32[4,48]{1,0:T(4,128)S(1)} collective-permute-done((s32[4,48]{1,0:T(4,128)}, s32[4,48]{1,0:T(4,128)S(1)}, u32[]{:S(2)}, u32[]{:S(2)}) %collective-permute-start.6) | collective-permute-done | bytes 800 | tf_op jit(solution)/shard_map/ppermute | solution.py:25
  18.6 3.1 %shard_map.85 = (f32[96,1536]{1,0:T(8,128)}, f32[96,1536]{1,0:T(8,128)}) custom-call(s32[3]{0:T(128)} %add_multiply_fusion.base, s32[4,48]{1,0:T(4,128)} %copy-done.11, s32[4,48]{1,0:T(4,128)} %copy-done.10, f32[96,3072]{1,0:T(8,128)} %bitcast.20), custom_call_target="tpu_custom_call" | custom-call | tf_op jit(solution)/shard_map/pallas_call | solution.py:237
  21.7 2.7 %collective-permute-start.8 = (f32[96,1536]{1,0:T(8,128)}, f32[96,1536]{1,0:T(8,128)S(1)}, u32[]{:S(2)}, u32[]{:S(2)}) collective-permute-start(f32[96,1536]{1,0:T(8,128)} %get-tuple-element.29), channel_id=1, source_target_pairs={{0,248},{4,252},{8,0},{12,4},{16,8},{20,12},{24,16},{28,20},{32,24... | collective-permute-start | bytes 1769480 | tf_op jit(solution)/shard_map/ppermute | solution.py:25
  24.4 4.6 %collective-permute-done.1.after = f32[96,3072]{1,0:T(8,128)S(1)} collective-permute-done((f32[96,3072]{1,0:T(8,128)}, f32[96,3072]{1,0:T(8,128)S(1)}, u32[]{:S(2)}, u32[]{:S(2)}) %collective-permute-start.1) | collective-permute-done | bytes 1179680 | tf_op jit(solution)/shard_map/ppermute | solution.py:25
  29.0 1.3 collective-permute-start.9
  30.3 0.9 slice.9
  31.1 1.0 collective-permute-done.before
  32.1 2.3 %collective-permute-start.3 = (f32[48,3072]{1,0:T(8,128)}, f32[48,3072]{1,0:T(8,128)S(1)}, u32[]{:S(2)}, u32[]{:S(2)}) collective-permute-start(f32[48,3072]{1,0:T(8,128)} %slice.9), channel_id=1, source_target_pairs={{0,3},{1,0},{2,1},{3,2},{4,7},{5,4},{6,5},{7,6},{8,11},{9,8},{10,9... | collective-permute-start | bytes 1769480 | tf_op jit(solution)/shard_map/ppermute | solution.py:25
  34.4 0.9 slice.8
  35.4 2.5 %collective-permute-done.8.up2 = f32[96,1536]{1,0:T(8,128)S(1)} collective-permute-done((f32[96,1536]{1,0:T(8,128)}, f32[96,1536]{1,0:T(8,128)S(1)}, u32[]{:S(2)}, u32[]{:S(2)}) %collective-permute-start.8) | collective-permute-done | bytes 589856 | tf_op jit(solution)/shard_map/ppermute | solution.py:25
  38.4 5.0 %shard_map.83 = (bf16[288,3072]{1,0:T(8,128)(2,1)}, bf16[288,3072]{1,0:T(8,128)(2,1)}, f32[3,96,96]{2,1,0:T(8,128)}, f32[1,128]{1,0:T(1,128)}) custom-call(s32[1]{0:T(128)} %bitcast.col, f32[96,3072]{1,0:T(8,128)} %bitcast.21, f32[96,3072]{1,0:T(8,128)} %copy-done.2, f32[96,3072]{1,0:T(8,128)} %copy-done.1, f32[384,128]{1,0:T(8,128)} %ritz.5), custom_call_target="tpu_custom_call" | custom-call | tf_op jit(solution)/shard_map/pallas_call | solution.py:251
  43.4 6.1 %collective-permute-done.9.down2 = f32[96,1536]{1,0:T(8,128)} collective-permute-done((f32[96,1536]{1,0:T(8,128)}, f32[96,1536]{1,0:T(8,128)}, u32[]{:S(2)}, u32[]{:S(2)}) %collective-permute-start.9) | collective-permute-done | bytes 589856 | tf_op jit(solution)/shard_map/ppermute | solution.py:25
  49.5 8.2 %shard_map.86 = (bf16[96,3072]{1,0:T(8,128)(2,1)}, bf16[96,3072]{1,0:T(8,128)(2,1)}) custom-call(s32[3]{0:T(128)} %add_multiply_fusion.base, s32[4,48]{1,0:T(4,128)} %bitcast.31, f32[96,3072]{1,0:T(8,128)} %bitcast.22, f32[96,3072]{1,0:T(8,128)} %collective-permute-done.4.up1, f32[96,3072]{1,0:T(8,128)} %collective-permute-done.5.down1, ...), custom_call_target="tpu_custom_call" | custom-call | tf_op jit(solution)/shard_map/pallas_call | solution.py:260
  57.7 4.6 %shard_map.87 = (f32[3,96,96]{2,1,0:T(8,128)}, f32[1,128]{1,0:T(1,128)}) custom-call(s32[1]{0:T(128)} %bitcast.col, bf16[288,3072]{1,0:T(8,128)(2,1)} %get-tuple-element.27.high.st_high, bf16[288,3072]{1,0:T(8,128)(2,1)} %get-tuple-element.28.low.st_low, bf16[96,3072]{1,0:T(8,128)(2,1)} %get-tuple-element.39.image_high.high, ...), custom_call_target="tpu_custom_call" | custom-call | tf_op jit(solution)/shard_map/pallas_call | solution.py:271
  62.3 0.8 copy-done.3
  63.4 3.9 %shard_map.88 = (f32[16,40,128]{2,1,0:T(8,128)}, f32[8,128]{1,0:T(8,128)}) custom-call(s32[1]{0:T(128)} %bitcast.col, f32[3,96,96]{2,1,0:T(8,128)} %get-tuple-element.33.stiff3, f32[1,128]{1,0:T(1,128)} %get-tuple-element.34.stiff_terms, f32[3,96,96]{2,1,0:T(8,128)} %get-tuple-element.35.mass3, f32[1,128]{1,0:T(1,128)} %get-tuple-element.36.mass_terms, ...), custom_call_target="tpu_custom_call" | custom-call | tf_op jit(solution)/shard_map/pallas_call | solution.py:275
  67.3 5.5 %all-to-all-start = ((f32[16,40,128]{2,1,0:T(8,128)}), f32[16,40,128]{2,1,0:T(8,128)S(1)}, u32[]{:S(2)}, u32[]{:S(2)}) async-start(f32[16,40,128]{2,1,0:T(8,128)} %get-tuple-element.37), calls=%async_computation | async-start | bytes 655360 | tf_op jit(solution)/shard_map/all_to_all | solution.py:283
  72.8 3.4 %collective-permute-start.12 = (f32[8,128]{1,0:T(8,128)}, f32[8,128]{1,0:T(8,128)S(1)}, u32[]{:S(2)}, u32[]{:S(2)}) collective-permute-start(f32[8,128]{1,0:T(8,128)} %get-tuple-element.38), channel_id=1, source_target_pairs={{0,3},{1,0},{2,1},{3,2},{4,7},{5,4},{6,5},{7,6},{8,11},{9,8},{10,9... | collective-permute-start | bytes 12296 | tf_op jit(solution)/shard_map/ppermute | solution.py:25
  77.1 3.2 %collective-permute-done.11 = f32[8,128]{1,0:T(8,128)S(1)} collective-permute-done((f32[8,128]{1,0:T(8,128)}, f32[8,128]{1,0:T(8,128)S(1)}, u32[]{:S(2)}, u32[]{:S(2)}) %collective-permute-start.11) | collective-permute-done | bytes 4128 | tf_op jit(solution)/shard_map/ppermute | solution.py:25
  81.1 13.1 %all_to_all.15 = f32[4,48,128]{2,1,0:T(8,128)S(1)} all-to-all(f32[4,48,128]{2,1,0:T(8,128)S(1)} %broadcast_in_dim.4), channel_id=1, replica_groups=mesh['zh'=4,'zl'=2,'y'=4,'core'=2,'col'=4] {'zh'}, dimensions={0} | all-to-all | bytes 196608 | tf_op jit(solution)/shard_map/all_to_all | solution.py:296
  94.2 0.8 broadcast_in_dim.5
  95.0 8.1 %all-to-all-start.2 = ((f32[16,48,128]{2,1,0:T(8,128)}), f32[16,48,128]{2,1,0:T(8,128)S(1)}, u32[]{:S(2)}, u32[]{:S(2)}) async-start(f32[16,48,128]{2,1,0:T(8,128)} %broadcast_in_dim.5), calls=%async_computation.2 | async-start | bytes 786432 | tf_op jit(solution)/shard_map/all_to_all | solution.py:298
  103.9 3.1 %shard_map.89 = (f32[32,3072]{1,0:T(8,128)}, f32[32,3072]{1,0:T(8,128)}, f32[32,3072]{1,0:T(8,128)}, f32[32,3072]{1,0:T(8,128)}) custom-call(bf16[96,3072]{1,0:T(8,128)(2,1)} %get-tuple-element.39.image_high.high, bf16[96,3072]{1,0:T(8,128)(2,1)} %get-tuple-element.40.image_low.low, f32[128,96]{1,0:T(8,128)} %fusion.coef), custom_call_target="tpu_custom_call" | custom-call | tf_op jit(solution)/shard_map/pallas_call | solution.py:286
  107.0 2.7 %collective-permute-start.14 = (f32[32,3072]{1,0:T(8,128)}, f32[32,3072]{1,0:T(8,128)S(1)}, u32[]{:S(2)}, u32[]{:S(2)}) collective-permute-start(f32[32,3072]{1,0:T(8,128)} %get-tuple-element.43), channel_id=1, source_target_pairs={{0,3},{1,0},{2,1},{3,2},{4,7},{5,4},{6,5},{7,6},{8,11},{9,8},{10,9... | collective-permute-start | bytes 1179656 | tf_op jit(solution)/shard_map/ppermute | solution.py:25
  110.1 0.7 pad_maximum_fusion.coef
  110.9 4.1 %shard_map.84.modes = f32[32,3072]{1,0:T(8,128)} custom-call(bf16[288,3072]{1,0:T(8,128)(2,1)} %get-tuple-element.27.high.st_high, bf16[288,3072]{1,0:T(8,128)(2,1)} %get-tuple-element.28.low.st_low, f32[48,3072]{1,0:T(8,128)} %copy-done.4, f32[48,3072]{1,0:T(8,128)} %copy-done.3, f32[32,384]{1,0:T(8,128)} %pad_maximum_fusion.coef), custom_call_target="tpu_custom_call" | custom-call | tf_op jit(solution)/shard_map/pallas_call | solution.py:290
  115.0 12.4 %collective-permute-done.13.from_prev = f32[32,3072]{1,0:T(8,128)S(1)} collective-permute-done((f32[32,3072]{1,0:T(8,128)}, f32[32,3072]{1,0:T(8,128)S(1)}, u32[]{:S(2)}, u32[]{:S(2)}) %collective-permute-start.13) | collective-permute-done | bytes 393248 | tf_op jit(solution)/shard_map/ppermute | solution.py:25
  128.6 2.6 %shard_map.90 = (f32[96,384]{1,0:T(8,128)}, f32[96,384]{1,0:T(8,128)}, f32[1,32]{1,0:T(1,128)}, f32[32,3072]{1,0:T(8,128)}) custom-call(s32[1]{0:T(128)} %bitcast.col, f32[16,48,128]{2,1,0:T(8,128)} %copy-done.5, f32[32,3072]{1,0:T(8,128)} %shard_map.84.modes, f32[32,3072]{1,0:T(8,128)} %get-tuple-element.41.own, f32[32,3072]{1,0:T(8,128)} %copy-done.7, ...), custom_call_target="tpu_custom_call" | custom-call | tf_op jit(solution)/shard_map/pallas_call | solution.py:300
  (55 shorter events, 6.0 us)
Async XLA Ops:
  0.6 28.3 %collective-permute-start.1 = (f32[96,3072]{1,0:T(8,128)}, f32[96,3072]{1,0:T(8,128)S(1)}, u32[]{:S(2)}, u32[]{:S(2)}) collective-permute-start(f32[96,3072]{1,0:T(8,128)} %bitcast.16), channel_id=1, source_target_pairs={{0,3},{1,0},{2,1},{3,2},{4,7},{5,4},{6,5},{7,6},{8,11},{9,8},{10,9... | collective-permute-start | bytes 3538952 | tf_op jit(solution)/shard_map/ppermute | solution.py:25
  4.0 28.1 %collective-permute-start = (f32[96,3072]{1,0:T(8,128)}, f32[96,3072]{1,0:T(8,128)S(1)}, u32[]{:S(2)}, u32[]{:S(2)}) collective-permute-start(f32[96,3072]{1,0:T(8,128)} %bitcast.17), channel_id=1, source_target_pairs={{0,1},{1,2},{2,3},{3,0},{4,5},{5,6},{6,7},{7,4},{8,9},{9,10},{10,1... | collective-permute-start | bytes 3538952 | tf_op jit(solution)/shard_map/ppermute | solution.py:25
  4.0 9.0 %collective-permute-start.7 = (s32[4,48]{1,0:T(4,128)}, s32[4,48]{1,0:T(4,128)S(1)}, u32[]{:S(2)}, u32[]{:S(2)}) collective-permute-start(s32[4,48]{1,0:T(4,128)} %bitcast.29), channel_id=1, source_target_pairs={{0,248},{4,252},{8,0},{12,4},{16,8},{20,12},{24,16},{28,20},{32,24... | collective-permute-start | bytes 2312 | tf_op jit(solution)/shard_map/ppermute | solution.py:25
  12.0 6.0 %collective-permute-start.6 = (s32[4,48]{1,0:T(4,128)}, s32[4,48]{1,0:T(4,128)S(1)}, u32[]{:S(2)}, u32[]{:S(2)}) collective-permute-start(s32[4,48]{1,0:T(4,128)} %bitcast.30), channel_id=1, source_target_pairs={{0,8},{4,12},{8,16},{12,20},{16,24},{20,28},{24,32},{28,36},{32,40... | collective-permute-start | bytes 2312 | tf_op jit(solution)/shard_map/ppermute | solution.py:25
  12.0 37.5 %collective-permute-start.5 = (f32[96,3072]{1,0:T(8,128)}, f32[96,3072]{1,0:T(8,128)}, u32[]{:S(2)}, u32[]{:S(2)}) collective-permute-start(f32[96,3072]{1,0:T(8,128)} %bitcast.18), channel_id=1, source_target_pairs={{0,4},{4,8},{8,12},{12,16},{16,20},{20,24},{24,28},{28,32},{32,36}... | collective-permute-start | bytes 3538952 | tf_op jit(solution)/shard_map/ppermute | solution.py:25
  13.0 5.0 %copy-start.10 = (s32[4,48]{1,0:T(4,128)}, s32[4,48]{1,0:T(4,128)S(1)}, u32[]{:S(2)}) copy-start(s32[4,48]{1,0:T(4,128)S(1)} %collective-permute-done.7.next2) | copy-start | bytes 2308
  13.0 36.5 %collective-permute-start.4 = (f32[96,3072]{1,0:T(8,128)}, f32[96,3072]{1,0:T(8,128)}, u32[]{:S(2)}, u32[]{:S(2)}) collective-permute-start(f32[96,3072]{1,0:T(8,128)} %bitcast.19), channel_id=1, source_target_pairs={{0,252},{4,0},{8,4},{12,8},{16,12},{20,16},{24,20},{28,24},{32,28}... | collective-permute-start | bytes 3538952 | tf_op jit(solution)/shard_map/ppermute | solution.py:25
  18.0 0.6 copy-start.11
  21.7 16.2 %collective-permute-start.8 = (f32[96,1536]{1,0:T(8,128)}, f32[96,1536]{1,0:T(8,128)S(1)}, u32[]{:S(2)}, u32[]{:S(2)}) collective-permute-start(f32[96,1536]{1,0:T(8,128)} %get-tuple-element.29), channel_id=1, source_target_pairs={{0,248},{4,252},{8,0},{12,4},{16,8},{20,12},{24,16},{28,20},{32,24... | collective-permute-start | bytes 1769480 | tf_op jit(solution)/shard_map/ppermute | solution.py:25
  29.0 6.4 %copy-start.1 = (f32[96,3072]{1,0:T(8,128)}, f32[96,3072]{1,0:T(8,128)S(1)}, u32[]{:S(2)}) copy-start(f32[96,3072]{1,0:T(8,128)S(1)} %collective-permute-done.1.after) | copy-start | bytes 3538948
  29.0 20.5 %collective-permute-start.9 = (f32[96,1536]{1,0:T(8,128)}, f32[96,1536]{1,0:T(8,128)}, u32[]{:S(2)}, u32[]{:S(2)}) collective-permute-start(f32[96,1536]{1,0:T(8,128)} %get-tuple-element.30), channel_id=1, source_target_pairs={{0,8},{4,12},{8,16},{12,20},{16,24},{20,28},{24,32},{28,36},{32,40... | collective-permute-start | bytes 1769480 | tf_op jit(solution)/shard_map/ppermute | solution.py:25
  32.1 6.3 %copy-start.2 = (f32[96,3072]{1,0:T(8,128)}, f32[96,3072]{1,0:T(8,128)S(1)}, u32[]{:S(2)}) copy-start(f32[96,3072]{1,0:T(8,128)S(1)} %collective-permute-done.before) | copy-start | bytes 3538948
  32.1 30.2 %collective-permute-start.3 = (f32[48,3072]{1,0:T(8,128)}, f32[48,3072]{1,0:T(8,128)S(1)}, u32[]{:S(2)}, u32[]{:S(2)}) collective-permute-start(f32[48,3072]{1,0:T(8,128)} %slice.9), channel_id=1, source_target_pairs={{0,3},{1,0},{2,1},{3,2},{4,7},{5,4},{6,5},{7,6},{8,11},{9,8},{10,9... | collective-permute-start | bytes 1769480 | tf_op jit(solution)/shard_map/ppermute | solution.py:25
  37.9 5.5 %copy-start.6 = (f32[96,1536]{1,0:T(8,128)}, f32[96,1536]{1,0:T(8,128)S(1)}, u32[]{:S(2)}) copy-start(f32[96,1536]{1,0:T(8,128)S(1)} %collective-permute-done.8.up2) | copy-start | bytes 1769476
  37.9 24.4 %collective-permute-start.2 = (f32[48,3072]{1,0:T(8,128)}, f32[48,3072]{1,0:T(8,128)S(1)}, u32[]{:S(2)}, u32[]{:S(2)}) collective-permute-start(f32[48,3072]{1,0:T(8,128)} %slice.8), channel_id=1, source_target_pairs={{0,1},{1,2},{2,3},{3,0},{4,5},{5,6},{6,7},{7,4},{8,9},{9,10},{10,1... | collective-permute-start | bytes 1769480 | tf_op jit(solution)/shard_map/ppermute | solution.py:25
  62.3 0.8 copy-start.3
  62.3 1.0 copy-start.4
  67.3 13.7 %all-to-all-start = ((f32[16,40,128]{2,1,0:T(8,128)}), f32[16,40,128]{2,1,0:T(8,128)S(1)}, u32[]{:S(2)}, u32[]{:S(2)}) async-start(f32[16,40,128]{2,1,0:T(8,128)} %get-tuple-element.37), calls=%async_computation | async-start | bytes 655360 | tf_op jit(solution)/shard_map/all_to_all | solution.py:283
  72.8 30.3 %copy-start = (f32[384,128]{1,0:T(8,128)S(1)}, f32[384,128]{1,0:T(8,128)}, u32[]{:S(2)}) copy-start(f32[384,128]{1,0:T(8,128)} %ritz.5) | copy-start | bytes 589828
  72.8 4.3 %collective-permute-start.12 = (f32[8,128]{1,0:T(8,128)}, f32[8,128]{1,0:T(8,128)S(1)}, u32[]{:S(2)}, u32[]{:S(2)}) collective-permute-start(f32[8,128]{1,0:T(8,128)} %get-tuple-element.38), channel_id=1, source_target_pairs={{0,3},{1,0},{2,1},{3,2},{4,7},{5,4},{6,5},{7,6},{8,11},{9,8},{10,9... | collective-permute-start | bytes 12296 | tf_op jit(solution)/shard_map/ppermute | solution.py:25
  76.2 4.2 %collective-permute-start.11 = (f32[8,128]{1,0:T(8,128)}, f32[8,128]{1,0:T(8,128)S(1)}, u32[]{:S(2)}, u32[]{:S(2)}) collective-permute-start(f32[8,128]{1,0:T(8,128)} %get-tuple-element.38), channel_id=1, source_target_pairs={{0,2},{1,3},{2,0},{3,1},{4,6},{5,7},{6,4},{7,5},{8,10},{9,11},{10,... | collective-permute-start | bytes 12296 | tf_op jit(solution)/shard_map/ppermute | solution.py:25
  76.2 4.2 %collective-permute-start.10 = (f32[8,128]{1,0:T(8,128)}, f32[8,128]{1,0:T(8,128)S(1)}, u32[]{:S(2)}, u32[]{:S(2)}) collective-permute-start(f32[8,128]{1,0:T(8,128)} %get-tuple-element.38), channel_id=1, source_target_pairs={{0,1},{1,2},{2,3},{3,0},{4,5},{5,6},{6,7},{7,4},{8,9},{9,10},{10,1... | collective-permute-start | bytes 12296 | tf_op jit(solution)/shard_map/ppermute | solution.py:25
  95.0 32.5 %all-to-all-start.2 = ((f32[16,48,128]{2,1,0:T(8,128)}), f32[16,48,128]{2,1,0:T(8,128)S(1)}, u32[]{:S(2)}, u32[]{:S(2)}) async-start(f32[16,48,128]{2,1,0:T(8,128)} %broadcast_in_dim.5), calls=%async_computation.2 | async-start | bytes 786432 | tf_op jit(solution)/shard_map/all_to_all | solution.py:298
  107.0 20.4 %collective-permute-start.13 = (f32[32,3072]{1,0:T(8,128)}, f32[32,3072]{1,0:T(8,128)S(1)}, u32[]{:S(2)}, u32[]{:S(2)}) collective-permute-start(f32[32,3072]{1,0:T(8,128)} %get-tuple-element.42), channel_id=1, source_target_pairs={{0,1},{1,2},{2,3},{3,0},{4,5},{5,6},{6,7},{7,4},{8,9},{9,10},{10,1... | collective-permute-start | bytes 1179656 | tf_op jit(solution)/shard_map/ppermute | solution.py:25
  107.0 20.4 %collective-permute-start.14 = (f32[32,3072]{1,0:T(8,128)}, f32[32,3072]{1,0:T(8,128)S(1)}, u32[]{:S(2)}, u32[]{:S(2)}) collective-permute-start(f32[32,3072]{1,0:T(8,128)} %get-tuple-element.43), channel_id=1, source_target_pairs={{0,3},{1,0},{2,1},{3,2},{4,7},{5,4},{6,5},{7,6},{8,11},{9,8},{10,9... | collective-permute-start | bytes 1179656 | tf_op jit(solution)/shard_map/ppermute | solution.py:25
  109.7 17.7 %collective-permute-start.15 = (f32[32,3072]{1,0:T(8,128)}, f32[32,3072]{1,0:T(8,128)S(1)}, u32[]{:S(2)}, u32[]{:S(2)}) collective-permute-start(f32[32,3072]{1,0:T(8,128)} %get-tuple-element.44), channel_id=1, source_target_pairs={{0,2},{1,3},{2,0},{3,1},{4,6},{5,7},{6,4},{7,5},{8,10},{9,11},{10,... | collective-permute-start | bytes 1179656 | tf_op jit(solution)/shard_map/ppermute | solution.py:25
  127.4 0.7 copy-start.7
  127.4 0.9 copy-start.8
  127.4 1.0 copy-start.9
  127.4 1.2 copy-start.5

commit v2 on v1

--- a/solution.py
+++ b/solution.py
@@ -38,6 +38,23 @@
     return first[:rows] + (first[rows:] + one(ah, bl))
 
 
+def lane_tile(x):
+    short = LANES - x.shape[0]
+    return jnp.concatenate([x, jnp.zeros((short, x.shape[1]), x.dtype)], axis=0) if short else x
+
+
+def dot4(a, b):
+    both = lax.dot_general(
+        jnp.concatenate(a, axis=0),
+        jnp.concatenate([lane_tile(b[0]), lane_tile(b[1])], axis=0),
+        NT,
+        preferred_element_type=F32,
+    )
+    rows = a[0].shape[0]
+    both = both[:rows] + both[rows:]
+    return both[:, :LANES] + both[:, LANES:]
+
+
 def low_half(shape):
     return lax.broadcasted_iota(jnp.int32, shape, 1) < BLOCK
 
@@ -60,12 +77,21 @@
     lax.fori_loop(0, to_prev2.shape[1] // LANES, step, 0, unroll=4)
 
 
-def image_kernel(base, cols, st, up1, down1, up2, down2, values, high, low):
+def image_kernel(
+    col, base, cols, st, up1, down1, up2, down2, values, high, low, send, ritz,
+    image_high, image_low, gram, terms, part_own, part_after, part_opp, part_before, sums
+):
     m = pl.program_id(0)
     width = st.shape[0]
     pairs = values.shape[0] // LANES
     left_half = low_half((width, LANES))
     flip = lambda x: pltpu.roll(x, BLOCK, 1)
+    images = []
+
+    @pl.when(m == 0)
+    def _():
+        sums[...] = jnp.zeros_like(sums)
+
     for h in range(pairs):
         tile = m * pairs + h
         own = st[:, pl.ds(pl.multiple_of(tile * LANES, LANES), LANES)]
@@ -84,11 +110,23 @@
             one = one if q == 0 else flip(one)
             two = flip(two) if side == 0 else two
             right.append(jnp.concatenate([one, two], axis=1))
-        part = dot3(
-            split(jnp.concatenate(left, axis=0)), split(jnp.concatenate(right, axis=0)), NT
-        )
-        image = 4.0 * own + jnp.where(left_half, part[:width], part[width:])
-        high[:, h * LANES : (h + 1) * LANES], low[:, h * LANES : (h + 1) * LANES] = split(image)
+        part = dot4(split(jnp.concatenate(left, axis=0)), split(jnp.concatenate(right, axis=0)))
+        images.append(split(4.0 * own + jnp.where(left_half, part[:width], part[width:])))
+        if h % 2:
+            span = slice((h - 1) * LANES, (h + 1) * LANES)
+            image = tuple(jnp.concatenate([images[h - 1][i], images[h][i]], axis=1) for i in range(2))
+            image_high[:, span], image_low[:, span] = image
+            sums[...] += dot4((high[:, span], low[:, span]), image)
+            part = dot3(split(send[...]), image, NN)
+            modes = part_own.shape[0]
+            for i, out in enumerate((part_own, part_after, part_opp, part_before)):
+                out[:, span] = part[i * modes : (i + 1) * modes]
+
+    @pl.when(m == pl.num_programs(0) - 1)
+    def _():
+        for i in range(3):
+            gram[i] = sums[i * width : (i + 1) * width, :width]
+        piece_terms(gram, col[0], ritz, terms)
 
 
 def quotient_terms(piece, mine, ritz, start):
@@ -109,17 +147,9 @@
     width = st.shape[0]
     for i, piece in enumerate((st, before, after)):
         high[i * width : (i + 1) * width, :], low[i * width : (i + 1) * width, :] = split(piece[...])
-    block = dot3((high[...], low[...]), (high[:width, :], low[:width, :]), NT)
+    block = dot4((high[...], low[...]), (high[:width, :], low[:width, :]))
     for i in range(3):
-        gram[i] = block[i * width : (i + 1) * width]
-    piece_terms(gram, col[0], ritz, terms)
-
-
-def stiff_kernel(col, high, low, image_high, image_low, ritz, gram, terms):
-    width = image_high.shape[0]
-    block = dot3((high[...], low[...]), (image_high[...], image_low[...]), NT)
-    for i in range(3):
-        gram[i] = block[i * width : (i + 1) * width]
+        gram[i] = block[i * width : (i + 1) * width, :width]
     piece_terms(gram, col[0], ritz, terms)
 
 
@@ -129,22 +159,17 @@
 ):
     c = col[0]
     width = st_high.shape[0]
-    far = dot3(
-        split(jnp.concatenate([opp_a[...], opp_b[...]], axis=0)),
-        (
-            jnp.concatenate([image_high[...], st_high[...]], axis=0),
-            jnp.concatenate([image_low[...], st_low[...]], axis=0),
-        ),
-        NT,
-    )
+    far = split(jnp.concatenate([opp_a[...], opp_b[...]], axis=0))
+    far_stiff = dot4(far, (image_high[...], image_low[...]))[:, :width]
+    far_mass = dot4(far, (st_high[...], st_low[...]))[:, :width]
     terms[...] = jnp.zeros_like(terms)
     at = lambda by: pl.multiple_of((c + by) % 4 * width, 8)
     mine = ritz[pl.ds(at(0), width), :]
     turned = []
     for i, (block, whole, pieces, sums) in enumerate(
         (
-            (far[:, :width], stiff, stiff3, stiff_terms),
-            (far[:, width:], mass, mass3, mass_terms),
+            (far_stiff, stiff, stiff3, stiff_terms),
+            (far_mass, mass, mass3, mass_terms),
         )
     ):
         for piece, by in ((pieces[0], 0), (pieces[1], 3), (pieces[2], 1), (block, 2)):
@@ -168,13 +193,6 @@
     )
 
 
-def image_part_kernel(high, low, coef, own, after, opp, before):
-    part = dot3(split(coef[...]), (high[...], low[...]), NN)
-    modes = own.shape[0]
-    for i, out in enumerate((own, after, opp, before)):
-        out[...] = part[i * modes : (i + 1) * modes]
-
-
 def final_kernel(col, parts, modes, own, from_prev, from_next, from_opp, stiff, mass, theta, residual):
     total = jnp.float32(196608.0)
     terms = parts[0, 8 * TILES :, :]
@@ -257,20 +275,26 @@
 
     tile = lambda n: pl.BlockSpec((width, n), lambda m: (0, m))
     whole = pl.BlockSpec((width, rows), lambda m: (0, 0))
-    image = call(
+    step_lanes = PAIRS * LANES
+    *image, stiff3, stiff_terms, part_own, part_after, part_opp, part_before = call(
         image_kernel,
-        [(width, rows)] * 2,
-        [SMEM, SMEM, whole, whole, whole]
-        + [tile(PAIRS // 2 * LANES)] * 2
-        + [pl.BlockSpec((PAIRS * LANES, values.shape[1]), lambda m: (m, 0))],
-        [jnp.bfloat16] * 2,
-        out_specs=[tile(PAIRS * LANES)] * 2,
-        grid=(rows // (PAIRS * LANES),),
-    )(base, cols, st, up1, down1, up2, down2, values)
-
-    stiff3, stiff_terms = call(
-        stiff_kernel, [(3, width, width), (1, LANES)], [SMEM] + [VMEM] * 5
-    )(col, high, low, *image, ritz)
+        [(width, rows)] * 2 + [(3, width, width), (1, LANES)] + [(modes, rows)] * 4,
+        [SMEM] * 3
+        + [whole] * 3
+        + [tile(step_lanes // 2)] * 2
+        + [pl.BlockSpec((step_lanes, values.shape[1]), lambda m: (m, 0))]
+        + [pl.BlockSpec((3 * width, step_lanes), lambda m: (0, m))] * 2
+        + [VMEM] * 2,
+        [jnp.bfloat16] * 2 + [F32] * 6,
+        out_specs=[tile(step_lanes)] * 2
+        + [
+            pl.BlockSpec((3, width, width), lambda m: (0, 0, 0)),
+            pl.BlockSpec((1, LANES), lambda m: (0, 0)),
+        ]
+        + [pl.BlockSpec((modes, step_lanes), lambda m: (0, m))] * 4,
+        grid=(rows // step_lanes,),
+        scratch_shapes=[pltpu.VMEM((3 * width, LANES), F32)],
+    )(col, base, cols, st, up1, down1, up2, down2, values, high, low, send, ritz)
 
     payload, terms = call(
         late_kernel,
@@ -282,8 +306,6 @@
 
     got = lax.all_to_all(payload, RING, 0, 0, tiled=True)
     around = [shifted(terms, "col", by) for by in (1, 2, 3)]
-    image, stiff3 = lax.optimization_barrier((image, stiff3))
-    part_own, part_after, part_opp, part_before = call(image_part_kernel, [(modes, rows)] * 4, [VMEM] * 3)(*image, send)
     from_prev = shifted(part_after, "col", 1)
     from_next = shifted(part_before, "col", -1)
     from_opp = shifted(part_opp, "col", 2)

time: 132 us -> 128 us (0.970)
  Pallas kernels: 34.8 us -> 30 us
  starting transfers between devices: 40.3 us -> 41.8 us
  waiting for transfers between devices: 33.6 us -> 32.1 us
    pallas_call x3 -> x1, Pallas kernels: 16 us -> 11.4 us  [shards(): call(image_kernel, [(width, rows)] * 2 + [(3, width, width), (1, LANES)]...]
    ppermute x16, waiting for transfers between devices: 33.6 us -> 32.1 us  [shifted(): lax.ppermute(array, axis, [(i, (i + by) % length) for i in range(length)])]
    unnamed x29 -> x35, local copies, waits for them, and re-layouts: 3.15 us -> 3.11 us
  transfers between devices with their start and end apart: 18 -> 18, of which waited for: 9 -> 9; matrix products, arithmetic and copies ran while one was open for 4% -> 5% of each run, Pallas kernels for 22% -> 18%
where the time goes in v2:
time: 128 us; the launch traced here: 127 us
  starting transfers between devices  41.8 us (33%)
  waiting for transfers between devices  32.1 us (25%)
  Pallas kernels  30 us (23%)
  blocking collectives  13.2 us (10%)
  local copies, waits for them, and re-layouts  6.63 us (5%)
  other arithmetic  2.69 us (2%)
    ppermute x16, waiting for transfers between devices, shifted(): lax.ppermute(array, axis, [(i, (i + by) % length) for i in range(length)])  32.1 us
    ppermute x16, starting transfers between devices, shifted(): lax.ppermute(array, axis, [(i, (i + by) % length) for i in range(length)])  27.5 us
    all_to_all x1, blocking collectives, shards(): part = lax.all_to_all(part, 'zh', 0, 0, tiled=True)  13.2 us
    pallas_call x1, Pallas kernels, shards(): call(image_kernel, [(width, rows)] * 2 + [(3, width, width), (1, LANES)]...  11.4 us
    all_to_all x1, starting transfers between devices, shards(): parts = lax.all_to_all(spread_out(part), RING, 0, 0, tiled=True)  8.29 us
    all_to_all x1, starting transfers between devices, shards(): got = lax.all_to_all(payload, RING, 0, 0, tiled=True)  6 us
    pallas_call x1, Pallas kernels, shards(): call(mass_kernel, [(3 * width, rows), (3 * width, rows), (3, width, width...  4.77 us
    pallas_call x1, Pallas kernels, shards(): call(modes_kernel, [(modes, rows)], [VMEM] * 5)  4.13 us
  transfers between devices with their start and end apart: 18, of which 9 were waited for; matrix products, arithmetic and copies ran while one was open for 5% of the time, Pallas kernels for 18%

profile of v2, /device:TPU:1, one launch (start us, length us, event | category | flops | bytes accessed | tf_op | source)
XLA Modules:
  0.0 127.2 jit_solution(361744313368803136)
XLA Ops:
  0.6 3.4 %collective-permute-start.1 = (f32[96,3072]{1,0:T(8,128)}, f32[96,3072]{1,0:T(8,128)S(1)}, u32[]{:S(2)}, u32[]{:S(2)}) collective-permute-start(f32[96,3072]{1,0:T(8,128)} %bitcast.16), channel_id=1, source_target_pairs={{0,3},{1,0},{2,1},{3,2},{4,7},{5,4},{6,5},{7,6},{8,11},{9,8},{10,9... | collective-permute-start | bytes 3538952 | tf_op jit(solution)/shard_map/ppermute | solution.py:25
  4.0 8.0 %collective-permute-start.7 = (s32[4,48]{1,0:T(4,128)}, s32[4,48]{1,0:T(4,128)S(1)}, u32[]{:S(2)}, u32[]{:S(2)}) collective-permute-start(s32[4,48]{1,0:T(4,128)} %bitcast.29), channel_id=1, source_target_pairs={{0,248},{4,252},{8,0},{12,4},{16,8},{20,12},{24,16},{28,20},{32,24... | collective-permute-start | bytes 2312 | tf_op jit(solution)/shard_map/ppermute | solution.py:25
  12.0 0.9 collective-permute-done.7.next2
  13.0 1.8 %collective-permute-start.4 = (f32[96,3072]{1,0:T(8,128)}, f32[96,3072]{1,0:T(8,128)}, u32[]{:S(2)}, u32[]{:S(2)}) collective-permute-start(f32[96,3072]{1,0:T(8,128)} %bitcast.19), channel_id=1, source_target_pairs={{0,252},{4,0},{8,4},{12,8},{16,12},{20,16},{24,20},{28,24},{32,28}... | collective-permute-start | bytes 3538952 | tf_op jit(solution)/shard_map/ppermute | solution.py:25
  15.4 2.6 %collective-permute-done.6.prev2 = s32[4,48]{1,0:T(4,128)S(1)} collective-permute-done((s32[4,48]{1,0:T(4,128)}, s32[4,48]{1,0:T(4,128)S(1)}, u32[]{:S(2)}, u32[]{:S(2)}) %collective-permute-start.6) | collective-permute-done | bytes 800 | tf_op jit(solution)/shard_map/ppermute | solution.py:25
  18.6 3.1 %shard_map.85 = (f32[96,1536]{1,0:T(8,128)}, f32[96,1536]{1,0:T(8,128)}) custom-call(s32[3]{0:T(128)} %add_multiply_fusion.base, s32[4,48]{1,0:T(4,128)} %copy-done.11, s32[4,48]{1,0:T(4,128)} %copy-done.10, f32[96,3072]{1,0:T(8,128)} %bitcast.20), custom_call_target="tpu_custom_call" | custom-call | tf_op jit(solution)/shard_map/pallas_call | solution.py:255
  21.7 2.7 %collective-permute-start.8 = (f32[96,1536]{1,0:T(8,128)}, f32[96,1536]{1,0:T(8,128)S(1)}, u32[]{:S(2)}, u32[]{:S(2)}) collective-permute-start(f32[96,1536]{1,0:T(8,128)} %get-tuple-element.27), channel_id=1, source_target_pairs={{0,248},{4,252},{8,0},{12,4},{16,8},{20,12},{24,16},{28,20},{32,24... | collective-permute-start | bytes 1769480 | tf_op jit(solution)/shard_map/ppermute | solution.py:25
  24.4 4.6 %collective-permute-done.1.after = f32[96,3072]{1,0:T(8,128)S(1)} collective-permute-done((f32[96,3072]{1,0:T(8,128)}, f32[96,3072]{1,0:T(8,128)S(1)}, u32[]{:S(2)}, u32[]{:S(2)}) %collective-permute-start.1) | collective-permute-done | bytes 1179680 | tf_op jit(solution)/shard_map/ppermute | solution.py:25
  29.0 1.3 %collective-permute-start.9 = (f32[96,1536]{1,0:T(8,128)}, f32[96,1536]{1,0:T(8,128)}, u32[]{:S(2)}, u32[]{:S(2)}) collective-permute-start(f32[96,1536]{1,0:T(8,128)} %get-tuple-element.28), channel_id=1, source_target_pairs={{0,8},{4,12},{8,16},{12,20},{16,24},{20,28},{24,32},{28,36},{32,40... | collective-permute-start | bytes 1769480 | tf_op jit(solution)/shard_map/ppermute | solution.py:25
  30.3 0.8 slice.9
  31.1 1.0 collective-permute-done.before
  32.1 2.3 %collective-permute-start.3 = (f32[48,3072]{1,0:T(8,128)}, f32[48,3072]{1,0:T(8,128)S(1)}, u32[]{:S(2)}, u32[]{:S(2)}) collective-permute-start(f32[48,3072]{1,0:T(8,128)} %slice.9), channel_id=1, source_target_pairs={{0,3},{1,0},{2,1},{3,2},{4,7},{5,4},{6,5},{7,6},{8,11},{9,8},{10,9... | collective-permute-start | bytes 1769480 | tf_op jit(solution)/shard_map/ppermute | solution.py:25
  34.4 0.9 slice.8
  35.4 2.5 %collective-permute-done.8.up2 = f32[96,1536]{1,0:T(8,128)S(1)} collective-permute-done((f32[96,1536]{1,0:T(8,128)}, f32[96,1536]{1,0:T(8,128)S(1)}, u32[]{:S(2)}, u32[]{:S(2)}) %collective-permute-start.8) | collective-permute-done | bytes 589856 | tf_op jit(solution)/shard_map/ppermute | solution.py:25
  38.4 0.8 constant_dynamic-slice_fusion
  39.9 4.8 %shard_map.83 = (bf16[288,3072]{1,0:T(8,128)(2,1)}, bf16[288,3072]{1,0:T(8,128)(2,1)}, f32[3,96,96]{2,1,0:T(8,128)}, f32[1,128]{1,0:T(1,128)}) custom-call(s32[1]{0:T(128)} %bitcast.col, f32[96,3072]{1,0:T(8,128)} %bitcast.21, f32[96,3072]{1,0:T(8,128)} %copy-done.2, f32[96,3072]{1,0:T(8,128)} %copy-done.1, f32[384,128]{1,0:T(8,128)} %ritz.5), custom_call_target="tpu_custom_call" | custom-call | tf_op jit(solution)/shard_map/pallas_call | solution.py:269
  44.7 4.8 %collective-permute-done.9.down2 = f32[96,1536]{1,0:T(8,128)} collective-permute-done((f32[96,1536]{1,0:T(8,128)}, f32[96,1536]{1,0:T(8,128)}, u32[]{:S(2)}, u32[]{:S(2)}) %collective-permute-start.9) | collective-permute-done | bytes 589856 | tf_op jit(solution)/shard_map/ppermute | solution.py:25
  49.5 11.4 %shard_map.86 = (bf16[96,3072]{1,0:T(8,128)(2,1)}, bf16[96,3072]{1,0:T(8,128)(2,1)}, f32[3,96,96]{2,1,0:T(8,128)}, f32[1,128]{1,0:T(1,128)}, f32[32,3072]{1,0:T(...) custom-call(s32[1]{0:T(128)} %bitcast.col, s32[3]{0:T(128)} %add_multiply_fusion.base, ...), custom_call_target="tpu_custom_call" | custom-call | tf_op jit(solution)/shard_map/pallas_call | solution.py:279
  60.9 0.8 copy-done.3
  61.9 4.0 %shard_map.87 = (f32[16,40,128]{2,1,0:T(8,128)}, f32[8,128]{1,0:T(8,128)}) custom-call(s32[1]{0:T(128)} %bitcast.col, f32[3,96,96]{2,1,0:T(8,128)} %get-tuple-element.29.stiff3, f32[1,128]{1,0:T(1,128)} %get-tuple-element.30.stiff_terms, f32[3,96,96]{2,1,0:T(8,128)} %get-tuple-element.31.mass3, f32[1,128]{1,0:T(1,128)} %get-tuple-element.32.mass_terms, ...), custom_call_target="tpu_custom_call" | custom-call | tf_op jit(solution)/shard_map/pallas_call | solution.py:299
  65.9 6.0 %all-to-all-start = ((f32[16,40,128]{2,1,0:T(8,128)}), f32[16,40,128]{2,1,0:T(8,128)S(1)}, u32[]{:S(2)}, u32[]{:S(2)}) async-start(f32[16,40,128]{2,1,0:T(8,128)} %get-tuple-element.35), calls=%async_computation | async-start | bytes 655360 | tf_op jit(solution)/shard_map/all_to_all | solution.py:307
  71.9 3.0 %collective-permute-start.12 = (f32[8,128]{1,0:T(8,128)}, f32[8,128]{1,0:T(8,128)S(1)}, u32[]{:S(2)}, u32[]{:S(2)}) collective-permute-start(f32[8,128]{1,0:T(8,128)} %get-tuple-element.36), channel_id=1, source_target_pairs={{0,3},{1,0},{2,1},{3,2},{4,7},{5,4},{6,5},{7,6},{8,11},{9,8},{10,9... | collective-permute-start | bytes 12296 | tf_op jit(solution)/shard_map/ppermute | solution.py:25
  74.9 1.0 collective-permute-start.11
  76.7 2.4 %collective-permute-done.11 = f32[8,128]{1,0:T(8,128)S(1)} collective-permute-done((f32[8,128]{1,0:T(8,128)}, f32[8,128]{1,0:T(8,128)S(1)}, u32[]{:S(2)}, u32[]{:S(2)}) %collective-permute-start.11) | collective-permute-done | bytes 4128 | tf_op jit(solution)/shard_map/ppermute | solution.py:25
  79.1 1.0 collective-permute-done.10
  80.9 13.2 %all_to_all.15 = f32[4,48,128]{2,1,0:T(8,128)S(1)} all-to-all(f32[4,48,128]{2,1,0:T(8,128)S(1)} %broadcast_in_dim.4), channel_id=1, replica_groups=mesh['zh'=4,'zl'=2,'y'=4,'core'=2,'col'=4] {'zh'}, dimensions={0} | all-to-all | bytes 196608 | tf_op jit(solution)/shard_map/all_to_all | solution.py:318
  94.1 0.8 broadcast_in_dim.5
  94.9 8.3 %all-to-all-start.2 = ((f32[16,48,128]{2,1,0:T(8,128)}), f32[16,48,128]{2,1,0:T(8,128)S(1)}, u32[]{:S(2)}, u32[]{:S(2)}) async-start(f32[16,48,128]{2,1,0:T(8,128)} %broadcast_in_dim.5), calls=%async_computation.2 | async-start | bytes 786432 | tf_op jit(solution)/shard_map/all_to_all | solution.py:320
  103.3 2.7 %collective-permute-start.14 = (f32[32,3072]{1,0:T(8,128)S(1)}, f32[32,3072]{1,0:T(8,128)S(1)}, u32[]{:S(2)}, u32[]{:S(2)}) collective-permute-start(f32[32,3072]{1,0:T(8,128)S(1)} %copy-done.13), channel_id=1, source_target_pairs={{0,3},{1,0},{2,1},{3,2},{4,7},{5,4},{6,5},{7,6},{8,11},{9,8},{10,9... | collective-permute-start | bytes 1179656 | tf_op jit(solution)/shard_map/ppermute | solution.py:25
  107.1 4.1 %shard_map.84.modes = f32[32,3072]{1,0:T(8,128)} custom-call(bf16[288,3072]{1,0:T(8,128)(2,1)} %get-tuple-element.25.high.st_high, bf16[288,3072]{1,0:T(8,128)(2,1)} %get-tuple-element.26.low.st_low, f32[48,3072]{1,0:T(8,128)} %copy-done.4, f32[48,3072]{1,0:T(8,128)} %copy-done.3, f32[32,384]{1,0:T(8,128)} %pad_maximum_fusion.coef), custom_call_target="tpu_custom_call" | custom-call | tf_op jit(solution)/shard_map/pallas_call | solution.py:312
  111.2 12.2 %collective-permute-done.13.from_prev = f32[32,3072]{1,0:T(8,128)S(1)} collective-permute-done((f32[32,3072]{1,0:T(8,128)S(1)}, f32[32,3072]{1,0:T(8,128)S(1)}, u32[]{:S(2)}, u32[]{:S(2)}) %collective-permute-start.13) | collective-permute-done | bytes 393248 | tf_op jit(solution)/shard_map/ppermute | solution.py:25
  124.6 2.6 %shard_map.88 = (f32[96,384]{1,0:T(8,128)}, f32[96,384]{1,0:T(8,128)}, f32[1,32]{1,0:T(1,128)}, f32[32,3072]{1,0:T(8,128)}) custom-call(s32[1]{0:T(128)} %bitcast.col, f32[16,48,128]{2,1,0:T(8,128)} %copy-done.5, f32[32,3072]{1,0:T(8,128)} %shard_map.84.modes, f32[32,3072]{1,0:T(8,128)} %get-tuple-element.37.own, f32[32,3072]{1,0:T(8,128)} %copy-done.7, ...), custom_call_target="tpu_custom_call" | custom-call | tf_op jit(solution)/shard_map/pallas_call | solution.py:322
  (59 shorter events, 6.5 us)
Async XLA Ops:
  0.6 28.3 %collective-permute-start.1 = (f32[96,3072]{1,0:T(8,128)}, f32[96,3072]{1,0:T(8,128)S(1)}, u32[]{:S(2)}, u32[]{:S(2)}) collective-permute-start(f32[96,3072]{1,0:T(8,128)} %bitcast.16), channel_id=1, source_target_pairs={{0,3},{1,0},{2,1},{3,2},{4,7},{5,4},{6,5},{7,6},{8,11},{9,8},{10,9... | collective-permute-start | bytes 3538952 | tf_op jit(solution)/shard_map/ppermute | solution.py:25
  4.0 28.1 %collective-permute-start = (f32[96,3072]{1,0:T(8,128)}, f32[96,3072]{1,0:T(8,128)S(1)}, u32[]{:S(2)}, u32[]{:S(2)}) collective-permute-start(f32[96,3072]{1,0:T(8,128)} %bitcast.17), channel_id=1, source_target_pairs={{0,1},{1,2},{2,3},{3,0},{4,5},{5,6},{6,7},{7,4},{8,9},{9,10},{10,1... | collective-permute-start | bytes 3538952 | tf_op jit(solution)/shard_map/ppermute | solution.py:25
  4.0 9.0 %collective-permute-start.7 = (s32[4,48]{1,0:T(4,128)}, s32[4,48]{1,0:T(4,128)S(1)}, u32[]{:S(2)}, u32[]{:S(2)}) collective-permute-start(s32[4,48]{1,0:T(4,128)} %bitcast.29), channel_id=1, source_target_pairs={{0,248},{4,252},{8,0},{12,4},{16,8},{20,12},{24,16},{28,20},{32,24... | collective-permute-start | bytes 2312 | tf_op jit(solution)/shard_map/ppermute | solution.py:25
  12.0 6.0 %collective-permute-start.6 = (s32[4,48]{1,0:T(4,128)}, s32[4,48]{1,0:T(4,128)S(1)}, u32[]{:S(2)}, u32[]{:S(2)}) collective-permute-start(s32[4,48]{1,0:T(4,128)} %bitcast.30), channel_id=1, source_target_pairs={{0,8},{4,12},{8,16},{12,20},{16,24},{20,28},{24,32},{28,36},{32,40... | collective-permute-start | bytes 2312 | tf_op jit(solution)/shard_map/ppermute | solution.py:25
  12.0 37.5 %collective-permute-start.5 = (f32[96,3072]{1,0:T(8,128)}, f32[96,3072]{1,0:T(8,128)}, u32[]{:S(2)}, u32[]{:S(2)}) collective-permute-start(f32[96,3072]{1,0:T(8,128)} %bitcast.18), channel_id=1, source_target_pairs={{0,4},{4,8},{8,12},{12,16},{16,20},{20,24},{24,28},{28,32},{32,36}... | collective-permute-start | bytes 3538952 | tf_op jit(solution)/shard_map/ppermute | solution.py:25
  13.0 5.0 %copy-start.10 = (s32[4,48]{1,0:T(4,128)}, s32[4,48]{1,0:T(4,128)S(1)}, u32[]{:S(2)}) copy-start(s32[4,48]{1,0:T(4,128)S(1)} %collective-permute-done.7.next2) | copy-start | bytes 2308
  13.0 36.5 %collective-permute-start.4 = (f32[96,3072]{1,0:T(8,128)}, f32[96,3072]{1,0:T(8,128)}, u32[]{:S(2)}, u32[]{:S(2)}) collective-permute-start(f32[96,3072]{1,0:T(8,128)} %bitcast.19), channel_id=1, source_target_pairs={{0,252},{4,0},{8,4},{12,8},{16,12},{20,16},{24,20},{28,24},{32,28}... | collective-permute-start | bytes 3538952 | tf_op jit(solution)/shard_map/ppermute | solution.py:25
  21.7 16.2 %collective-permute-start.8 = (f32[96,1536]{1,0:T(8,128)}, f32[96,1536]{1,0:T(8,128)S(1)}, u32[]{:S(2)}, u32[]{:S(2)}) collective-permute-start(f32[96,1536]{1,0:T(8,128)} %get-tuple-element.27), channel_id=1, source_target_pairs={{0,248},{4,252},{8,0},{12,4},{16,8},{20,12},{24,16},{28,20},{32,24... | collective-permute-start | bytes 1769480 | tf_op jit(solution)/shard_map/ppermute | solution.py:25
  29.0 6.4 %copy-start.1 = (f32[96,3072]{1,0:T(8,128)}, f32[96,3072]{1,0:T(8,128)S(1)}, u32[]{:S(2)}) copy-start(f32[96,3072]{1,0:T(8,128)S(1)} %collective-permute-done.1.after) | copy-start | bytes 3538948
  29.0 20.5 %collective-permute-start.9 = (f32[96,1536]{1,0:T(8,128)}, f32[96,1536]{1,0:T(8,128)}, u32[]{:S(2)}, u32[]{:S(2)}) collective-permute-start(f32[96,1536]{1,0:T(8,128)} %get-tuple-element.28), channel_id=1, source_target_pairs={{0,8},{4,12},{8,16},{12,20},{16,24},{20,28},{24,32},{28,36},{32,40... | collective-permute-start | bytes 1769480 | tf_op jit(solution)/shard_map/ppermute | solution.py:25
  32.1 7.8 %copy-start.2 = (f32[96,3072]{1,0:T(8,128)}, f32[96,3072]{1,0:T(8,128)S(1)}, u32[]{:S(2)}) copy-start(f32[96,3072]{1,0:T(8,128)S(1)} %collective-permute-done.before) | copy-start | bytes 3538948
  32.1 28.8 %collective-permute-start.3 = (f32[48,3072]{1,0:T(8,128)}, f32[48,3072]{1,0:T(8,128)S(1)}, u32[]{:S(2)}, u32[]{:S(2)}) collective-permute-start(f32[48,3072]{1,0:T(8,128)} %slice.9), channel_id=1, source_target_pairs={{0,3},{1,0},{2,1},{3,2},{4,7},{5,4},{6,5},{7,6},{8,11},{9,8},{10,9... | collective-permute-start | bytes 1769480 | tf_op jit(solution)/shard_map/ppermute | solution.py:25
  37.9 6.8 %copy-start.6 = (f32[96,1536]{1,0:T(8,128)}, f32[96,1536]{1,0:T(8,128)S(1)}, u32[]{:S(2)}) copy-start(f32[96,1536]{1,0:T(8,128)S(1)} %collective-permute-done.8.up2) | copy-start | bytes 1769476
  37.9 23.0 %collective-permute-start.2 = (f32[48,3072]{1,0:T(8,128)}, f32[48,3072]{1,0:T(8,128)S(1)}, u32[]{:S(2)}, u32[]{:S(2)}) collective-permute-start(f32[48,3072]{1,0:T(8,128)} %slice.8), channel_id=1, source_target_pairs={{0,1},{1,2},{2,3},{3,0},{4,5},{5,6},{6,7},{7,4},{8,9},{9,10},{10,1... | collective-permute-start | bytes 1769480 | tf_op jit(solution)/shard_map/ppermute | solution.py:25
  60.9 0.8 copy-start.3
  60.9 1.0 copy-start.4
  65.9 14.9 %all-to-all-start = ((f32[16,40,128]{2,1,0:T(8,128)}), f32[16,40,128]{2,1,0:T(8,128)S(1)}, u32[]{:S(2)}, u32[]{:S(2)}) async-start(f32[16,40,128]{2,1,0:T(8,128)} %get-tuple-element.35), calls=%async_computation | async-start | bytes 655360 | tf_op jit(solution)/shard_map/all_to_all | solution.py:307
  71.9 31.3 %copy-start.14 = (f32[32,3072]{1,0:T(8,128)S(1)}, f32[32,3072]{1,0:T(8,128)}, u32[]{:S(2)}) copy-start(f32[32,3072]{1,0:T(8,128)} %get-tuple-element.38) | copy-start | bytes 1179652
  71.9 31.4 %copy-start.13 = (f32[32,3072]{1,0:T(8,128)S(1)}, f32[32,3072]{1,0:T(8,128)}, u32[]{:S(2)}) copy-start(f32[32,3072]{1,0:T(8,128)} %get-tuple-element.39) | copy-start | bytes 1179652
  71.9 34.0 %copy-start.12 = (f32[32,3072]{1,0:T(8,128)S(1)}, f32[32,3072]{1,0:T(8,128)}, u32[]{:S(2)}) copy-start(f32[32,3072]{1,0:T(8,128)} %get-tuple-element.40) | copy-start | bytes 1179652
  71.9 34.0 %copy-start = (f32[384,128]{1,0:T(8,128)S(1)}, f32[384,128]{1,0:T(8,128)}, u32[]{:S(2)}) copy-start(f32[384,128]{1,0:T(8,128)} %ritz.5) | copy-start | bytes 589828
  71.9 4.8 %collective-permute-start.12 = (f32[8,128]{1,0:T(8,128)}, f32[8,128]{1,0:T(8,128)S(1)}, u32[]{:S(2)}, u32[]{:S(2)}) collective-permute-start(f32[8,128]{1,0:T(8,128)} %get-tuple-element.36), channel_id=1, source_target_pairs={{0,3},{1,0},{2,1},{3,2},{4,7},{5,4},{6,5},{7,6},{8,11},{9,8},{10,9... | collective-permute-start | bytes 12296 | tf_op jit(solution)/shard_map/ppermute | solution.py:25
  74.9 4.2 %collective-permute-start.11 = (f32[8,128]{1,0:T(8,128)}, f32[8,128]{1,0:T(8,128)S(1)}, u32[]{:S(2)}, u32[]{:S(2)}) collective-permute-start(f32[8,128]{1,0:T(8,128)} %get-tuple-element.36), channel_id=1, source_target_pairs={{0,2},{1,3},{2,0},{3,1},{4,6},{5,7},{6,4},{7,5},{8,10},{9,11},{10,... | collective-permute-start | bytes 12296 | tf_op jit(solution)/shard_map/ppermute | solution.py:25
  75.9 4.2 %collective-permute-start.10 = (f32[8,128]{1,0:T(8,128)}, f32[8,128]{1,0:T(8,128)S(1)}, u32[]{:S(2)}, u32[]{:S(2)}) collective-permute-start(f32[8,128]{1,0:T(8,128)} %get-tuple-element.36), channel_id=1, source_target_pairs={{0,1},{1,2},{2,3},{3,0},{4,5},{5,6},{6,7},{7,4},{8,9},{9,10},{10,1... | collective-permute-start | bytes 12296 | tf_op jit(solution)/shard_map/ppermute | solution.py:25
  94.9 28.6 %all-to-all-start.2 = ((f32[16,48,128]{2,1,0:T(8,128)}), f32[16,48,128]{2,1,0:T(8,128)S(1)}, u32[]{:S(2)}, u32[]{:S(2)}) async-start(f32[16,48,128]{2,1,0:T(8,128)} %broadcast_in_dim.5), calls=%async_computation.2 | async-start | bytes 786432 | tf_op jit(solution)/shard_map/all_to_all | solution.py:320
  103.2 20.3 %collective-permute-start.13 = (f32[32,3072]{1,0:T(8,128)S(1)}, f32[32,3072]{1,0:T(8,128)S(1)}, u32[]{:S(2)}, u32[]{:S(2)}) collective-permute-start(f32[32,3072]{1,0:T(8,128)S(1)} %copy-done.14), channel_id=1, source_target_pairs={{0,1},{1,2},{2,3},{3,0},{4,5},{5,6},{6,7},{7,4},{8,9},{9,10},{10,1... | collective-permute-start | bytes 1179656 | tf_op jit(solution)/shard_map/ppermute | solution.py:25
  103.3 20.2 %collective-permute-start.14 = (f32[32,3072]{1,0:T(8,128)S(1)}, f32[32,3072]{1,0:T(8,128)S(1)}, u32[]{:S(2)}, u32[]{:S(2)}) collective-permute-start(f32[32,3072]{1,0:T(8,128)S(1)} %copy-done.13), channel_id=1, source_target_pairs={{0,3},{1,0},{2,1},{3,2},{4,7},{5,4},{6,5},{7,6},{8,11},{9,8},{10,9... | collective-permute-start | bytes 1179656 | tf_op jit(solution)/shard_map/ppermute | solution.py:25
  105.9 17.5 %collective-permute-start.15 = (f32[32,3072]{1,0:T(8,128)S(1)}, f32[32,3072]{1,0:T(8,128)S(1)}, u32[]{:S(2)}, u32[]{:S(2)}) collective-permute-start(f32[32,3072]{1,0:T(8,128)S(1)} %copy-done.12), channel_id=1, source_target_pairs={{0,2},{1,3},{2,0},{3,1},{4,6},{5,7},{6,4},{7,5},{8,10},{9,11},{10,... | collective-permute-start | bytes 1179656 | tf_op jit(solution)/shard_map/ppermute | solution.py:25
  123.5 0.7 copy-start.7
  123.5 0.9 copy-start.8
  123.5 1.0 copy-start.9
  123.5 1.1 copy-start.5
  (1 other events, 0.6 us)

commit v3 on v2

--- a/solution.py
+++ b/solution.py
@@ -78,8 +78,8 @@
 
 
 def image_kernel(
-    col, base, cols, st, up1, down1, up2, down2, values, high, low, send, ritz,
-    image_high, image_low, gram, terms, part_own, part_after, part_opp, part_before, sums
+    col, base, cols, st, up1, down1, up2, down2, values, high, low, ritz,
+    image_high, image_low, gram, terms, part_own, part_after, part_opp, part_before, sums, turned
 ):
     m = pl.program_id(0)
     width = st.shape[0]
@@ -91,7 +91,14 @@
     @pl.when(m == 0)
     def _():
         sums[...] = jnp.zeros_like(sums)
-
+        turned[...] = ritz[pl.ds(pl.multiple_of(col[0] * width, 8), width), :].T
+
+    modes = part_own.shape[0]
+    send = split(
+        jnp.concatenate(
+            [turned[pl.ds(pl.multiple_of((col[0] + i) % 4 * modes, 8), modes), :] for i in range(4)], axis=0
+        )
+    )
     for h in range(pairs):
         tile = m * pairs + h
         own = st[:, pl.ds(pl.multiple_of(tile * LANES, LANES), LANES)]
@@ -117,8 +124,7 @@
             image = tuple(jnp.concatenate([images[h - 1][i], images[h][i]], axis=1) for i in range(2))
             image_high[:, span], image_low[:, span] = image
             sums[...] += dot4((high[:, span], low[:, span]), image)
-            part = dot3(split(send[...]), image, NN)
-            modes = part_own.shape[0]
+            part = dot3(send, image, NN)
             for i, out in enumerate((part_own, part_after, part_opp, part_before)):
                 out[:, span] = part[i * modes : (i + 1) * modes]
 
@@ -143,10 +149,13 @@
     terms[...] = total + quotient_terms(gram[2], mine, ritz, at(1))
 
 
-def mass_kernel(col, st, before, after, ritz, high, low, gram, terms):
+def mass_kernel(col, st, before_a, before_b, after_a, after_b, ritz, high, low, gram, terms):
     width = st.shape[0]
-    for i, piece in enumerate((st, before, after)):
-        high[i * width : (i + 1) * width, :], low[i * width : (i + 1) * width, :] = split(piece[...])
+    at = 0
+    for piece in (st, before_a, before_b, after_a, after_b):
+        to = at + piece.shape[0]
+        high[at:to, :], low[at:to, :] = split(piece[...])
+        at = to
     block = dot4((high[...], low[...]), (high[:width, :], low[:width, :]))
     for i in range(3):
         gram[i] = block[i * width : (i + 1) * width, :width]
@@ -185,15 +194,23 @@
             payload[k, to : to + 8, :] = jnp.zeros((8, LANES), F32)
 
 
-def modes_kernel(high, low, opp_a, opp_b, coef, modes):
+def modes_kernel(
+    col, high, low, opp_a, opp_b, ritz, own, from_prev, from_next, from_opp, modes, image, turned
+):
     rest = high.shape[0]
+    width = rest // 3
+    coef = []
+    for by in (0, 3, 1, 2):
+        turned[...] = ritz[pl.ds(pl.multiple_of((col[0] + by) % 4 * width, 8), width), :].T
+        coef.append(turned[pl.ds(pl.multiple_of(col[0] * modes.shape[0], 8), modes.shape[0]), :])
     opp = jnp.concatenate([opp_a[...], opp_b[...]], axis=0)
-    modes[...] = dot3(split(coef[:, :rest]), (high[...], low[...]), NN) + dot3(
-        split(coef[:, rest:]), split(opp), NN
-    )
-
-
-def final_kernel(col, parts, modes, own, from_prev, from_next, from_opp, stiff, mass, theta, residual):
+    modes[...] = dot3(
+        split(jnp.concatenate(coef[:3], axis=1)), (high[...], low[...]), NN
+    ) + dot3(split(coef[3]), split(opp), NN)
+    image[...] = (own[...] + from_opp[...]) + (from_prev[...] + from_next[...])
+
+
+def final_kernel(col, parts, modes, image, stiff, mass, theta, residual):
     total = jnp.float32(196608.0)
     terms = parts[0, 8 * TILES :, :]
     for k in range(1, PARTS):
@@ -207,8 +224,7 @@
     theta[...] = pltpu.roll(
         jnp.broadcast_to(quotient, (8, LANES)), (4 - col[0]) % 4 * shape[0], 1
     )[0:1, : shape[0]]
-    image = (own[...] + from_opp[...]) + (from_prev[...] + from_next[...])
-    residual[...] = image - column * modes[...]
+    residual[...] = image[...] - column * modes[...]
     width = stiff.shape[0]
     for t in range(2 * width // 8 * 3):
         k, at = t // TILES, t % TILES * 8
@@ -245,10 +261,12 @@
     st = search.T
     cols = block_cols.T
 
-    before = shifted(st, "col", 1)
-    after = shifted(st, "col", -1)
     prev2 = shifted(cols, WIRE, 2)
     next2 = shifted(cols, WIRE, -2)
+    before_a = shifted(st[:half], "col", 1)
+    after_b = shifted(st[half:], "col", -1)
+    before_b = shifted(st[half:], "col", 1)
+    after_a = shifted(st[:half], "col", -1)
     up1 = shifted(st, WIRE, -1)
     down1 = shifted(st, WIRE, 1)
 
@@ -256,22 +274,15 @@
     up2 = shifted(packed[0], WIRE, -2)
     down2 = shifted(packed[1], WIRE, 2)
 
-    opp_a = shifted(before[:half], "col", 1)
-    opp_b = shifted(after[half:], "col", -1)
-
-    mine = lax.dynamic_slice_in_dim(ritz, c * modes, modes, 1).T
-    coef = jnp.concatenate(
-        [lax.dynamic_slice_in_dim(mine, (c + by) % 4 * width, width, 1) for by in (0, 3, 1, 2)], axis=1
-    )
-    ours = lax.dynamic_slice_in_dim(ritz, c * width, width, 0).T
-    send = jnp.roll(ours, -c * modes, 0)
+    opp_a = shifted(before_a, "col", 1)
+    opp_b = shifted(after_b, "col", -1)
 
     high, low, mass3, mass_terms = call(
         mass_kernel,
         [(3 * width, rows), (3 * width, rows), (3, width, width), (1, LANES)],
-        [SMEM] + [VMEM] * 4,
+        [SMEM] + [VMEM] * 6,
         [jnp.bfloat16, jnp.bfloat16, F32, F32],
-    )(col, st, before, after, ritz)
+    )(col, st, before_a, before_b, after_a, after_b, ritz)
 
     tile = lambda n: pl.BlockSpec((width, n), lambda m: (0, m))
     whole = pl.BlockSpec((width, rows), lambda m: (0, 0))
@@ -284,7 +295,7 @@
         + [tile(step_lanes // 2)] * 2
         + [pl.BlockSpec((step_lanes, values.shape[1]), lambda m: (m, 0))]
         + [pl.BlockSpec((3 * width, step_lanes), lambda m: (0, m))] * 2
-        + [VMEM] * 2,
+        + [VMEM],
         [jnp.bfloat16] * 2 + [F32] * 6,
         out_specs=[tile(step_lanes)] * 2
         + [
@@ -293,8 +304,8 @@
         ]
         + [pl.BlockSpec((modes, step_lanes), lambda m: (0, m))] * 4,
         grid=(rows // step_lanes,),
-        scratch_shapes=[pltpu.VMEM((3 * width, LANES), F32)],
-    )(col, base, cols, st, up1, down1, up2, down2, values, high, low, send, ritz)
+        scratch_shapes=[pltpu.VMEM((3 * width, LANES), F32), pltpu.VMEM((4 * modes, width), F32)],
+    )(col, base, cols, st, up1, down1, up2, down2, values, high, low, ritz)
 
     payload, terms = call(
         late_kernel,
@@ -309,7 +320,12 @@
     from_prev = shifted(part_after, "col", 1)
     from_next = shifted(part_before, "col", -1)
     from_opp = shifted(part_opp, "col", 2)
-    new_modes = call(modes_kernel, [(modes, rows)], [VMEM] * 5)(high, low, opp_a, opp_b, coef)[0]
+    new_modes, new_image = call(
+        modes_kernel,
+        [(modes, rows)] * 2,
+        [SMEM] + [VMEM] * 9,
+        scratch_shapes=[pltpu.VMEM((4 * modes, width), F32)],
+    )(col, high, low, opp_a, opp_b, ritz, part_own, from_prev, from_next, from_opp)
 
     part = jnp.concatenate(
         [jnp.sum(got, axis=0), terms + around[0] + around[1] + around[2]], axis=0
@@ -322,8 +338,8 @@
     stiff, mass, theta, residual = call(
         final_kernel,
         [(width, 4 * width), (width, 4 * width), (1, modes), (modes, rows)],
-        [SMEM] + [VMEM] * 6,
-    )(col, parts, new_modes, part_own, from_prev, from_next, from_opp)
+        [SMEM] + [VMEM] * 3,
+    )(col, parts, new_modes, new_image)
     return (new_modes.T, residual.T, theta[0], stiff.T, mass.T)
 
 

time: 128 us -> 137 us (1.070)
  starting transfers between devices: 41.8 us -> 47.4 us
  waiting for transfers between devices: 32.1 us -> 36 us
    ppermute x16 -> x18, starting transfers between devices: 27.5 us -> 31.7 us  [shifted(): lax.ppermute(array, axis, [(i, (i + by) % length) for i in range(length)])]
    ppermute x16 -> x18, waiting for transfers between devices: 32.1 us -> 36 us  [shifted(): lax.ppermute(array, axis, [(i, (i + by) % length) for i in range(length)])]
    concatenate x2 -> x0, other arithmetic: 1.39 us -> none  [the longest x1 0.74 us: shards(): jnp.concatenate([lax.dynamic_slice_in_dim(mine, (c + by) % 4 * width, wid...]
    unnamed x35 -> x32, local copies, waits for them, and re-layouts: 3.11 us -> 3.86 us
  transfers between devices with their start and end apart: 18 -> 20, of which waited for: 9 -> 7; matrix products, arithmetic and copies ran while one was open for 5% -> 1% of each run, Pallas kernels for 18% -> 18%
where the time goes in v3:
time: 137 us; the launch traced here: 136 us
  starting transfers between devices  47.4 us (35%)
  waiting for transfers between devices  36 us (26%)
  Pallas kernels  30.6 us (22%)
  blocking collectives  13.4 us (10%)
  local copies, waits for them, and re-layouts  7.08 us (5%)
    ppermute x18, waiting for transfers between devices, shifted(): lax.ppermute(array, axis, [(i, (i + by) % length) for i in range(length)])  36 us
    ppermute x18, starting transfers between devices, shifted(): lax.ppermute(array, axis, [(i, (i + by) % length) for i in range(length)])  31.7 us
    all_to_all x1, blocking collectives, shards(): part = lax.all_to_all(part, 'zh', 0, 0, tiled=True)  13.4 us
    pallas_call x1, Pallas kernels, shards(): call(image_kernel, [(width, rows)] * 2 + [(3, width, width), (1, LANES)]...  11.5 us
    all_to_all x1, starting transfers between devices, shards(): parts = lax.all_to_all(spread_out(part), RING, 0, 0, tiled=True)  8.3 us
    all_to_all x1, starting transfers between devices, shards(): got = lax.all_to_all(payload, RING, 0, 0, tiled=True)  7.36 us
    pallas_call x1, Pallas kernels, shards(): call(modes_kernel, [(modes, rows)] * 2, [SMEM] + [VMEM] * 9, scratch_shap...  4.98 us
    pallas_call x1, Pallas kernels, shards(): call(mass_kernel, [(3 * width, rows), (3 * width, rows), (3, width, width...  4.76 us
  transfers between devices with their start and end apart: 20, of which 7 were waited for; matrix products, arithmetic and copies ran while one was open for 1% of the time, Pallas kernels for 18%

profile of v3, /device:TPU:1, one launch (start us, length us, event | category | flops | bytes accessed | tf_op | source)
XLA Modules:
  0.0 136.5 jit_solution(2608467384718772499)
XLA Ops:
  0.7 2.4 %fusion = (f32[48,3072]{1,0:T(8,128)}, f32[48,3072]{1,0:T(8,128)}) fusion(f32[96,3072]{1,0:T(8,128)} %bitcast.11), kind=kLoop, calls=%fused_computation.3 | loop fusion | bytes 2359296 | tf_op jit(solution)/shard_map/slice | solution.py:268
  3.1 3.3 %collective-permute-start.3 = (f32[48,3072]{1,0:T(8,128)}, f32[48,3072]{1,0:T(8,128)}, u32[]{:S(2)}, u32[]{:S(2)}) collective-permute-start(f32[48,3072]{1,0:T(8,128)} %get-tuple-element.49), channel_id=1, source_target_pairs={{0,3},{1,0},{2,1},{3,2},{4,7},{5,4},{6,5},{7,6},{8,11},{9,8},{10,9... | collective-permute-start | bytes 1769480 | tf_op jit(solution)/shard_map/ppermute | solution.py:25
  6.4 8.0 %collective-permute-start.9 = (s32[4,48]{1,0:T(4,128)S(1)}, s32[4,48]{1,0:T(4,128)S(1)}, u32[]{:S(2)}, u32[]{:S(2)}) collective-permute-start(s32[4,48]{1,0:T(4,128)S(1)} %bitcast.19), channel_id=1, source_target_pairs={{0,248},{4,252},{8,0},{12,4},{16,8},{20,12},{24,16},{28,20},{32,24... | collective-permute-start | bytes 2312 | tf_op jit(solution)/shard_map/ppermute | solution.py:25
  14.4 2.7 %collective-permute-start.2 = (f32[48,3072]{1,0:T(8,128)}, f32[48,3072]{1,0:T(8,128)S(1)}, u32[]{:S(2)}, u32[]{:S(2)}) collective-permute-start(f32[48,3072]{1,0:T(8,128)} %get-tuple-element.50), channel_id=1, source_target_pairs={{0,3},{1,0},{2,1},{3,2},{4,7},{5,4},{6,5},{7,6},{8,11},{9,8},{10,9... | collective-permute-start | bytes 1769480 | tf_op jit(solution)/shard_map/ppermute | solution.py:25
  17.8 2.4 %collective-permute-done.8.prev2 = s32[4,48]{1,0:T(4,128)S(1)} collective-permute-done((s32[4,48]{1,0:T(4,128)S(1)}, s32[4,48]{1,0:T(4,128)S(1)}, u32[]{:S(2)}, u32[]{:S(2)}) %collective-permute-start.8) | collective-permute-done | bytes 800 | tf_op jit(solution)/shard_map/ppermute | solution.py:25
  20.2 2.4 %collective-permute-start.6 = (f32[96,3072]{1,0:T(8,128)S(1)}, f32[96,3072]{1,0:T(8,128)}, u32[]{:S(2)}, u32[]{:S(2)}) collective-permute-start(f32[96,3072]{1,0:T(8,128)S(1)} %bitcast.16), channel_id=1, source_target_pairs={{0,252},{4,0},{8,4},{12,8},{16,12},{20,16},{24,20},{28,24},{32,28}... | collective-permute-start | bytes 3538952 | tf_op jit(solution)/shard_map/ppermute | solution.py:25
  22.6 3.2 %shard_map.84 = (f32[96,1536]{1,0:T(8,128)}, f32[96,1536]{1,0:T(8,128)}) custom-call(s32[3]{0:T(128)} %add_multiply_fusion.base, s32[4,48]{1,0:T(4,128)} %copy-done.12, s32[4,48]{1,0:T(4,128)} %copy-done.11, f32[96,3072]{1,0:T(8,128)} %bitcast.12), custom_call_target="tpu_custom_call" | custom-call | tf_op jit(solution)/shard_map/pallas_call | solution.py:273
  26.2 3.6 %collective-permute-start.10 = (f32[96,1536]{1,0:T(8,128)}, f32[96,1536]{1,0:T(8,128)}, u32[]{:S(2)}, u32[]{:S(2)}) collective-permute-start(f32[96,1536]{1,0:T(8,128)} %get-tuple-element.29), channel_id=1, source_target_pairs={{0,248},{4,252},{8,0},{12,4},{16,8},{20,12},{24,16},{28,20},{32,24... | collective-permute-start | bytes 1769480 | tf_op jit(solution)/shard_map/ppermute | solution.py:25
  29.8 1.6 %collective-permute-done.2.after_a = f32[48,3072]{1,0:T(8,128)S(1)} collective-permute-done((f32[48,3072]{1,0:T(8,128)}, f32[48,3072]{1,0:T(8,128)S(1)}, u32[]{:S(2)}, u32[]{:S(2)}) %collective-permute-start.2) | collective-permute-done | bytes 589856 | tf_op jit(solution)/shard_map/ppermute | solution.py:25
  31.3 1.3 collective-permute-start.11
  32.6 7.9 %collective-permute-done.before_a = f32[48,3072]{1,0:T(8,128)} collective-permute-done((f32[48,3072]{1,0:T(8,128)}, f32[48,3072]{1,0:T(8,128)}, u32[]{:S(2)}, u32[]{:S(2)}) %collective-permute-start) | collective-permute-done | bytes 589856 | tf_op jit(solution)/shard_map/ppermute | solution.py:25
  40.6 2.7 %collective-permute-start.5 = (f32[48,3072]{1,0:T(8,128)}, f32[48,3072]{1,0:T(8,128)S(1)}, u32[]{:S(2)}, u32[]{:S(2)}) collective-permute-start(f32[48,3072]{1,0:T(8,128)} %collective-permute-done.3.after_b), channel_id=1, source_target_pairs={{0,3},{1,0},{2,1},{3,2},{4,7},{5,4},{6,5},{7,6},{8,11},{9,8},{10,9... | collective-permute-start | bytes 1769480 | tf_op jit(solution)/shard_map/ppermute | solution.py:25
  43.3 4.8 %shard_map.83 = (bf16[288,3072]{1,0:T(8,128)(2,1)}, bf16[288,3072]{1,0:T(8,128)(2,1)}, f32[3,96,96]{2,1,0:T(8,128)}, f32[1,128]{1,0:T(1,128)}) custom-call(s32[1]{0:T(128)} %bitcast.col, f32[96,3072]{1,0:T(8,128)} %bitcast.13, f32[48,3072]{1,0:T(8,128)} %collective-permute-done.before_a, f32[48,3072]{1,0:T(8,128)} %copy-done.5, f32[48,3072]{1,0:T(8,128)} %copy-done.6, ...), custom_call_target="tpu_custom_call" | custom-call | tf_op jit(solution)/shard_map/pallas_call | solution.py:280
  48.1 3.8 %collective-permute-done.11.down2 = f32[96,1536]{1,0:T(8,128)} collective-permute-done((f32[96,1536]{1,0:T(8,128)}, f32[96,1536]{1,0:T(8,128)}, u32[]{:S(2)}, u32[]{:S(2)}) %collective-permute-start.11) | collective-permute-done | bytes 589856 | tf_op jit(solution)/shard_map/ppermute | solution.py:25
  51.9 1.0 copy-done.4
  52.9 11.5 %shard_map.85 = (bf16[96,3072]{1,0:T(8,128)(2,1)}, bf16[96,3072]{1,0:T(8,128)(2,1)}, f32[3,96,96]{2,1,0:T(8,128)}, f32[1,128]{1,0:T(1,128)}, f32[32,3072]{1,0:T(...) custom-call(s32[1]{0:T(128)} %bitcast.col, s32[3]{0:T(128)} %add_multiply_fusion.base, ...), custom_call_target="tpu_custom_call" | custom-call | tf_op jit(solution)/shard_map/pallas_call | solution.py:290
  64.5 0.8 copy-done.1
  65.5 4.0 %shard_map.87 = (f32[16,40,128]{2,1,0:T(8,128)}, f32[8,128]{1,0:T(8,128)}) custom-call(s32[1]{0:T(128)} %bitcast.col, f32[3,96,96]{2,1,0:T(8,128)} %get-tuple-element.36.stiff3, f32[1,128]{1,0:T(1,128)} %get-tuple-element.37.stiff_terms, f32[3,96,96]{2,1,0:T(8,128)} %get-tuple-element.38.mass3, f32[1,128]{1,0:T(1,128)} %get-tuple-element.39.mass_terms, ...), custom_call_target="tpu_custom_call" | custom-call | tf_op jit(solution)/shard_map/pallas_call | solution.py:310
  69.5 7.4 %all-to-all-start = ((f32[16,40,128]{2,1,0:T(8,128)}), f32[16,40,128]{2,1,0:T(8,128)S(1)}, u32[]{:S(2)}, u32[]{:S(2)}) async-start(f32[16,40,128]{2,1,0:T(8,128)} %get-tuple-element.42), calls=%async_computation | async-start | bytes 655360 | tf_op jit(solution)/shard_map/all_to_all | solution.py:318
  76.9 3.0 %collective-permute-start.17 = (f32[8,128]{1,0:T(8,128)}, f32[8,128]{1,0:T(8,128)S(1)}, u32[]{:S(2)}, u32[]{:S(2)}) collective-permute-start(f32[8,128]{1,0:T(8,128)} %get-tuple-element.43), channel_id=1, source_target_pairs={{0,3},{1,0},{2,1},{3,2},{4,7},{5,4},{6,5},{7,6},{8,11},{9,8},{10,9... | collective-permute-start | bytes 12296 | tf_op jit(solution)/shard_map/ppermute | solution.py:25
  80.9 3.2 %collective-permute-done.16 = f32[8,128]{1,0:T(8,128)S(1)} collective-permute-done((f32[8,128]{1,0:T(8,128)}, f32[8,128]{1,0:T(8,128)S(1)}, u32[]{:S(2)}, u32[]{:S(2)}) %collective-permute-start.16) | collective-permute-done | bytes 4128 | tf_op jit(solution)/shard_map/ppermute | solution.py:25
  84.1 0.7 add_add_fusion
  84.8 13.4 %all_to_all.15 = f32[4,48,128]{2,1,0:T(8,128)S(1)} all-to-all(f32[4,48,128]{2,1,0:T(8,128)S(1)} %broadcast_in_dim.4), channel_id=1, replica_groups=mesh['zh'=4,'zl'=2,'y'=4,'core'=2,'col'=4] {'zh'}, dimensions={0} | all-to-all | bytes 196608 | tf_op jit(solution)/shard_map/all_to_all | solution.py:334
  98.2 0.8 broadcast_in_dim.5
  99.0 8.3 %all-to-all-start.2 = ((f32[16,48,128]{2,1,0:T(8,128)}), f32[16,48,128]{2,1,0:T(8,128)S(1)}, u32[]{:S(2)}, u32[]{:S(2)}) async-start(f32[16,48,128]{2,1,0:T(8,128)} %broadcast_in_dim.5), calls=%async_computation.2 | async-start | bytes 786432 | tf_op jit(solution)/shard_map/all_to_all | solution.py:336
  107.4 2.7 %collective-permute-start.13 = (f32[32,3072]{1,0:T(8,128)S(1)}, f32[32,3072]{1,0:T(8,128)S(1)}, u32[]{:S(2)}, u32[]{:S(2)}) collective-permute-start(f32[32,3072]{1,0:T(8,128)S(1)} %copy-done.14), channel_id=1, source_target_pairs={{0,3},{1,0},{2,1},{3,2},{4,7},{5,4},{6,5},{7,6},{8,11},{9,8},{10,9... | collective-permute-start | bytes 1179656 | tf_op jit(solution)/shard_map/ppermute | solution.py:25
  110.0 0.8 collective-permute-start.14
  110.8 16.7 %collective-permute-done.12.from_prev = f32[32,3072]{1,0:T(8,128)S(1)} collective-permute-done((f32[32,3072]{1,0:T(8,128)S(1)}, f32[32,3072]{1,0:T(8,128)S(1)}, u32[]{:S(2)}, u32[]{:S(2)}) %collective-permute-start.12) | collective-permute-done | bytes 393248 | tf_op jit(solution)/shard_map/ppermute | solution.py:25
  127.6 0.7 copy-done.7
  128.6 5.0 %shard_map.86 = (f32[32,3072]{1,0:T(8,128)}, f32[32,3072]{1,0:T(8,128)}) custom-call(s32[1]{0:T(128)} %bitcast.col, bf16[288,3072]{1,0:T(8,128)(2,1)} %get-tuple-element.27.high.st_high, bf16[288,3072]{1,0:T(8,128)(2,1)} %get-tuple-element.28.low.st_low, f32[48,3072]{1,0:T(8,128)} %copy-done.2, f32[48,3072]{1,0:T(8,128)} %copy-done.1, f32[384,128]{1,0:T(8,128)} %ritz.7, ...), custom_call_target="tpu_custom_call" | custom-call | tf_op jit(solution)/shard_map/pallas_call | solution.py:323
  133.6 0.8 copy-done.3
  134.4 2.1 %shard_map.88 = (f32[96,384]{1,0:T(8,128)}, f32[96,384]{1,0:T(8,128)}, f32[1,32]{1,0:T(1,128)}, f32[32,3072]{1,0:T(8,128)}) custom-call(s32[1]{0:T(128)} %bitcast.col, f32[16,48,128]{2,1,0:T(8,128)} %copy-done.3, f32[32,3072]{1,0:T(8,128)} %get-tuple-element.35.modes, f32[32,3072]{1,0:T(8,128)} %get-tuple-element.44.image), custom_call_target="tpu_custom_call" | custom-call | tf_op jit(solution)/shard_map/pallas_call | solution.py:338
  (55 shorter events, 2.8 us)
Async XLA Ops:
  0.6 5.8 %copy-start.10 = (s32[48,4]{0,1:T(4,128)S(1)}, s32[48,4]{0,1:T(4,128)}, u32[]{:S(2)}) copy-start(s32[48,4]{0,1:T(4,128)} %param.6) | copy-start | bytes 2308
  0.6 17.1 %copy-start = (f32[3072,96]{0,1:T(8,128)S(1)}, f32[3072,96]{0,1:T(8,128)}, u32[]{:S(2)}) copy-start(f32[3072,96]{0,1:T(8,128)} %param.4) | copy-start | bytes 3538948
  3.1 22.6 %collective-permute-start.3 = (f32[48,3072]{1,0:T(8,128)}, f32[48,3072]{1,0:T(8,128)}, u32[]{:S(2)}, u32[]{:S(2)}) collective-permute-start(f32[48,3072]{1,0:T(8,128)} %get-tuple-element.49), channel_id=1, source_target_pairs={{0,3},{1,0},{2,1},{3,2},{4,7},{5,4},{6,5},{7,6},{8,11},{9,8},{10,9... | collective-permute-start | bytes 1769480 | tf_op jit(solution)/shard_map/ppermute | solution.py:25
  6.4 19.8 %collective-permute-start.1 = (f32[48,3072]{1,0:T(8,128)}, f32[48,3072]{1,0:T(8,128)S(1)}, u32[]{:S(2)}, u32[]{:S(2)}) collective-permute-start(f32[48,3072]{1,0:T(8,128)} %get-tuple-element.49), channel_id=1, source_target_pairs={{0,1},{1,2},{2,3},{3,0},{4,5},{5,6},{6,7},{7,4},{8,9},{9,10},{10,1... | collective-permute-start | bytes 1769480 | tf_op jit(solution)/shard_map/ppermute | solution.py:25
  6.4 11.3 %collective-permute-start.9 = (s32[4,48]{1,0:T(4,128)S(1)}, s32[4,48]{1,0:T(4,128)S(1)}, u32[]{:S(2)}, u32[]{:S(2)}) collective-permute-start(s32[4,48]{1,0:T(4,128)S(1)} %bitcast.19), channel_id=1, source_target_pairs={{0,248},{4,252},{8,0},{12,4},{16,8},{20,12},{24,16},{28,20},{32,24... | collective-permute-start | bytes 2312 | tf_op jit(solution)/shard_map/ppermute | solution.py:25
  14.4 5.8 %collective-permute-start.8 = (s32[4,48]{1,0:T(4,128)S(1)}, s32[4,48]{1,0:T(4,128)S(1)}, u32[]{:S(2)}, u32[]{:S(2)}) collective-permute-start(s32[4,48]{1,0:T(4,128)S(1)} %bitcast.20), channel_id=1, source_target_pairs={{0,8},{4,12},{8,16},{12,20},{16,24},{20,28},{24,32},{28,36},{32,40... | collective-permute-start | bytes 2312 | tf_op jit(solution)/shard_map/ppermute | solution.py:25
  14.4 16.9 %collective-permute-start.2 = (f32[48,3072]{1,0:T(8,128)}, f32[48,3072]{1,0:T(8,128)S(1)}, u32[]{:S(2)}, u32[]{:S(2)}) collective-permute-start(f32[48,3072]{1,0:T(8,128)} %get-tuple-element.50), channel_id=1, source_target_pairs={{0,3},{1,0},{2,1},{3,2},{4,7},{5,4},{6,5},{7,6},{8,11},{9,8},{10,9... | collective-permute-start | bytes 1769480 | tf_op jit(solution)/shard_map/ppermute | solution.py:25
  17.7 4.9 %copy-start.11 = (s32[4,48]{1,0:T(4,128)}, s32[4,48]{1,0:T(4,128)S(1)}, u32[]{:S(2)}) copy-start(s32[4,48]{1,0:T(4,128)S(1)} %collective-permute-done.9.next2) | copy-start | bytes 2308
  17.7 34.2 %collective-permute-start.7 = (f32[96,3072]{1,0:T(8,128)S(1)}, f32[96,3072]{1,0:T(8,128)S(1)}, u32[]{:S(2)}, u32[]{:S(2)}) collective-permute-start(f32[96,3072]{1,0:T(8,128)S(1)} %bitcast.15), channel_id=1, source_target_pairs={{0,4},{4,8},{8,12},{12,16},{16,20},{20,24},{24,28},{28,32},{32,36}... | collective-permute-start | bytes 3538952 | tf_op jit(solution)/shard_map/ppermute | solution.py:25
  20.2 2.4 %copy-start.12 = (s32[4,48]{1,0:T(4,128)}, s32[4,48]{1,0:T(4,128)S(1)}, u32[]{:S(2)}) copy-start(s32[4,48]{1,0:T(4,128)S(1)} %collective-permute-done.8.prev2) | copy-start | bytes 2308
  20.2 31.7 %collective-permute-start.6 = (f32[96,3072]{1,0:T(8,128)S(1)}, f32[96,3072]{1,0:T(8,128)}, u32[]{:S(2)}, u32[]{:S(2)}) collective-permute-start(f32[96,3072]{1,0:T(8,128)S(1)} %bitcast.16), channel_id=1, source_target_pairs={{0,252},{4,0},{8,4},{12,8},{16,12},{20,16},{24,20},{28,24},{32,28}... | collective-permute-start | bytes 3538952 | tf_op jit(solution)/shard_map/ppermute | solution.py:25
  25.7 14.9 %collective-permute-start = (f32[48,3072]{1,0:T(8,128)}, f32[48,3072]{1,0:T(8,128)}, u32[]{:S(2)}, u32[]{:S(2)}) collective-permute-start(f32[48,3072]{1,0:T(8,128)} %get-tuple-element.50), channel_id=1, source_target_pairs={{0,1},{1,2},{2,3},{3,0},{4,5},{5,6},{6,7},{7,4},{8,9},{9,10},{10,1... | collective-permute-start | bytes 1769480 | tf_op jit(solution)/shard_map/ppermute | solution.py:25
  26.2 6.4 %copy-start.5 = (f32[48,3072]{1,0:T(8,128)}, f32[48,3072]{1,0:T(8,128)S(1)}, u32[]{:S(2)}) copy-start(f32[48,3072]{1,0:T(8,128)S(1)} %collective-permute-done.1.before_b) | copy-start | bytes 1769476
  26.2 17.1 %collective-permute-start.10 = (f32[96,1536]{1,0:T(8,128)}, f32[96,1536]{1,0:T(8,128)}, u32[]{:S(2)}, u32[]{:S(2)}) collective-permute-start(f32[96,1536]{1,0:T(8,128)} %get-tuple-element.29), channel_id=1, source_target_pairs={{0,248},{4,252},{8,0},{12,4},{16,8},{20,12},{24,16},{28,20},{32,24... | collective-permute-start | bytes 1769480 | tf_op jit(solution)/shard_map/ppermute | solution.py:25
  31.3 12.0 %copy-start.6 = (f32[48,3072]{1,0:T(8,128)}, f32[48,3072]{1,0:T(8,128)S(1)}, u32[]{:S(2)}) copy-start(f32[48,3072]{1,0:T(8,128)S(1)} %collective-permute-done.2.after_a) | copy-start | bytes 1769476
  31.3 20.5 %collective-permute-start.11 = (f32[96,1536]{1,0:T(8,128)}, f32[96,1536]{1,0:T(8,128)}, u32[]{:S(2)}, u32[]{:S(2)}) collective-permute-start(f32[96,1536]{1,0:T(8,128)} %get-tuple-element.30), channel_id=1, source_target_pairs={{0,8},{4,12},{8,16},{12,20},{16,24},{20,28},{24,32},{28,36},{32,40... | collective-permute-start | bytes 1769480 | tf_op jit(solution)/shard_map/ppermute | solution.py:25
  40.6 23.9 %collective-permute-start.5 = (f32[48,3072]{1,0:T(8,128)}, f32[48,3072]{1,0:T(8,128)S(1)}, u32[]{:S(2)}, u32[]{:S(2)}) collective-permute-start(f32[48,3072]{1,0:T(8,128)} %collective-permute-done.3.after_b), channel_id=1, source_target_pairs={{0,3},{1,0},{2,1},{3,2},{4,7},{5,4},{6,5},{7,6},{8,11},{9,8},{10,9... | collective-permute-start | bytes 1769480 | tf_op jit(solution)/shard_map/ppermute | solution.py:25
  43.3 21.2 %collective-permute-start.4 = (f32[48,3072]{1,0:T(8,128)}, f32[48,3072]{1,0:T(8,128)S(1)}, u32[]{:S(2)}, u32[]{:S(2)}) collective-permute-start(f32[48,3072]{1,0:T(8,128)} %collective-permute-done.before_a), channel_id=1, source_target_pairs={{0,1},{1,2},{2,3},{3,0},{4,5},{5,6},{6,7},{7,4},{8,9},{9,10},{10,1... | collective-permute-start | bytes 1769480 | tf_op jit(solution)/shard_map/ppermute | solution.py:25
  51.9 1.1 copy-start.4
  64.5 1.0 copy-start.2
  69.5 15.3 %all-to-all-start = ((f32[16,40,128]{2,1,0:T(8,128)}), f32[16,40,128]{2,1,0:T(8,128)S(1)}, u32[]{:S(2)}, u32[]{:S(2)}) async-start(f32[16,40,128]{2,1,0:T(8,128)} %get-tuple-element.42), calls=%async_computation | async-start | bytes 655360 | tf_op jit(solution)/shard_map/all_to_all | solution.py:318
  76.8 30.4 %copy-start.15 = (f32[32,3072]{1,0:T(8,128)S(1)}, f32[32,3072]{1,0:T(8,128)}, u32[]{:S(2)}) copy-start(f32[32,3072]{1,0:T(8,128)} %get-tuple-element.32) | copy-start | bytes 1179652
  76.8 30.5 %copy-start.14 = (f32[32,3072]{1,0:T(8,128)S(1)}, f32[32,3072]{1,0:T(8,128)}, u32[]{:S(2)}) copy-start(f32[32,3072]{1,0:T(8,128)} %get-tuple-element.33) | copy-start | bytes 1179652
  76.9 33.2 %copy-start.13 = (f32[32,3072]{1,0:T(8,128)S(1)}, f32[32,3072]{1,0:T(8,128)}, u32[]{:S(2)}) copy-start(f32[32,3072]{1,0:T(8,128)} %get-tuple-element.34) | copy-start | bytes 1179652
  76.9 4.0 %collective-permute-start.17 = (f32[8,128]{1,0:T(8,128)}, f32[8,128]{1,0:T(8,128)S(1)}, u32[]{:S(2)}, u32[]{:S(2)}) collective-permute-start(f32[8,128]{1,0:T(8,128)} %get-tuple-element.43), channel_id=1, source_target_pairs={{0,3},{1,0},{2,1},{3,2},{4,7},{5,4},{6,5},{7,6},{8,11},{9,8},{10,9... | collective-permute-start | bytes 12296 | tf_op jit(solution)/shard_map/ppermute | solution.py:25
  79.9 4.2 %collective-permute-start.16 = (f32[8,128]{1,0:T(8,128)}, f32[8,128]{1,0:T(8,128)S(1)}, u32[]{:S(2)}, u32[]{:S(2)}) collective-permute-start(f32[8,128]{1,0:T(8,128)} %get-tuple-element.43), channel_id=1, source_target_pairs={{0,2},{1,3},{2,0},{3,1},{4,6},{5,7},{6,4},{7,5},{8,10},{9,11},{10,... | collective-permute-start | bytes 12296 | tf_op jit(solution)/shard_map/ppermute | solution.py:25
  79.9 4.2 %collective-permute-start.15 = (f32[8,128]{1,0:T(8,128)}, f32[8,128]{1,0:T(8,128)S(1)}, u32[]{:S(2)}, u32[]{:S(2)}) collective-permute-start(f32[8,128]{1,0:T(8,128)} %get-tuple-element.43), channel_id=1, source_target_pairs={{0,1},{1,2},{2,3},{3,0},{4,5},{5,6},{6,7},{7,4},{8,9},{9,10},{10,1... | collective-permute-start | bytes 12296 | tf_op jit(solution)/shard_map/ppermute | solution.py:25
  99.0 34.6 %all-to-all-start.2 = ((f32[16,48,128]{2,1,0:T(8,128)}), f32[16,48,128]{2,1,0:T(8,128)S(1)}, u32[]{:S(2)}, u32[]{:S(2)}) async-start(f32[16,48,128]{2,1,0:T(8,128)} %broadcast_in_dim.5), calls=%async_computation.2 | async-start | bytes 786432 | tf_op jit(solution)/shard_map/all_to_all | solution.py:336
  107.3 20.3 %collective-permute-start.12 = (f32[32,3072]{1,0:T(8,128)S(1)}, f32[32,3072]{1,0:T(8,128)S(1)}, u32[]{:S(2)}, u32[]{:S(2)}) collective-permute-start(f32[32,3072]{1,0:T(8,128)S(1)} %copy-done.15), channel_id=1, source_target_pairs={{0,1},{1,2},{2,3},{3,0},{4,5},{5,6},{6,7},{7,4},{8,9},{9,10},{10,1... | collective-permute-start | bytes 1179656 | tf_op jit(solution)/shard_map/ppermute | solution.py:25
  107.4 20.2 %collective-permute-start.13 = (f32[32,3072]{1,0:T(8,128)S(1)}, f32[32,3072]{1,0:T(8,128)S(1)}, u32[]{:S(2)}, u32[]{:S(2)}) collective-permute-start(f32[32,3072]{1,0:T(8,128)S(1)} %copy-done.14), channel_id=1, source_target_pairs={{0,3},{1,0},{2,1},{3,2},{4,7},{5,4},{6,5},{7,6},{8,11},{9,8},{10,9... | collective-permute-start | bytes 1179656 | tf_op jit(solution)/shard_map/ppermute | solution.py:25
  110.0 17.5 %collective-permute-start.14 = (f32[32,3072]{1,0:T(8,128)S(1)}, f32[32,3072]{1,0:T(8,128)S(1)}, u32[]{:S(2)}, u32[]{:S(2)}) collective-permute-start(f32[32,3072]{1,0:T(8,128)S(1)} %copy-done.13), channel_id=1, source_target_pairs={{0,2},{1,3},{2,0},{3,1},{4,6},{5,7},{6,4},{7,5},{8,10},{9,11},{10,... | collective-permute-start | bytes 1179656 | tf_op jit(solution)/shard_map/ppermute | solution.py:25
  127.6 1.0 copy-start.9
  (4 other events, 3.2 us)

commit v4 on v3

--- a/solution.py
+++ b/solution.py
@@ -78,19 +78,21 @@
 
 
 def image_kernel(
-    col, base, cols, st, up1, down1, up2, down2, values, high, low, ritz,
-    image_high, image_low, gram, terms, part_own, part_after, part_opp, part_before, sums, turned
+    col, base, cols, st, up1, down1, up2, down2, values, before, after, ritz,
+    image_high, image_low, stiff, stiff_terms, mass, mass_terms,
+    part_own, part_after, part_opp, part_before, stiff_sum, mass_sum, turned
 ):
     m = pl.program_id(0)
     width = st.shape[0]
     pairs = values.shape[0] // LANES
     left_half = low_half((width, LANES))
     flip = lambda x: pltpu.roll(x, BLOCK, 1)
-    images = []
+    images, owns = [], []
 
     @pl.when(m == 0)
     def _():
-        sums[...] = jnp.zeros_like(sums)
+        stiff_sum[...] = jnp.zeros_like(stiff_sum)
+        mass_sum[...] = jnp.zeros_like(mass_sum)
         turned[...] = ritz[pl.ds(pl.multiple_of(col[0] * width, 8), width), :].T
 
     modes = part_own.shape[0]
@@ -102,6 +104,7 @@
     for h in range(pairs):
         tile = m * pairs + h
         own = st[:, pl.ds(pl.multiple_of(tile * LANES, LANES), LANES)]
+        owns.append(own)
         left, right = [], []
         for q, (far1, far2, at) in enumerate(((up1, up2, 1), (down1, down2, 2))):
             row = 2 * tile + q
@@ -123,16 +126,20 @@
             span = slice((h - 1) * LANES, (h + 1) * LANES)
             image = tuple(jnp.concatenate([images[h - 1][i], images[h][i]], axis=1) for i in range(2))
             image_high[:, span], image_low[:, span] = image
-            sums[...] += dot4((high[:, span], low[:, span]), image)
+            mine = jnp.concatenate(owns[h - 1 :], axis=1)
+            pieces = split(jnp.concatenate([mine, before[:, span], after[:, span]], axis=0))
+            mass_sum[...] += dot4(pieces, (pieces[0][:width], pieces[1][:width]))
+            stiff_sum[...] += dot4(pieces, image)
             part = dot3(send, image, NN)
             for i, out in enumerate((part_own, part_after, part_opp, part_before)):
                 out[:, span] = part[i * modes : (i + 1) * modes]
 
     @pl.when(m == pl.num_programs(0) - 1)
     def _():
-        for i in range(3):
-            gram[i] = sums[i * width : (i + 1) * width, :width]
-        piece_terms(gram, col[0], ritz, terms)
+        for gram, terms, total in ((stiff, stiff_terms, stiff_sum), (mass, mass_terms, mass_sum)):
+            for i in range(3):
+                gram[i] = total[i * width : (i + 1) * width, :width]
+            piece_terms(gram, col[0], ritz, terms)
 
 
 def quotient_terms(piece, mine, ritz, start):
@@ -149,28 +156,15 @@
     terms[...] = total + quotient_terms(gram[2], mine, ritz, at(1))
 
 
-def mass_kernel(col, st, before_a, before_b, after_a, after_b, ritz, high, low, gram, terms):
-    width = st.shape[0]
-    at = 0
-    for piece in (st, before_a, before_b, after_a, after_b):
-        to = at + piece.shape[0]
-        high[at:to, :], low[at:to, :] = split(piece[...])
-        at = to
-    block = dot4((high[...], low[...]), (high[:width, :], low[:width, :]))
-    for i in range(3):
-        gram[i] = block[i * width : (i + 1) * width, :width]
-    piece_terms(gram, col[0], ritz, terms)
-
-
 def late_kernel(
-    col, stiff3, stiff_terms, mass3, mass_terms, opp_a, opp_b, image_high, image_low, st_high, st_low,
-    ritz, payload, terms, stiff, mass
+    col, stiff3, stiff_terms, mass3, mass_terms, opp_a, opp_b, image_high, image_low, st, ritz,
+    payload, terms, stiff, mass
 ):
     c = col[0]
-    width = st_high.shape[0]
+    width = st.shape[0]
     far = split(jnp.concatenate([opp_a[...], opp_b[...]], axis=0))
     far_stiff = dot4(far, (image_high[...], image_low[...]))[:, :width]
-    far_mass = dot4(far, (st_high[...], st_low[...]))[:, :width]
+    far_mass = dot4(far, split(st[...]))[:, :width]
     terms[...] = jnp.zeros_like(terms)
     at = lambda by: pl.multiple_of((c + by) % 4 * width, 8)
     mine = ritz[pl.ds(at(0), width), :]
@@ -195,18 +189,20 @@
 
 
 def modes_kernel(
-    col, high, low, opp_a, opp_b, ritz, own, from_prev, from_next, from_opp, modes, image, turned
+    col, st, before, after, opp_a, opp_b, ritz, own, from_prev, from_next, from_opp, modes, image, turned
 ):
-    rest = high.shape[0]
-    width = rest // 3
+    width = st.shape[0]
     coef = []
     for by in (0, 3, 1, 2):
         turned[...] = ritz[pl.ds(pl.multiple_of((col[0] + by) % 4 * width, 8), width), :].T
         coef.append(turned[pl.ds(pl.multiple_of(col[0] * modes.shape[0], 8), modes.shape[0]), :])
     opp = jnp.concatenate([opp_a[...], opp_b[...]], axis=0)
-    modes[...] = dot3(
-        split(jnp.concatenate(coef[:3], axis=1)), (high[...], low[...]), NN
-    ) + dot3(split(coef[3]), split(opp), NN)
+    modes[...] = (
+        dot3(split(coef[0]), split(st[...]), NN)
+        + dot3(split(coef[1]), split(before[...]), NN)
+        + dot3(split(coef[2]), split(after[...]), NN)
+        + dot3(split(coef[3]), split(opp), NN)
+    )
     image[...] = (own[...] + from_opp[...]) + (from_prev[...] + from_next[...])
 
 
@@ -261,12 +257,10 @@
     st = search.T
     cols = block_cols.T
 
+    before = shifted(st, "col", 1)
+    after = shifted(st, "col", -1)
     prev2 = shifted(cols, WIRE, 2)
     next2 = shifted(cols, WIRE, -2)
-    before_a = shifted(st[:half], "col", 1)
-    after_b = shifted(st[half:], "col", -1)
-    before_b = shifted(st[half:], "col", 1)
-    after_a = shifted(st[:half], "col", -1)
     up1 = shifted(st, WIRE, -1)
     down1 = shifted(st, WIRE, 1)
 
@@ -274,46 +268,38 @@
     up2 = shifted(packed[0], WIRE, -2)
     down2 = shifted(packed[1], WIRE, 2)
 
-    opp_a = shifted(before_a, "col", 1)
-    opp_b = shifted(after_b, "col", -1)
-
-    high, low, mass3, mass_terms = call(
-        mass_kernel,
-        [(3 * width, rows), (3 * width, rows), (3, width, width), (1, LANES)],
-        [SMEM] + [VMEM] * 6,
-        [jnp.bfloat16, jnp.bfloat16, F32, F32],
-    )(col, st, before_a, before_b, after_a, after_b, ritz)
+    opp_a = shifted(before[:half], "col", 1)
+    opp_b = shifted(after[half:], "col", -1)
 
     tile = lambda n: pl.BlockSpec((width, n), lambda m: (0, m))
     whole = pl.BlockSpec((width, rows), lambda m: (0, 0))
     step_lanes = PAIRS * LANES
-    *image, stiff3, stiff_terms, part_own, part_after, part_opp, part_before = call(
+    grams = [(3, width, width), (1, LANES)] * 2
+    gram_specs = [pl.BlockSpec((3, width, width), lambda m: (0, 0, 0)), pl.BlockSpec((1, LANES), lambda m: (0, 0))] * 2
+    made = call(
         image_kernel,
-        [(width, rows)] * 2 + [(3, width, width), (1, LANES)] + [(modes, rows)] * 4,
+        [(width, rows)] * 2 + grams + [(modes, rows)] * 4,
         [SMEM] * 3
         + [whole] * 3
         + [tile(step_lanes // 2)] * 2
         + [pl.BlockSpec((step_lanes, values.shape[1]), lambda m: (m, 0))]
-        + [pl.BlockSpec((3 * width, step_lanes), lambda m: (0, m))] * 2
+        + [tile(step_lanes)] * 2
         + [VMEM],
-        [jnp.bfloat16] * 2 + [F32] * 6,
+        [jnp.bfloat16] * 2 + [F32] * 8,
         out_specs=[tile(step_lanes)] * 2
-        + [
-            pl.BlockSpec((3, width, width), lambda m: (0, 0, 0)),
-            pl.BlockSpec((1, LANES), lambda m: (0, 0)),
-        ]
+        + gram_specs
         + [pl.BlockSpec((modes, step_lanes), lambda m: (0, m))] * 4,
         grid=(rows // step_lanes,),
-        scratch_shapes=[pltpu.VMEM((3 * width, LANES), F32), pltpu.VMEM((4 * modes, width), F32)],
-    )(col, base, cols, st, up1, down1, up2, down2, values, high, low, ritz)
+        scratch_shapes=[pltpu.VMEM((3 * width, LANES), F32)] * 2 + [pltpu.VMEM((4 * modes, width), F32)],
+    )(col, base, cols, st, up1, down1, up2, down2, values, before, after, ritz)
+    image, grams, (part_own, part_after, part_opp, part_before) = made[:2], made[2:6], made[6:]
 
     payload, terms = call(
         late_kernel,
         [(PARTS, 8 * TILES, LANES), (8, LANES)],
-        [SMEM] + [VMEM] * 8 + [whole] * 2 + [VMEM],
-        grid=(1,),
+        [SMEM] + [VMEM] * 10,
         scratch_shapes=[pltpu.VMEM((4 * width, width), F32)] * 2,
-    )(col, stiff3, stiff_terms, mass3, mass_terms, opp_a, opp_b, *image, high, low, ritz)
+    )(col, *grams, opp_a, opp_b, *image, st, ritz)
 
     got = lax.all_to_all(payload, RING, 0, 0, tiled=True)
     around = [shifted(terms, "col", by) for by in (1, 2, 3)]
@@ -323,9 +309,9 @@
     new_modes, new_image = call(
         modes_kernel,
         [(modes, rows)] * 2,
-        [SMEM] + [VMEM] * 9,
+        [SMEM] + [VMEM] * 10,
         scratch_shapes=[pltpu.VMEM((4 * modes, width), F32)],
-    )(col, high, low, opp_a, opp_b, ritz, part_own, from_prev, from_next, from_opp)
+    )(col, st, before, after, opp_a, opp_b, ritz, part_own, from_prev, from_next, from_opp)
 
     part = jnp.concatenate(
         [jnp.sum(got, axis=0), terms + around[0] + around[1] + around[2]], axis=0

time: 137 us -> 131 us (0.956)
  Pallas kernels: 30.6 us -> 26.3 us
  waiting for transfers between devices: 36 us -> 40.3 us
  starting transfers between devices: 47.4 us -> 44.2 us
  local copies, waits for them, and re-layouts: 7.08 us -> 5.65 us
  blocking collectives: 13.4 us -> 12 us
    pallas_call x3 -> x2, Pallas kernels: 21.3 us -> 17 us  [the longest x1 12.2 us: shards(): call(image_kernel, [(width, rows)] * 2 + grams + [(modes, rows)] * 4, [SM...]
    ppermute x18 -> x16, waiting for transfers between devices: 36 us -> 38.7 us  [shifted(): lax.ppermute(array, axis, [(i, (i + by) % length) for i in range(length)])]
    all_to_all x1, starting transfers between devices: 7.36 us -> 5.43 us  [shards(): got = lax.all_to_all(payload, RING, 0, 0, tiled=True)]
    all_to_all x1, waiting for transfers between devices: 0.01 us -> 1.54 us  [shards(): got = lax.all_to_all(payload, RING, 0, 0, tiled=True)]
    unnamed x32 -> x28, local copies, waits for them, and re-layouts: 3.86 us -> 3.1 us
    ppermute x18 -> x16, starting transfers between devices: 31.7 us -> 31.8 us  [shifted(): lax.ppermute(array, axis, [(i, (i + by) % length) for i in range(length)])]
  transfers between devices with their start and end apart: 20 -> 18, of which waited for: 7 -> 9; matrix products, arithmetic and copies ran while one was open for 1% -> 2% of each run, Pallas kernels for 18% -> 15%
where the time goes in v4:
time: 131 us; the launch traced here: 130 us
  starting transfers between devices  44.2 us (34%)
  waiting for transfers between devices  40.3 us (31%)
  Pallas kernels  26.3 us (20%)
  blocking collectives  12 us (9%)
  local copies, waits for them, and re-layouts  5.65 us (4%)
    ppermute x16, waiting for transfers between devices, shifted(): lax.ppermute(array, axis, [(i, (i + by) % length) for i in range(length)])  38.7 us
    ppermute x16, starting transfers between devices, shifted(): lax.ppermute(array, axis, [(i, (i + by) % length) for i in range(length)])  31.8 us
    pallas_call x1, Pallas kernels, shards(): call(image_kernel, [(width, rows)] * 2 + grams + [(modes, rows)] * 4, [SM...  12.2 us
    all_to_all x1, blocking collectives, shards(): part = lax.all_to_all(part, 'zh', 0, 0, tiled=True)  12 us
    all_to_all x1, starting transfers between devices, shards(): parts = lax.all_to_all(spread_out(part), RING, 0, 0, tiled=True)  7 us
    all_to_all x1, starting transfers between devices, shards(): got = lax.all_to_all(payload, RING, 0, 0, tiled=True)  5.43 us
    pallas_call x1, Pallas kernels, shards(): call(modes_kernel, [(modes, rows)] * 2, [SMEM] + [VMEM] * 10, scratch_sha...  4.75 us
    pallas_call x1, Pallas kernels, shards(): call(late_kernel, [(PARTS, 8 * TILES, LANES), (8, LANES)], [SMEM] + [VMEM...  4.08 us
  transfers between devices with their start and end apart: 18, of which 9 were waited for; matrix products, arithmetic and copies ran while one was open for 2% of the time, Pallas kernels for 15%

profile of v4, /device:TPU:1, one launch (start us, length us, event | category | flops | bytes accessed | tf_op | source)
XLA Modules:
  0.0 130.5 jit_solution(5196714517362482755)
XLA Ops:
  0.6 2.1 %collective-permute-start = (f32[96,3072]{1,0:T(8,128)}, f32[96,3072]{1,0:T(8,128)S(1)}, u32[]{:S(2)}, u32[]{:S(2)}) collective-permute-start(f32[96,3072]{1,0:T(8,128)} %bitcast.11), channel_id=1, source_target_pairs={{0,1},{1,2},{2,3},{3,0},{4,5},{5,6},{6,7},{7,4},{8,9},{9,10},{10,1... | collective-permute-start | bytes 3538952 | tf_op jit(solution)/shard_map/ppermute | solution.py:25
  2.7 1.4 %collective-permute-start.1 = (f32[96,3072]{1,0:T(8,128)}, f32[96,3072]{1,0:T(8,128)S(1)}, u32[]{:S(2)}, u32[]{:S(2)}) collective-permute-start(f32[96,3072]{1,0:T(8,128)} %bitcast.12), channel_id=1, source_target_pairs={{0,3},{1,0},{2,1},{3,2},{4,7},{5,4},{6,5},{7,6},{8,11},{9,8},{10,9... | collective-permute-start | bytes 3538952 | tf_op jit(solution)/shard_map/ppermute | solution.py:25
  4.1 1.4 %collective-permute-start.6 = (s32[4,48]{1,0:T(4,128)}, s32[4,48]{1,0:T(4,128)S(1)}, u32[]{:S(2)}, u32[]{:S(2)}) collective-permute-start(s32[4,48]{1,0:T(4,128)} %bitcast.20), channel_id=1, source_target_pairs={{0,8},{4,12},{8,16},{12,20},{16,24},{20,28},{24,32},{28,36},{32,40... | collective-permute-start | bytes 2312 | tf_op jit(solution)/shard_map/ppermute | solution.py:25
  5.5 6.7 %collective-permute-start.7 = (s32[4,48]{1,0:T(4,128)}, s32[4,48]{1,0:T(4,128)S(1)}, u32[]{:S(2)}, u32[]{:S(2)}) collective-permute-start(s32[4,48]{1,0:T(4,128)} %bitcast.21), channel_id=1, source_target_pairs={{0,248},{4,252},{8,0},{12,4},{16,8},{20,12},{24,16},{28,20},{32,24... | collective-permute-start | bytes 2312 | tf_op jit(solution)/shard_map/ppermute | solution.py:25
  12.2 1.5 %collective-permute-start.4 = (f32[96,3072]{1,0:T(8,128)}, f32[96,3072]{1,0:T(8,128)}, u32[]{:S(2)}, u32[]{:S(2)}) collective-permute-start(f32[96,3072]{1,0:T(8,128)} %bitcast.13), channel_id=1, source_target_pairs={{0,252},{4,0},{8,4},{12,8},{16,12},{20,16},{24,20},{28,24},{32,28}... | collective-permute-start | bytes 3538952 | tf_op jit(solution)/shard_map/ppermute | solution.py:25
  15.2 3.1 %shard_map.83 = (f32[96,1536]{1,0:T(8,128)}, f32[96,1536]{1,0:T(8,128)}) custom-call(s32[3]{0:T(128)} %add_multiply_fusion.base, s32[4,48]{1,0:T(4,128)} %copy-done.9, s32[4,48]{1,0:T(4,128)} %copy-done.10, f32[96,3072]{1,0:T(8,128)} %bitcast.15), custom_call_target="tpu_custom_call" | custom-call | tf_op jit(solution)/shard_map/pallas_call | solution.py:267
  18.3 6.2 %collective-permute-start.8 = (f32[96,1536]{1,0:T(8,128)}, f32[96,1536]{1,0:T(8,128)S(1)}, u32[]{:S(2)}, u32[]{:S(2)}) collective-permute-start(f32[96,1536]{1,0:T(8,128)} %get-tuple-element.25), channel_id=1, source_target_pairs={{0,248},{4,252},{8,0},{12,4},{16,8},{20,12},{24,16},{28,20},{32,24... | collective-permute-start | bytes 1769480 | tf_op jit(solution)/shard_map/ppermute | solution.py:25
  24.5 3.3 %collective-permute-done.before = f32[96,3072]{1,0:T(8,128)S(1)} collective-permute-done((f32[96,3072]{1,0:T(8,128)}, f32[96,3072]{1,0:T(8,128)S(1)}, u32[]{:S(2)}, u32[]{:S(2)}) %collective-permute-start) | collective-permute-done | bytes 1179680 | tf_op jit(solution)/shard_map/ppermute | solution.py:25
  27.8 3.3 %collective-permute-start.9 = (f32[96,1536]{1,0:T(8,128)}, f32[96,1536]{1,0:T(8,128)}, u32[]{:S(2)}, u32[]{:S(2)}) collective-permute-start(f32[96,1536]{1,0:T(8,128)} %get-tuple-element.26), channel_id=1, source_target_pairs={{0,8},{4,12},{8,16},{12,20},{16,24},{20,28},{24,32},{28,36},{32,40... | collective-permute-start | bytes 1769480 | tf_op jit(solution)/shard_map/ppermute | solution.py:25
  31.1 0.9 slice.8
  32.0 0.9 slice.9
  32.9 5.1 %collective-permute-done.8.up2 = f32[96,1536]{1,0:T(8,128)S(1)} collective-permute-done((f32[96,1536]{1,0:T(8,128)}, f32[96,1536]{1,0:T(8,128)S(1)}, u32[]{:S(2)}, u32[]{:S(2)}) %collective-permute-start.8) | collective-permute-done | bytes 589856 | tf_op jit(solution)/shard_map/ppermute | solution.py:25
  38.0 1.3 collective-permute-start.3
  39.2 11.1 %collective-permute-done.9.down2 = f32[96,1536]{1,0:T(8,128)} collective-permute-done((f32[96,1536]{1,0:T(8,128)}, f32[96,1536]{1,0:T(8,128)}, u32[]{:S(2)}, u32[]{:S(2)}) %collective-permute-start.9) | collective-permute-done | bytes 589856 | tf_op jit(solution)/shard_map/ppermute | solution.py:25
  50.3 12.2 %shard_map.84 = (bf16[96,3072]{1,0:T(8,128)(2,1)}, bf16[96,3072]{1,0:T(8,128)(2,1)}, f32[3,96,96]{2,1,0:T(8,128)}, f32[1,128]{1,0:T(1,128)}, f32[3,96,96]{2,1,0:...) custom-call(s32[1]{0:T(128)} %bitcast.col, ...), custom_call_target="tpu_custom_call" | custom-call | tf_op jit(solution)/shard_map/pallas_call | solution.py:279
  62.6 0.8 copy-done.2
  63.6 4.1 %shard_map.86 = (f32[16,40,128]{2,1,0:T(8,128)}, f32[8,128]{1,0:T(8,128)}) custom-call(s32[1]{0:T(128)} %bitcast.col, f32[3,96,96]{2,1,0:T(8,128)} %get-tuple-element.32.stiff3, f32[1,128]{1,0:T(1,128)} %get-tuple-element.33.stiff_terms, f32[3,96,96]{2,1,0:T(8,128)} %get-tuple-element.34.mass3, f32[1,128]{1,0:T(1,128)} %get-tuple-element.35.mass_terms, ...), custom_call_target="tpu_custom_call" | custom-call | tf_op jit(solution)/shard_map/pallas_call | solution.py:297
  67.7 5.4 %all-to-all-start = ((f32[16,40,128]{2,1,0:T(8,128)}), f32[16,40,128]{2,1,0:T(8,128)S(1)}, u32[]{:S(2)}, u32[]{:S(2)}) async-start(f32[16,40,128]{2,1,0:T(8,128)} %get-tuple-element.38), calls=%async_computation | async-start | bytes 655360 | tf_op jit(solution)/shard_map/all_to_all | solution.py:304
  73.2 2.4 %collective-permute-start.14 = (f32[8,128]{1,0:T(8,128)}, f32[8,128]{1,0:T(8,128)S(1)}, u32[]{:S(2)}, u32[]{:S(2)}) collective-permute-start(f32[8,128]{1,0:T(8,128)} %get-tuple-element.39), channel_id=1, source_target_pairs={{0,2},{1,3},{2,0},{3,1},{4,6},{5,7},{6,4},{7,5},{8,10},{9,11},{10,... | collective-permute-start | bytes 12296 | tf_op jit(solution)/shard_map/ppermute | solution.py:25
  75.7 1.2 collective-permute-start.15
  77.5 1.1 collective-permute-done.15
  79.3 1.5 %all-to-all-done = f32[16,40,128]{2,1,0:T(8,128)S(1)} async-done(((f32[16,40,128]{2,1,0:T(8,128)}), f32[16,40,128]{2,1,0:T(8,128)S(1)}, u32[]{:S(2)}, u32[]{:S(2)}) %all-to-all-start) | async-done | bytes 327712 | tf_op jit(solution)/shard_map/all_to_all | solution.py:304
  80.9 12.0 %all_to_all.15 = f32[4,48,128]{2,1,0:T(8,128)S(1)} all-to-all(f32[4,48,128]{2,1,0:T(8,128)S(1)} %broadcast_in_dim.4), channel_id=1, replica_groups=mesh['zh'=4,'zl'=2,'y'=4,'core'=2,'col'=4] {'zh'}, dimensions={0} | all-to-all | bytes 196608 | tf_op jit(solution)/shard_map/all_to_all | solution.py:320
  92.9 0.8 broadcast_in_dim.5
  93.7 7.0 %all-to-all-start.2 = ((f32[16,48,128]{2,1,0:T(8,128)}), f32[16,48,128]{2,1,0:T(8,128)S(1)}, u32[]{:S(2)}, u32[]{:S(2)}) async-start(f32[16,48,128]{2,1,0:T(8,128)} %broadcast_in_dim.5), calls=%async_computation.2 | async-start | bytes 786432 | tf_op jit(solution)/shard_map/all_to_all | solution.py:322
  100.7 1.1 collective-permute-start.10
  101.8 1.7 %collective-permute-start.11 = (f32[32,3072]{1,0:T(8,128)S(1)}, f32[32,3072]{1,0:T(8,128)S(1)}, u32[]{:S(2)}, u32[]{:S(2)}) collective-permute-start(f32[32,3072]{1,0:T(8,128)S(1)} %copy-done.12), channel_id=1, source_target_pairs={{0,3},{1,0},{2,1},{3,2},{4,7},{5,4},{6,5},{7,6},{8,11},{9,8},{10,9... | collective-permute-start | bytes 1179656 | tf_op jit(solution)/shard_map/ppermute | solution.py:25
  103.5 1.2 collective-permute-start.12
  104.7 7.9 %collective-permute-done.10.from_prev = f32[32,3072]{1,0:T(8,128)S(1)} collective-permute-done((f32[32,3072]{1,0:T(8,128)S(1)}, f32[32,3072]{1,0:T(8,128)S(1)}, u32[]{:S(2)}, u32[]{:S(2)}) %collective-permute-start.10) | collective-permute-done | bytes 393248 | tf_op jit(solution)/shard_map/ppermute | solution.py:25
  112.6 9.5 %collective-permute-done.12.from_opp = f32[32,3072]{1,0:T(8,128)S(1)} collective-permute-done((f32[32,3072]{1,0:T(8,128)S(1)}, f32[32,3072]{1,0:T(8,128)S(1)}, u32[]{:S(2)}, u32[]{:S(2)}) %collective-permute-start.12) | collective-permute-done | bytes 393248 | tf_op jit(solution)/shard_map/ppermute | solution.py:25
  122.9 4.8 %shard_map.85 = (f32[32,3072]{1,0:T(8,128)}, f32[32,3072]{1,0:T(8,128)}) custom-call(s32[1]{0:T(128)} %bitcast.col, f32[96,3072]{1,0:T(8,128)} %bitcast.18, f32[96,3072]{1,0:T(8,128)} %copy-done, f32[96,3072]{1,0:T(8,128)} %copy-done.1, f32[48,3072]{1,0:T(8,128)} %copy-done.2, f32[48,3072]{1,0:T(8,128)} %copy-done.3, f32[384,128]{1,0:T(8,128)} %ritz.5, ...), custom_call_target="tpu_custom_call" | custom-call | tf_op jit(solution)/shard_map/pallas_call | solution.py:309
  128.4 2.1 %shard_map.87 = (f32[96,384]{1,0:T(8,128)}, f32[96,384]{1,0:T(8,128)}, f32[1,32]{1,0:T(1,128)}, f32[32,3072]{1,0:T(8,128)}) custom-call(s32[1]{0:T(128)} %bitcast.col, f32[16,48,128]{2,1,0:T(8,128)} %copy-done.4, f32[32,3072]{1,0:T(8,128)} %get-tuple-element.31.modes, f32[32,3072]{1,0:T(8,128)} %get-tuple-element.40.image), custom_call_target="tpu_custom_call" | custom-call | tf_op jit(solution)/shard_map/pallas_call | solution.py:324
  (47 shorter events, 4.6 us)
Async XLA Ops:
  0.6 27.2 %collective-permute-start = (f32[96,3072]{1,0:T(8,128)}, f32[96,3072]{1,0:T(8,128)S(1)}, u32[]{:S(2)}, u32[]{:S(2)}) collective-permute-start(f32[96,3072]{1,0:T(8,128)} %bitcast.11), channel_id=1, source_target_pairs={{0,1},{1,2},{2,3},{3,0},{4,5},{5,6},{6,7},{7,4},{8,9},{9,10},{10,1... | collective-permute-start | bytes 3538952 | tf_op jit(solution)/shard_map/ppermute | solution.py:25
  2.7 29.2 %collective-permute-start.1 = (f32[96,3072]{1,0:T(8,128)}, f32[96,3072]{1,0:T(8,128)S(1)}, u32[]{:S(2)}, u32[]{:S(2)}) collective-permute-start(f32[96,3072]{1,0:T(8,128)} %bitcast.12), channel_id=1, source_target_pairs={{0,3},{1,0},{2,1},{3,2},{4,7},{5,4},{6,5},{7,6},{8,11},{9,8},{10,9... | collective-permute-start | bytes 3538952 | tf_op jit(solution)/shard_map/ppermute | solution.py:25
  4.1 9.7 %collective-permute-start.6 = (s32[4,48]{1,0:T(4,128)}, s32[4,48]{1,0:T(4,128)S(1)}, u32[]{:S(2)}, u32[]{:S(2)}) collective-permute-start(s32[4,48]{1,0:T(4,128)} %bitcast.20), channel_id=1, source_target_pairs={{0,8},{4,12},{8,16},{12,20},{16,24},{20,28},{24,32},{28,36},{32,40... | collective-permute-start | bytes 2312 | tf_op jit(solution)/shard_map/ppermute | solution.py:25
  5.5 9.1 %collective-permute-start.7 = (s32[4,48]{1,0:T(4,128)}, s32[4,48]{1,0:T(4,128)S(1)}, u32[]{:S(2)}, u32[]{:S(2)}) collective-permute-start(s32[4,48]{1,0:T(4,128)} %bitcast.21), channel_id=1, source_target_pairs={{0,248},{4,252},{8,0},{12,4},{16,8},{20,12},{24,16},{28,20},{32,24... | collective-permute-start | bytes 2312 | tf_op jit(solution)/shard_map/ppermute | solution.py:25
  12.2 38.1 %collective-permute-start.4 = (f32[96,3072]{1,0:T(8,128)}, f32[96,3072]{1,0:T(8,128)}, u32[]{:S(2)}, u32[]{:S(2)}) collective-permute-start(f32[96,3072]{1,0:T(8,128)} %bitcast.13), channel_id=1, source_target_pairs={{0,252},{4,0},{8,4},{12,8},{16,12},{20,16},{24,20},{28,24},{32,28}... | collective-permute-start | bytes 3538952 | tf_op jit(solution)/shard_map/ppermute | solution.py:25
  13.8 0.8 copy-start.9
  13.8 36.6 %collective-permute-start.5 = (f32[96,3072]{1,0:T(8,128)}, f32[96,3072]{1,0:T(8,128)}, u32[]{:S(2)}, u32[]{:S(2)}) collective-permute-start(f32[96,3072]{1,0:T(8,128)} %bitcast.14), channel_id=1, source_target_pairs={{0,4},{4,8},{8,12},{12,16},{16,20},{20,24},{24,28},{28,32},{32,36}... | collective-permute-start | bytes 3538952 | tf_op jit(solution)/shard_map/ppermute | solution.py:25
  14.6 0.6 copy-start.10
  18.3 19.7 %collective-permute-start.8 = (f32[96,1536]{1,0:T(8,128)}, f32[96,1536]{1,0:T(8,128)S(1)}, u32[]{:S(2)}, u32[]{:S(2)}) collective-permute-start(f32[96,1536]{1,0:T(8,128)} %get-tuple-element.25), channel_id=1, source_target_pairs={{0,248},{4,252},{8,0},{12,4},{16,8},{20,12},{24,16},{28,20},{32,24... | collective-permute-start | bytes 1769480 | tf_op jit(solution)/shard_map/ppermute | solution.py:25
  27.8 5.1 %copy-start = (f32[96,3072]{1,0:T(8,128)}, f32[96,3072]{1,0:T(8,128)S(1)}, u32[]{:S(2)}) copy-start(f32[96,3072]{1,0:T(8,128)S(1)} %collective-permute-done.before) | copy-start | bytes 3538948
  27.8 22.5 %collective-permute-start.9 = (f32[96,1536]{1,0:T(8,128)}, f32[96,1536]{1,0:T(8,128)}, u32[]{:S(2)}, u32[]{:S(2)}) collective-permute-start(f32[96,1536]{1,0:T(8,128)} %get-tuple-element.26), channel_id=1, source_target_pairs={{0,8},{4,12},{8,16},{12,20},{16,24},{20,28},{24,32},{28,36},{32,40... | collective-permute-start | bytes 1769480 | tf_op jit(solution)/shard_map/ppermute | solution.py:25
  32.0 18.4 %copy-start.1 = (f32[96,3072]{1,0:T(8,128)}, f32[96,3072]{1,0:T(8,128)S(1)}, u32[]{:S(2)}) copy-start(f32[96,3072]{1,0:T(8,128)S(1)} %collective-permute-done.1.after) | copy-start | bytes 3538948
  32.0 30.6 %collective-permute-start.2 = (f32[48,3072]{1,0:T(8,128)}, f32[48,3072]{1,0:T(8,128)S(1)}, u32[]{:S(2)}, u32[]{:S(2)}) collective-permute-start(f32[48,3072]{1,0:T(8,128)} %slice.8), channel_id=1, source_target_pairs={{0,1},{1,2},{2,3},{3,0},{4,5},{5,6},{6,7},{7,4},{8,9},{9,10},{10,1... | collective-permute-start | bytes 1769480 | tf_op jit(solution)/shard_map/ppermute | solution.py:25
  38.0 12.4 %copy-start.5 = (f32[96,1536]{1,0:T(8,128)}, f32[96,1536]{1,0:T(8,128)S(1)}, u32[]{:S(2)}) copy-start(f32[96,1536]{1,0:T(8,128)S(1)} %collective-permute-done.8.up2) | copy-start | bytes 1769476
  38.0 24.6 %collective-permute-start.3 = (f32[48,3072]{1,0:T(8,128)}, f32[48,3072]{1,0:T(8,128)S(1)}, u32[]{:S(2)}, u32[]{:S(2)}) collective-permute-start(f32[48,3072]{1,0:T(8,128)} %slice.9), channel_id=1, source_target_pairs={{0,3},{1,0},{2,1},{3,2},{4,7},{5,4},{6,5},{7,6},{8,11},{9,8},{10,9... | collective-permute-start | bytes 1769480 | tf_op jit(solution)/shard_map/ppermute | solution.py:25
  62.6 0.8 copy-start.2
  62.6 1.0 copy-start.3
  67.7 13.2 %all-to-all-start = ((f32[16,40,128]{2,1,0:T(8,128)}), f32[16,40,128]{2,1,0:T(8,128)S(1)}, u32[]{:S(2)}, u32[]{:S(2)}) async-start(f32[16,40,128]{2,1,0:T(8,128)} %get-tuple-element.38), calls=%async_computation | async-start | bytes 655360 | tf_op jit(solution)/shard_map/all_to_all | solution.py:304
  73.1 27.6 %copy-start.13 = (f32[32,3072]{1,0:T(8,128)S(1)}, f32[32,3072]{1,0:T(8,128)}, u32[]{:S(2)}) copy-start(f32[32,3072]{1,0:T(8,128)} %get-tuple-element.28) | copy-start | bytes 1179652
  73.1 28.7 %copy-start.12 = (f32[32,3072]{1,0:T(8,128)S(1)}, f32[32,3072]{1,0:T(8,128)}, u32[]{:S(2)}) copy-start(f32[32,3072]{1,0:T(8,128)} %get-tuple-element.29) | copy-start | bytes 1179652
  73.1 30.4 %copy-start.11 = (f32[32,3072]{1,0:T(8,128)S(1)}, f32[32,3072]{1,0:T(8,128)}, u32[]{:S(2)}) copy-start(f32[32,3072]{1,0:T(8,128)} %get-tuple-element.30) | copy-start | bytes 1179652
  73.1 4.3 %collective-permute-start.13 = (f32[8,128]{1,0:T(8,128)}, f32[8,128]{1,0:T(8,128)S(1)}, u32[]{:S(2)}, u32[]{:S(2)}) collective-permute-start(f32[8,128]{1,0:T(8,128)} %get-tuple-element.39), channel_id=1, source_target_pairs={{0,1},{1,2},{2,3},{3,0},{4,5},{5,6},{6,7},{7,4},{8,9},{9,10},{10,1... | collective-permute-start | bytes 12296 | tf_op jit(solution)/shard_map/ppermute | solution.py:25
  73.2 4.3 %collective-permute-start.14 = (f32[8,128]{1,0:T(8,128)}, f32[8,128]{1,0:T(8,128)S(1)}, u32[]{:S(2)}, u32[]{:S(2)}) collective-permute-start(f32[8,128]{1,0:T(8,128)} %get-tuple-element.39), channel_id=1, source_target_pairs={{0,2},{1,3},{2,0},{3,1},{4,6},{5,7},{6,4},{7,5},{8,10},{9,11},{10,... | collective-permute-start | bytes 12296 | tf_op jit(solution)/shard_map/ppermute | solution.py:25
  75.7 3.0 %collective-permute-start.15 = (f32[8,128]{1,0:T(8,128)}, f32[8,128]{1,0:T(8,128)S(1)}, u32[]{:S(2)}, u32[]{:S(2)}) collective-permute-start(f32[8,128]{1,0:T(8,128)} %get-tuple-element.39), channel_id=1, source_target_pairs={{0,3},{1,0},{2,1},{3,2},{4,7},{5,4},{6,5},{7,6},{8,11},{9,8},{10,9... | collective-permute-start | bytes 12296 | tf_op jit(solution)/shard_map/ppermute | solution.py:25
  93.7 33.9 %all-to-all-start.2 = ((f32[16,48,128]{2,1,0:T(8,128)}), f32[16,48,128]{2,1,0:T(8,128)S(1)}, u32[]{:S(2)}, u32[]{:S(2)}) async-start(f32[16,48,128]{2,1,0:T(8,128)} %broadcast_in_dim.5), calls=%async_computation.2 | async-start | bytes 786432 | tf_op jit(solution)/shard_map/all_to_all | solution.py:322
  100.7 11.9 %collective-permute-start.10 = (f32[32,3072]{1,0:T(8,128)S(1)}, f32[32,3072]{1,0:T(8,128)S(1)}, u32[]{:S(2)}, u32[]{:S(2)}) collective-permute-start(f32[32,3072]{1,0:T(8,128)S(1)} %copy-done.13), channel_id=1, source_target_pairs={{0,1},{1,2},{2,3},{3,0},{4,5},{5,6},{6,7},{7,4},{8,9},{9,10},{10,1... | collective-permute-start | bytes 1179656 | tf_op jit(solution)/shard_map/ppermute | solution.py:25
  101.8 10.7 %collective-permute-start.11 = (f32[32,3072]{1,0:T(8,128)S(1)}, f32[32,3072]{1,0:T(8,128)S(1)}, u32[]{:S(2)}, u32[]{:S(2)}) collective-permute-start(f32[32,3072]{1,0:T(8,128)S(1)} %copy-done.12), channel_id=1, source_target_pairs={{0,3},{1,0},{2,1},{3,2},{4,7},{5,4},{6,5},{7,6},{8,11},{9,8},{10,9... | collective-permute-start | bytes 1179656 | tf_op jit(solution)/shard_map/ppermute | solution.py:25
  103.5 18.6 %collective-permute-start.12 = (f32[32,3072]{1,0:T(8,128)S(1)}, f32[32,3072]{1,0:T(8,128)S(1)}, u32[]{:S(2)}, u32[]{:S(2)}) collective-permute-start(f32[32,3072]{1,0:T(8,128)S(1)} %copy-done.11), channel_id=1, source_target_pairs={{0,2},{1,3},{2,0},{3,1},{4,6},{5,7},{6,4},{7,5},{8,10},{9,11},{10,... | collective-permute-start | bytes 1179656 | tf_op jit(solution)/shard_map/ppermute | solution.py:25
  112.5 9.6 %copy-start.6 = (f32[32,3072]{1,0:T(8,128)}, f32[32,3072]{1,0:T(8,128)S(1)}, u32[]{:S(2)}) copy-start(f32[32,3072]{1,0:T(8,128)S(1)} %collective-permute-done.10.from_prev) | copy-start | bytes 1179652
  112.6 9.6 %copy-start.7 = (f32[32,3072]{1,0:T(8,128)}, f32[32,3072]{1,0:T(8,128)S(1)}, u32[]{:S(2)}) copy-start(f32[32,3072]{1,0:T(8,128)S(1)} %collective-permute-done.11.from_next) | copy-start | bytes 1179652
  122.1 0.8 copy-start.8
  127.6 0.7 copy-start.4

commit v5 on v4

--- a/solution.py
+++ b/solution.py
@@ -1,3 +1,5 @@
+import functools
+
 import jax
 import jax.numpy as jnp
 from jax import lax
@@ -6,10 +8,10 @@
 from jax.sharding import Mesh, PartitionSpec as P
 
 
-RING = ("zl", "y", "core")
+RING = ("zl", "y")
 WIRE = ("zh", "zl", "y", "core")
 BLOCK = 64
-PARTS = 16
+PARTS = 8
 TILES = 5
 PAIRS = 4
 LANES = 128
@@ -64,13 +66,22 @@
     return jnp.where(index % 2 == half, tile, pltpu.roll(tile, BLOCK, 1))
 
 
-def pack_kernel(base, prev2, next2, st, to_prev2, to_next2):
+def group_starts(cols, count):
+    blk = cols.shape[1]
+    here = cols[0, 0]
+    above = jnp.where(here + blk == count, 0, here + blk)
+    below = jnp.where(here == 0, count - blk, here - blk)
+    return here, above, below
+
+
+def pack_kernel(cols, prev2, next2, st, to_prev2, to_next2):
     low = low_half((st.shape[0], LANES))
+    here = cols[0, 0]
 
     def step(m, carry):
         for asked, parity, out in ((prev2, 0, to_prev2), (next2, 1, to_next2)):
-            first = block_at(st, asked[3, 4 * m + parity] - base[0], 0)
-            second = block_at(st, asked[3, 4 * m + 2 + parity] - base[0], 1)
+            first = block_at(st, asked[3, 4 * m + parity] - here, 0)
+            second = block_at(st, asked[3, 4 * m + 2 + parity] - here, 1)
             out[:, pl.ds(pl.multiple_of(m * LANES, LANES), LANES)] = jnp.where(low, first, second)
         return carry
 
@@ -78,7 +89,7 @@
 
 
 def image_kernel(
-    col, base, cols, st, up1, down1, up2, down2, values, before, after, ritz,
+    count, col, cols, st, up1, down1, up2, down2, values, before, after, ritz,
     image_high, image_low, stiff, stiff_terms, mass, mass_terms,
     part_own, part_after, part_opp, part_before, stiff_sum, mass_sum, turned
 ):
@@ -88,6 +99,7 @@
     left_half = low_half((width, LANES))
     flip = lambda x: pltpu.roll(x, BLOCK, 1)
     images, owns = [], []
+    base = group_starts(cols, count)
 
     @pl.when(m == 0)
     def _():
@@ -157,10 +169,10 @@
 
 
 def late_kernel(
-    col, stiff3, stiff_terms, mass3, mass_terms, opp_a, opp_b, image_high, image_low, st, ritz,
-    payload, terms, stiff, mass
+    place, stiff3, stiff_terms, mass3, mass_terms, opp_a, opp_b, image_high, image_low, st, ritz,
+    kept, given, terms, stiff, mass
 ):
-    c = col[0]
+    c = place[0]
     width = st.shape[0]
     far = split(jnp.concatenate([opp_a[...], opp_b[...]], axis=0))
     far_stiff = dot4(far, (image_high[...], image_low[...]))[:, :width]
@@ -179,13 +191,19 @@
             whole[pl.ds(at(by), width), :] = piece
         terms[i : i + 1, :] = sums[...] + quotient_terms(block, mine, ritz, at(2))
         turned.append(whole[...].T)
+
+    def gram_tile(t):
+        i, j = t // 3 * 8, t % 3 * LANES
+        if i >= 2 * width:
+            return jnp.zeros((8, LANES), F32)
+        return turned[i // width][i % width : i % width + 8, j : j + LANES]
+
+    first = place[1] == 0
     for t in range(PARTS * TILES):
         k, to = t // TILES, t % TILES * 8
-        i, j = t // 3 * 8, t % 3 * LANES
-        if i < 2 * width:
-            payload[k, to : to + 8, :] = turned[i // width][i % width : i % width + 8, j : j + LANES]
-        else:
-            payload[k, to : to + 8, :] = jnp.zeros((8, LANES), F32)
+        zero, one = gram_tile(t), gram_tile(t + PARTS * TILES)
+        kept[k, to : to + 8, :] = jnp.where(first, zero, one)
+        given[k, to : to + 8, :] = jnp.where(first, one, zero)
 
 
 def modes_kernel(
@@ -206,19 +224,25 @@
     image[...] = (own[...] + from_opp[...]) + (from_prev[...] + from_next[...])
 
 
-def final_kernel(col, parts, modes, image, stiff, mass, theta, residual):
+def final_kernel(place, parts, others, modes, image, stiff, mass, theta, residual):
     total = jnp.float32(196608.0)
-    terms = parts[0, 8 * TILES :, :]
-    for k in range(1, PARTS):
-        terms = terms + parts[k, 8 * TILES :, :]
+    first = place[1] == 0
+
+    def part_tile(k, at):
+        mine, other = parts[k % PARTS, at : at + 8, :], others[k % PARTS, at : at + 8, :]
+        return jnp.where(first, mine, other) if k < PARTS else jnp.where(first, other, mine)
+
+    terms = part_tile(0, 8 * TILES)
+    for k in range(1, 2 * PARTS):
+        terms = terms + part_tile(k, 8 * TILES)
     quotient = terms[0:1, :] / terms[1:2, :]
     shape = (modes.shape[0], LANES)
     here = lax.broadcasted_iota(jnp.int32, shape, 1) == (
-        lax.broadcasted_iota(jnp.int32, shape, 0) + col[0] * shape[0]
+        lax.broadcasted_iota(jnp.int32, shape, 0) + place[0] * shape[0]
     )
     column = jnp.sum(jnp.where(here, jnp.broadcast_to(quotient, shape), 0.0), axis=1, keepdims=True)
     theta[...] = pltpu.roll(
-        jnp.broadcast_to(quotient, (8, LANES)), (4 - col[0]) % 4 * shape[0], 1
+        jnp.broadcast_to(quotient, (8, LANES)), (4 - place[0]) % 4 * shape[0], 1
     )[0:1, : shape[0]]
     residual[...] = image[...] - column * modes[...]
     width = stiff.shape[0]
@@ -226,7 +250,7 @@
         k, at = t // TILES, t % TILES * 8
         i, j = t // 3 * 8, t % 3 * LANES
         out = stiff if i < width else mass
-        out[i % width : i % width + 8, j : j + LANES] = parts[k, at : at + 8, :] / total
+        out[i % width : i % width + 8, j : j + LANES] = part_tile(k, at) / total
 
 
 def call(kernel, shapes, in_specs, dtypes=None, **kwargs):
@@ -250,10 +274,9 @@
     modes = ritz.shape[1] // 4
     half = width // 2
     c = lax.axis_index("col")
-    w = lax.axis_index(WIRE)
-    groups = lax.axis_size(WIRE)
+    count = blk * lax.axis_size(WIRE)
     col = jnp.reshape(c, (1,)).astype(jnp.int32)
-    base = (jnp.stack([w, (w + 1) % groups, (w + groups - 1) % groups]) * blk).astype(jnp.int32)
+    place = jnp.stack([c, lax.axis_index("core")]).astype(jnp.int32)
     st = search.T
     cols = block_cols.T
 
@@ -264,7 +287,7 @@
     up1 = shifted(st, WIRE, -1)
     down1 = shifted(st, WIRE, 1)
 
-    packed = call(pack_kernel, [(width, rows // 2)] * 2, [SMEM] * 3 + [VMEM])(base, prev2, next2, st)
+    packed = call(pack_kernel, [(width, rows // 2)] * 2, [SMEM] * 3 + [VMEM])(cols, prev2, next2, st)
     up2 = shifted(packed[0], WIRE, -2)
     down2 = shifted(packed[1], WIRE, 2)
 
@@ -277,9 +300,9 @@
     grams = [(3, width, width), (1, LANES)] * 2
     gram_specs = [pl.BlockSpec((3, width, width), lambda m: (0, 0, 0)), pl.BlockSpec((1, LANES), lambda m: (0, 0))] * 2
     made = call(
-        image_kernel,
+        functools.partial(image_kernel, count),
         [(width, rows)] * 2 + grams + [(modes, rows)] * 4,
-        [SMEM] * 3
+        [SMEM] * 2
         + [whole] * 3
         + [tile(step_lanes // 2)] * 2
         + [pl.BlockSpec((step_lanes, values.shape[1]), lambda m: (m, 0))]
@@ -291,16 +314,17 @@
         + [pl.BlockSpec((modes, step_lanes), lambda m: (0, m))] * 4,
         grid=(rows // step_lanes,),
         scratch_shapes=[pltpu.VMEM((3 * width, LANES), F32)] * 2 + [pltpu.VMEM((4 * modes, width), F32)],
-    )(col, base, cols, st, up1, down1, up2, down2, values, before, after, ritz)
+    )(col, cols, st, up1, down1, up2, down2, values, before, after, ritz)
     image, grams, (part_own, part_after, part_opp, part_before) = made[:2], made[2:6], made[6:]
 
-    payload, terms = call(
+    kept, given, terms = call(
         late_kernel,
-        [(PARTS, 8 * TILES, LANES), (8, LANES)],
+        [(PARTS, 8 * TILES, LANES)] * 2 + [(8, LANES)],
         [SMEM] + [VMEM] * 10,
         scratch_shapes=[pltpu.VMEM((4 * width, width), F32)] * 2,
-    )(col, *grams, opp_a, opp_b, *image, st, ritz)
-
+    )(place, *grams, opp_a, opp_b, *image, st, ritz)
+
+    payload = kept + shifted(given, "core", 1)
     got = lax.all_to_all(payload, RING, 0, 0, tiled=True)
     around = [shifted(terms, "col", by) for by in (1, 2, 3)]
     from_prev = shifted(part_after, "col", 1)
@@ -320,12 +344,13 @@
     part = lax.all_to_all(part, "zh", 0, 0, tiled=True)
     part = jnp.sum(part, axis=0)
     parts = lax.all_to_all(spread_out(part), RING, 0, 0, tiled=True)
+    others = shifted(parts, "core", 1)
 
     stiff, mass, theta, residual = call(
         final_kernel,
         [(width, 4 * width), (width, 4 * width), (1, modes), (modes, rows)],
-        [SMEM] + [VMEM] * 3,
-    )(col, parts, new_modes, new_image)
+        [SMEM] + [VMEM] * 4,
+    )(place, parts, others, new_modes, new_image)
     return (new_modes.T, residual.T, theta[0], stiff.T, mass.T)
 
 

time: 131 us -> 129 us (0.985)
  the two profiles are of different devices: /device:TPU:1 before, /device:TPU:8 now
where the time goes in v5:
time: 129 us
  starting transfers between devices  41.8 us (32%)
  waiting for transfers between devices  37.1 us (29%)
  Pallas kernels  26.3 us (20%)
  blocking collectives  13.9 us (11%)
  local copies, waits for them, and re-layouts  6.1 us (5%)
  other arithmetic  2.91 us (2%)
    ppermute x18, waiting for transfers between devices, shifted(): lax.ppermute(array, axis, [(i, (i + by) % length) for i in range(length)])  36 us
    ppermute x18, starting transfers between devices, shifted(): lax.ppermute(array, axis, [(i, (i + by) % length) for i in range(length)])  26 us
    all_to_all x1, blocking collectives, shards(): part = lax.all_to_all(part, 'zh', 0, 0, tiled=True)  13.9 us
    pallas_call x1, Pallas kernels, shards(): call(functools.partial(image_kernel, count), [(width, rows)] * 2 + grams...  12.1 us
    all_to_all x1, starting transfers between devices, shards(): got = lax.all_to_all(payload, RING, 0, 0, tiled=True)  10.3 us
    all_to_all x1, starting transfers between devices, shards(): parts = lax.all_to_all(spread_out(part), RING, 0, 0, tiled=True)  5.47 us
    pallas_call x1, Pallas kernels, shards(): call(modes_kernel, [(modes, rows)] * 2, [SMEM] + [VMEM] * 10, scratch_sha...  4.76 us
    pallas_call x1, Pallas kernels, shards(): call(late_kernel, [(PARTS, 8 * TILES, LANES)] * 2 + [(8, LANES)], [SMEM]...  4.01 us
  transfers between devices with their start and end apart: 20, of which 11 were waited for; matrix products, arithmetic and copies ran while one was open for 2% of the time, Pallas kernels for 16%

profile of v5, /device:TPU:8, one launch (start us, length us, event | category | flops | bytes accessed | tf_op | source)
XLA Modules:
  0.0 128.7 jit_solution(1658202335722723501)
XLA Ops:
  0.6 1.6 %collective-permute-start = (f32[96,3072]{1,0:T(8,128)}, f32[96,3072]{1,0:T(8,128)S(1)}, u32[]{:S(2)}, u32[]{:S(2)}) collective-permute-start(f32[96,3072]{1,0:T(8,128)} %bitcast.9), channel_id=1, source_target_pairs={{0,1},{1,2},{2,3},{3,0},{4,5},{5,6},{6,7},{7,4},{8,9},{9,10},{10,1... | collective-permute-start | bytes 3538952 | tf_op jit(solution)/shard_map/ppermute | solution.py:27
  2.2 1.7 %collective-permute-start.1 = (f32[96,3072]{1,0:T(8,128)}, f32[96,3072]{1,0:T(8,128)S(1)}, u32[]{:S(2)}, u32[]{:S(2)}) collective-permute-start(f32[96,3072]{1,0:T(8,128)} %bitcast.10), channel_id=1, source_target_pairs={{0,3},{1,0},{2,1},{3,2},{4,7},{5,4},{6,5},{7,6},{8,11},{9,8},{10,9... | collective-permute-start | bytes 3538952 | tf_op jit(solution)/shard_map/ppermute | solution.py:27
  3.9 1.6 %collective-permute-start.6 = (s32[4,48]{1,0:T(4,128)}, s32[4,48]{1,0:T(4,128)S(1)}, u32[]{:S(2)}, u32[]{:S(2)}) collective-permute-start(s32[4,48]{1,0:T(4,128)} %bitcast.18), channel_id=1, source_target_pairs={{0,8},{4,12},{8,16},{12,20},{16,24},{20,28},{24,32},{28,36},{32,40... | collective-permute-start | bytes 2312 | tf_op jit(solution)/shard_map/ppermute | solution.py:27
  6.1 5.2 %collective-permute-start.4 = (f32[96,3072]{1,0:T(8,128)}, f32[96,3072]{1,0:T(8,128)}, u32[]{:S(2)}, u32[]{:S(2)}) collective-permute-start(f32[96,3072]{1,0:T(8,128)} %bitcast.11), channel_id=1, source_target_pairs={{0,252},{4,0},{8,4},{12,8},{16,12},{20,16},{24,20},{28,24},{32,28}... | collective-permute-start | bytes 3538952 | tf_op jit(solution)/shard_map/ppermute | solution.py:27
  12.5 3.1 %shard_map.83 = (f32[96,1536]{1,0:T(8,128)}, f32[96,1536]{1,0:T(8,128)}) custom-call(s32[4,48]{1,0:T(4,128)} %bitcast.20, s32[4,48]{1,0:T(4,128)} %copy-done.10, s32[4,48]{1,0:T(4,128)} %copy-done.11, f32[96,3072]{1,0:T(8,128)} %bitcast.13), custom_call_target="tpu_custom_call" | custom-call | tf_op jit(solution)/shard_map/pallas_call | solution.py:290
  15.6 3.2 %collective-permute-start.8 = (f32[96,1536]{1,0:T(8,128)}, f32[96,1536]{1,0:T(8,128)S(1)}, u32[]{:S(2)}, u32[]{:S(2)}) collective-permute-start(f32[96,1536]{1,0:T(8,128)} %get-tuple-element.26), channel_id=1, source_target_pairs={{0,248},{4,252},{8,0},{12,4},{16,8},{20,12},{24,16},{28,20},{32,24... | collective-permute-start | bytes 1769480 | tf_op jit(solution)/shard_map/ppermute | solution.py:27
  18.8 11.1 %collective-permute-done.before = f32[96,3072]{1,0:T(8,128)S(1)} collective-permute-done((f32[96,3072]{1,0:T(8,128)}, f32[96,3072]{1,0:T(8,128)S(1)}, u32[]{:S(2)}, u32[]{:S(2)}) %collective-permute-start) | collective-permute-done | bytes 1179680 | tf_op jit(solution)/shard_map/ppermute | solution.py:27
  29.8 1.6 %collective-permute-start.9 = (f32[96,1536]{1,0:T(8,128)}, f32[96,1536]{1,0:T(8,128)}, u32[]{:S(2)}, u32[]{:S(2)}) collective-permute-start(f32[96,1536]{1,0:T(8,128)} %get-tuple-element.27), channel_id=1, source_target_pairs={{0,8},{4,12},{8,16},{12,20},{16,24},{20,28},{24,32},{28,36},{32,40... | collective-permute-start | bytes 1769480 | tf_op jit(solution)/shard_map/ppermute | solution.py:27
  31.4 0.9 slice.8
  32.6 0.9 slice.9
  33.5 4.4 %collective-permute-done.8.up2 = f32[96,1536]{1,0:T(8,128)S(1)} collective-permute-done((f32[96,1536]{1,0:T(8,128)}, f32[96,1536]{1,0:T(8,128)S(1)}, u32[]{:S(2)}, u32[]{:S(2)}) %collective-permute-start.8) | collective-permute-done | bytes 589856 | tf_op jit(solution)/shard_map/ppermute | solution.py:27
  38.0 1.5 %collective-permute-start.3 = (f32[48,3072]{1,0:T(8,128)}, f32[48,3072]{1,0:T(8,128)S(1)}, u32[]{:S(2)}, u32[]{:S(2)}) collective-permute-start(f32[48,3072]{1,0:T(8,128)} %slice.9), channel_id=1, source_target_pairs={{0,3},{1,0},{2,1},{3,2},{4,7},{5,4},{6,5},{7,6},{8,11},{9,8},{10,9... | collective-permute-start | bytes 1769480 | tf_op jit(solution)/shard_map/ppermute | solution.py:27
  40.1 4.2 %collective-permute-done.9.down2 = f32[96,1536]{1,0:T(8,128)} collective-permute-done((f32[96,1536]{1,0:T(8,128)}, f32[96,1536]{1,0:T(8,128)}, u32[]{:S(2)}, u32[]{:S(2)}) %collective-permute-start.9) | collective-permute-done | bytes 589856 | tf_op jit(solution)/shard_map/ppermute | solution.py:27
  44.4 12.1 %shard_map.84 = (bf16[96,3072]{1,0:T(8,128)(2,1)}, bf16[96,3072]{1,0:T(8,128)(2,1)}, f32[3,96,96]{2,1,0:T(8,128)}, f32[1,128]{1,0:T(1,128)}, f32[3,96,96]{2,1,0:...) custom-call(s32[1]{0:T(128)} %bitcast.col, ...), custom_call_target="tpu_custom_call" | custom-call | tf_op jit(solution)/shard_map/pallas_call | solution.py:302
  57.5 4.0 %shard_map.86 = (f32[8,40,128]{2,1,0:T(8,128)}, f32[8,40,128]{2,1,0:T(8,128)}, f32[8,128]{1,0:T(8,128)}) custom-call(s32[2]{0:T(128)} %pad_add_fusion.place, f32[3,96,96]{2,1,0:T(8,128)} %get-tuple-element.33.stiff3, f32[1,128]{1,0:T(1,128)} %get-tuple-element.34.stiff_terms, f32[3,96,96]{2,1,0:T(8,128)} %get-tuple-element.35.mass3, ...), custom_call_target="tpu_custom_call" | custom-call | tf_op jit(solution)/shard_map/pallas_call | solution.py:320
  61.7 1.6 %collective-permute-done.13 = f32[8,40,128]{2,1,0:T(8,128)S(1)} collective-permute-done((f32[8,40,128]{2,1,0:T(8,128)}, f32[8,40,128]{2,1,0:T(8,128)S(1)}, u32[]{:S(2)}, u32[]{:S(2)}) %collective-permute-start.13) | collective-permute-done | bytes 163872 | tf_op jit(solution)/shard_map/ppermute | solution.py:27
  63.3 1.6 %add.12 = f32[8,40,128]{2,1,0:T(8,128)} add(f32[8,40,128]{2,1,0:T(8,128)} %get-tuple-element.39, f32[8,40,128]{2,1,0:T(8,128)S(1)} %collective-permute-done.13) | non-fusion elementwise | flops 40960 | bytes 491520 | tf_op jit(solution)/shard_map/add | solution.py:327
  64.8 10.3 %all-to-all-start = ((f32[8,40,128]{2,1,0:T(8,128)}), f32[8,40,128]{2,1,0:T(8,128)S(1)}, u32[]{:S(2)}, u32[]{:S(2)}) async-start(f32[8,40,128]{2,1,0:T(8,128)} %add.12), calls=%async_computation | async-start | bytes 327680 | tf_op jit(solution)/shard_map/all_to_all | solution.py:328
  75.5 2.7 %collective-permute-start.15 = (f32[8,128]{1,0:T(8,128)}, f32[8,128]{1,0:T(8,128)S(1)}, u32[]{:S(2)}, u32[]{:S(2)}) collective-permute-start(f32[8,128]{1,0:T(8,128)} %get-tuple-element.41), channel_id=1, source_target_pairs={{0,2},{1,3},{2,0},{3,1},{4,6},{5,7},{6,4},{7,5},{8,10},{9,11},{10,... | collective-permute-start | bytes 12296 | tf_op jit(solution)/shard_map/ppermute | solution.py:27
  78.2 1.4 %collective-permute-start.16 = (f32[8,128]{1,0:T(8,128)}, f32[8,128]{1,0:T(8,128)S(1)}, u32[]{:S(2)}, u32[]{:S(2)}) collective-permute-start(f32[8,128]{1,0:T(8,128)} %get-tuple-element.41), channel_id=1, source_target_pairs={{0,3},{1,0},{2,1},{3,2},{4,7},{5,4},{6,5},{7,6},{8,11},{9,8},{10,9... | collective-permute-start | bytes 12296 | tf_op jit(solution)/shard_map/ppermute | solution.py:27
  80.8 1.2 collective-permute-done.16
  82.7 13.9 %all_to_all.15 = f32[4,48,128]{2,1,0:T(8,128)S(1)} all-to-all(f32[4,48,128]{2,1,0:T(8,128)S(1)} %broadcast_in_dim.4), channel_id=1, replica_groups=mesh['zh'=4,'zl'=2,'y'=4,'core'=2,'col'=4] {'zh'}, dimensions={0} | all-to-all | bytes 196608 | tf_op jit(solution)/shard_map/all_to_all | solution.py:344
  97.3 5.5 %all-to-all-start.2 = ((f32[8,48,128]{2,1,0:T(8,128)}), f32[8,48,128]{2,1,0:T(8,128)S(1)}, u32[]{:S(2)}, u32[]{:S(2)}) async-start(f32[8,48,128]{2,1,0:T(8,128)} %broadcast_in_dim.5), calls=%async_computation.2 | async-start | bytes 393216 | tf_op jit(solution)/shard_map/all_to_all | solution.py:346
  102.8 1.1 collective-permute-start.10
  103.9 2.2 %collective-permute-start.11 = (f32[32,3072]{1,0:T(8,128)S(1)}, f32[32,3072]{1,0:T(8,128)S(1)}, u32[]{:S(2)}, u32[]{:S(2)}) collective-permute-start(f32[32,3072]{1,0:T(8,128)S(1)} %copy-done.13), channel_id=1, source_target_pairs={{0,3},{1,0},{2,1},{3,2},{4,7},{5,4},{6,5},{7,6},{8,11},{9,8},{10,9... | collective-permute-start | bytes 1179656 | tf_op jit(solution)/shard_map/ppermute | solution.py:27
  106.0 1.0 collective-permute-start.12
  107.0 1.0 all-to-all-done.2.parts
  108.0 8.0 %collective-permute-done.10.from_prev = f32[32,3072]{1,0:T(8,128)S(1)} collective-permute-done((f32[32,3072]{1,0:T(8,128)S(1)}, f32[32,3072]{1,0:T(8,128)S(1)}, u32[]{:S(2)}, u32[]{:S(2)}) %collective-permute-start.10) | collective-permute-done | bytes 393248 | tf_op jit(solution)/shard_map/ppermute | solution.py:27
  116.0 3.0 %collective-permute-done.11.from_next = f32[32,3072]{1,0:T(8,128)S(1)} collective-permute-done((f32[32,3072]{1,0:T(8,128)S(1)}, f32[32,3072]{1,0:T(8,128)S(1)}, u32[]{:S(2)}, u32[]{:S(2)}) %collective-permute-start.11) | collective-permute-done | bytes 393248 | tf_op jit(solution)/shard_map/ppermute | solution.py:27
  119.0 1.3 %collective-permute-done.12.from_opp = f32[32,3072]{1,0:T(8,128)S(1)} collective-permute-done((f32[32,3072]{1,0:T(8,128)S(1)}, f32[32,3072]{1,0:T(8,128)S(1)}, u32[]{:S(2)}, u32[]{:S(2)}) %collective-permute-start.12) | collective-permute-done | bytes 393248 | tf_op jit(solution)/shard_map/ppermute | solution.py:27
  121.1 4.8 %shard_map.85 = (f32[32,3072]{1,0:T(8,128)}, f32[32,3072]{1,0:T(8,128)}) custom-call(s32[1]{0:T(128)} %bitcast.col, f32[96,3072]{1,0:T(8,128)} %bitcast.16, f32[96,3072]{1,0:T(8,128)} %copy-done, f32[96,3072]{1,0:T(8,128)} %copy-done.1, f32[48,3072]{1,0:T(8,128)} %copy-done.2, f32[48,3072]{1,0:T(8,128)} %copy-done.3, f32[384,128]{1,0:T(8,128)} %ritz.5, ...), custom_call_target="tpu_custom_call" | custom-call | tf_op jit(solution)/shard_map/pallas_call | solution.py:333
  126.5 2.2 %shard_map.87 = (f32[96,384]{1,0:T(8,128)}, f32[96,384]{1,0:T(8,128)}, f32[1,32]{1,0:T(1,128)}, f32[32,3072]{1,0:T(8,128)}) custom-call(s32[2]{0:T(128)} %pad_add_fusion.place, f32[8,48,128]{2,1,0:T(8,128)} %copy-done.4, f32[8,48,128]{2,1,0:T(8,128)} %copy-done.9, f32[32,3072]{1,0:T(8,128)} %get-tuple-element.32.modes, f32[32,3072]{1,0:T(8,128)} %get-tuple-element.42.image), custom_call_target="tpu_custom_call" | custom-call | tf_op jit(solution)/shard_map/pallas_call | solution.py:349
  (54 shorter events, 8.0 us)
Async XLA Ops:
  0.6 29.2 %collective-permute-start = (f32[96,3072]{1,0:T(8,128)}, f32[96,3072]{1,0:T(8,128)S(1)}, u32[]{:S(2)}, u32[]{:S(2)}) collective-permute-start(f32[96,3072]{1,0:T(8,128)} %bitcast.9), channel_id=1, source_target_pairs={{0,1},{1,2},{2,3},{3,0},{4,5},{5,6},{6,7},{7,4},{8,9},{9,10},{10,1... | collective-permute-start | bytes 3538952 | tf_op jit(solution)/shard_map/ppermute | solution.py:27
  2.2 30.1 %collective-permute-start.1 = (f32[96,3072]{1,0:T(8,128)}, f32[96,3072]{1,0:T(8,128)S(1)}, u32[]{:S(2)}, u32[]{:S(2)}) collective-permute-start(f32[96,3072]{1,0:T(8,128)} %bitcast.10), channel_id=1, source_target_pairs={{0,3},{1,0},{2,1},{3,2},{4,7},{5,4},{6,5},{7,6},{8,11},{9,8},{10,9... | collective-permute-start | bytes 3538952 | tf_op jit(solution)/shard_map/ppermute | solution.py:27
  3.9 7.4 %collective-permute-start.6 = (s32[4,48]{1,0:T(4,128)}, s32[4,48]{1,0:T(4,128)S(1)}, u32[]{:S(2)}, u32[]{:S(2)}) collective-permute-start(s32[4,48]{1,0:T(4,128)} %bitcast.18), channel_id=1, source_target_pairs={{0,8},{4,12},{8,16},{12,20},{16,24},{20,28},{24,32},{28,36},{32,40... | collective-permute-start | bytes 2312 | tf_op jit(solution)/shard_map/ppermute | solution.py:27
  5.5 5.8 %collective-permute-start.7 = (s32[4,48]{1,0:T(4,128)}, s32[4,48]{1,0:T(4,128)S(1)}, u32[]{:S(2)}, u32[]{:S(2)}) collective-permute-start(s32[4,48]{1,0:T(4,128)} %bitcast.19), channel_id=1, source_target_pairs={{0,248},{4,252},{8,0},{12,4},{16,8},{20,12},{24,16},{28,20},{32,24... | collective-permute-start | bytes 2312 | tf_op jit(solution)/shard_map/ppermute | solution.py:27
  6.1 38.3 %collective-permute-start.4 = (f32[96,3072]{1,0:T(8,128)}, f32[96,3072]{1,0:T(8,128)}, u32[]{:S(2)}, u32[]{:S(2)}) collective-permute-start(f32[96,3072]{1,0:T(8,128)} %bitcast.11), channel_id=1, source_target_pairs={{0,252},{4,0},{8,4},{12,8},{16,12},{20,16},{24,20},{28,24},{32,28}... | collective-permute-start | bytes 3538952 | tf_op jit(solution)/shard_map/ppermute | solution.py:27
  11.3 33.1 %collective-permute-start.5 = (f32[96,3072]{1,0:T(8,128)}, f32[96,3072]{1,0:T(8,128)}, u32[]{:S(2)}, u32[]{:S(2)}) collective-permute-start(f32[96,3072]{1,0:T(8,128)} %bitcast.12), channel_id=1, source_target_pairs={{0,4},{4,8},{8,12},{12,16},{16,20},{20,24},{24,28},{28,32},{32,36}... | collective-permute-start | bytes 3538952 | tf_op jit(solution)/shard_map/ppermute | solution.py:27
  15.6 22.4 %collective-permute-start.8 = (f32[96,1536]{1,0:T(8,128)}, f32[96,1536]{1,0:T(8,128)S(1)}, u32[]{:S(2)}, u32[]{:S(2)}) collective-permute-start(f32[96,1536]{1,0:T(8,128)} %get-tuple-element.26), channel_id=1, source_target_pairs={{0,248},{4,252},{8,0},{12,4},{16,8},{20,12},{24,16},{28,20},{32,24... | collective-permute-start | bytes 1769480 | tf_op jit(solution)/shard_map/ppermute | solution.py:27
  29.8 3.7 %copy-start = (f32[96,3072]{1,0:T(8,128)}, f32[96,3072]{1,0:T(8,128)S(1)}, u32[]{:S(2)}) copy-start(f32[96,3072]{1,0:T(8,128)S(1)} %collective-permute-done.before) | copy-start | bytes 3538948
  29.8 14.5 %collective-permute-start.9 = (f32[96,1536]{1,0:T(8,128)}, f32[96,1536]{1,0:T(8,128)}, u32[]{:S(2)}, u32[]{:S(2)}) collective-permute-start(f32[96,1536]{1,0:T(8,128)} %get-tuple-element.27), channel_id=1, source_target_pairs={{0,8},{4,12},{8,16},{12,20},{16,24},{20,28},{24,32},{28,36},{32,40... | collective-permute-start | bytes 1769480 | tf_op jit(solution)/shard_map/ppermute | solution.py:27
  32.3 12.1 %copy-start.1 = (f32[96,3072]{1,0:T(8,128)}, f32[96,3072]{1,0:T(8,128)S(1)}, u32[]{:S(2)}) copy-start(f32[96,3072]{1,0:T(8,128)S(1)} %collective-permute-done.1.after) | copy-start | bytes 3538948
  32.3 24.2 %collective-permute-start.2 = (f32[48,3072]{1,0:T(8,128)}, f32[48,3072]{1,0:T(8,128)S(1)}, u32[]{:S(2)}, u32[]{:S(2)}) collective-permute-start(f32[48,3072]{1,0:T(8,128)} %slice.8), channel_id=1, source_target_pairs={{0,1},{1,2},{2,3},{3,0},{4,5},{5,6},{6,7},{7,4},{8,9},{9,10},{10,1... | collective-permute-start | bytes 1769480 | tf_op jit(solution)/shard_map/ppermute | solution.py:27
  38.0 6.4 %copy-start.5 = (f32[96,1536]{1,0:T(8,128)}, f32[96,1536]{1,0:T(8,128)S(1)}, u32[]{:S(2)}) copy-start(f32[96,1536]{1,0:T(8,128)S(1)} %collective-permute-done.8.up2) | copy-start | bytes 1769476
  38.0 18.5 %collective-permute-start.3 = (f32[48,3072]{1,0:T(8,128)}, f32[48,3072]{1,0:T(8,128)S(1)}, u32[]{:S(2)}, u32[]{:S(2)}) collective-permute-start(f32[48,3072]{1,0:T(8,128)} %slice.9), channel_id=1, source_target_pairs={{0,3},{1,0},{2,1},{3,2},{4,7},{5,4},{6,5},{7,6},{8,11},{9,8},{10,9... | collective-permute-start | bytes 1769480 | tf_op jit(solution)/shard_map/ppermute | solution.py:27
  56.5 0.8 copy-start.2
  56.5 1.0 copy-start.3
  61.5 41.2 %copy-start.14 = (f32[32,3072]{1,0:T(8,128)S(1)}, f32[32,3072]{1,0:T(8,128)}, u32[]{:S(2)}) copy-start(f32[32,3072]{1,0:T(8,128)} %get-tuple-element.29) | copy-start | bytes 1179652
  61.5 42.3 %copy-start.13 = (f32[32,3072]{1,0:T(8,128)S(1)}, f32[32,3072]{1,0:T(8,128)}, u32[]{:S(2)}) copy-start(f32[32,3072]{1,0:T(8,128)} %get-tuple-element.30) | copy-start | bytes 1179652
  61.6 44.5 %copy-start.12 = (f32[32,3072]{1,0:T(8,128)S(1)}, f32[32,3072]{1,0:T(8,128)}, u32[]{:S(2)}) copy-start(f32[32,3072]{1,0:T(8,128)} %get-tuple-element.31) | copy-start | bytes 1179652
  61.6 1.7 %collective-permute-start.13 = (f32[8,40,128]{2,1,0:T(8,128)}, f32[8,40,128]{2,1,0:T(8,128)S(1)}, u32[]{:S(2)}, u32[]{:S(2)}) collective-permute-start(f32[8,40,128]{2,1,0:T(8,128)} %get-tuple-element.40), channel_id=1, source_target_pairs={{0,4},{4,0},{1,5},{5,1},{2,6},{6,2},{3,7},{7,3},{8,12},{12,8},{9,1... | collective-permute-start | bytes 491528 | tf_op jit(solution)/shard_map/ppermute | solution.py:27
  64.8 17.8 %all-to-all-start = ((f32[8,40,128]{2,1,0:T(8,128)}), f32[8,40,128]{2,1,0:T(8,128)S(1)}, u32[]{:S(2)}, u32[]{:S(2)}) async-start(f32[8,40,128]{2,1,0:T(8,128)} %add.12), calls=%async_computation | async-start | bytes 327680 | tf_op jit(solution)/shard_map/all_to_all | solution.py:328
  75.2 5.0 %collective-permute-start.14 = (f32[8,128]{1,0:T(8,128)}, f32[8,128]{1,0:T(8,128)S(1)}, u32[]{:S(2)}, u32[]{:S(2)}) collective-permute-start(f32[8,128]{1,0:T(8,128)} %get-tuple-element.41), channel_id=1, source_target_pairs={{0,1},{1,2},{2,3},{3,0},{4,5},{5,6},{6,7},{7,4},{8,9},{9,10},{10,1... | collective-permute-start | bytes 12296 | tf_op jit(solution)/shard_map/ppermute | solution.py:27
  75.5 5.3 %collective-permute-start.15 = (f32[8,128]{1,0:T(8,128)}, f32[8,128]{1,0:T(8,128)S(1)}, u32[]{:S(2)}, u32[]{:S(2)}) collective-permute-start(f32[8,128]{1,0:T(8,128)} %get-tuple-element.41), channel_id=1, source_target_pairs={{0,2},{1,3},{2,0},{3,1},{4,6},{5,7},{6,4},{7,5},{8,10},{9,11},{10,... | collective-permute-start | bytes 12296 | tf_op jit(solution)/shard_map/ppermute | solution.py:27
  78.2 3.8 %collective-permute-start.16 = (f32[8,128]{1,0:T(8,128)}, f32[8,128]{1,0:T(8,128)S(1)}, u32[]{:S(2)}, u32[]{:S(2)}) collective-permute-start(f32[8,128]{1,0:T(8,128)} %get-tuple-element.41), channel_id=1, source_target_pairs={{0,3},{1,0},{2,1},{3,2},{4,7},{5,4},{6,5},{7,6},{8,11},{9,8},{10,9... | collective-permute-start | bytes 12296 | tf_op jit(solution)/shard_map/ppermute | solution.py:27
  97.3 10.7 %all-to-all-start.2 = ((f32[8,48,128]{2,1,0:T(8,128)}), f32[8,48,128]{2,1,0:T(8,128)S(1)}, u32[]{:S(2)}, u32[]{:S(2)}) async-start(f32[8,48,128]{2,1,0:T(8,128)} %broadcast_in_dim.5), calls=%async_computation.2 | async-start | bytes 393216 | tf_op jit(solution)/shard_map/all_to_all | solution.py:346
  102.8 13.2 %collective-permute-start.10 = (f32[32,3072]{1,0:T(8,128)S(1)}, f32[32,3072]{1,0:T(8,128)S(1)}, u32[]{:S(2)}, u32[]{:S(2)}) collective-permute-start(f32[32,3072]{1,0:T(8,128)S(1)} %copy-done.14), channel_id=1, source_target_pairs={{0,1},{1,2},{2,3},{3,0},{4,5},{5,6},{6,7},{7,4},{8,9},{9,10},{10,1... | collective-permute-start | bytes 1179656 | tf_op jit(solution)/shard_map/ppermute | solution.py:27
  103.9 15.1 %collective-permute-start.11 = (f32[32,3072]{1,0:T(8,128)S(1)}, f32[32,3072]{1,0:T(8,128)S(1)}, u32[]{:S(2)}, u32[]{:S(2)}) collective-permute-start(f32[32,3072]{1,0:T(8,128)S(1)} %copy-done.13), channel_id=1, source_target_pairs={{0,3},{1,0},{2,1},{3,2},{4,7},{5,4},{6,5},{7,6},{8,11},{9,8},{10,9... | collective-permute-start | bytes 1179656 | tf_op jit(solution)/shard_map/ppermute | solution.py:27
  106.0 14.3 %collective-permute-start.12 = (f32[32,3072]{1,0:T(8,128)S(1)}, f32[32,3072]{1,0:T(8,128)S(1)}, u32[]{:S(2)}, u32[]{:S(2)}) collective-permute-start(f32[32,3072]{1,0:T(8,128)S(1)} %copy-done.12), channel_id=1, source_target_pairs={{0,2},{1,3},{2,0},{3,1},{4,6},{5,7},{6,4},{7,5},{8,10},{9,11},{10,... | collective-permute-start | bytes 1179656 | tf_op jit(solution)/shard_map/ppermute | solution.py:27
  108.0 17.8 %copy-start.4 = (f32[8,48,128]{2,1,0:T(8,128)}, f32[8,48,128]{2,1,0:T(8,128)S(1)}, u32[]{:S(2)}) copy-start(f32[8,48,128]{2,1,0:T(8,128)S(1)} %all-to-all-done.2.parts) | copy-start | bytes 589828
  108.0 17.8 %collective-permute-start.17 = (f32[8,48,128]{2,1,0:T(8,128)S(1)}, f32[8,48,128]{2,1,0:T(8,128)S(1)}, u32[]{:S(2)}, u32[]{:S(2)}) collective-permute-start(f32[8,48,128]{2,1,0:T(8,128)S(1)} %all-to-all-done.2.parts), channel_id=1, source_target_pairs={{0,4},{4,0},{1,5},{5,1},{2,6},{6,2},{3,7},{7,3},{8,12},{12,8},{9,1... | collective-permute-start | bytes 589832 | tf_op jit(solution)/shard_map/ppermute | solution.py:27
  116.0 4.3 %copy-start.6 = (f32[32,3072]{1,0:T(8,128)}, f32[32,3072]{1,0:T(8,128)S(1)}, u32[]{:S(2)}) copy-start(f32[32,3072]{1,0:T(8,128)S(1)} %collective-permute-done.10.from_prev) | copy-start | bytes 1179652
  119.0 1.3 %copy-start.7 = (f32[32,3072]{1,0:T(8,128)}, f32[32,3072]{1,0:T(8,128)S(1)}, u32[]{:S(2)}) copy-start(f32[32,3072]{1,0:T(8,128)S(1)} %collective-permute-done.11.from_next) | copy-start | bytes 1179652
  120.3 0.8 copy-start.8
  (3 other events, 1.8 us)

commit v6 on v4

--- a/solution.py
+++ b/solution.py
@@ -1,3 +1,5 @@
+import functools
+
 import jax
 import jax.numpy as jnp
 from jax import lax
@@ -25,6 +27,12 @@
     return lax.ppermute(array, axis, [(i, (i + by) % length) for i in range(length)])
 
 
+def to_sides(array, distance):
+    length = lax.axis_size(WIRE)
+    pairs = [((i - distance if i % 2 == 0 else i + distance) % length, i) for i in range(length)]
+    return lax.ppermute(array, WIRE, pairs)
+
+
 def split(x):
     high = x.astype(jnp.bfloat16)
     return high, (x - high.astype(F32)).astype(jnp.bfloat16)
@@ -59,26 +67,21 @@
     return lax.broadcasted_iota(jnp.int32, shape, 1) < BLOCK
 
 
-def block_at(ref, index, half):
-    tile = ref[:, pl.ds(pl.multiple_of(index // 2 * LANES, LANES), LANES)]
+def tile_at(ref, index):
+    return ref[:, pl.ds(pl.multiple_of(index // 2 * LANES, LANES), LANES)]
+
+
+def in_half(tile, index, half):
     return jnp.where(index % 2 == half, tile, pltpu.roll(tile, BLOCK, 1))
 
 
-def pack_kernel(base, prev2, next2, st, to_prev2, to_next2):
-    low = low_half((st.shape[0], LANES))
-
-    def step(m, carry):
-        for asked, parity, out in ((prev2, 0, to_prev2), (next2, 1, to_next2)):
-            first = block_at(st, asked[3, 4 * m + parity] - base[0], 0)
-            second = block_at(st, asked[3, 4 * m + 2 + parity] - base[0], 1)
-            out[:, pl.ds(pl.multiple_of(m * LANES, LANES), LANES)] = jnp.where(low, first, second)
-        return carry
-
-    lax.fori_loop(0, to_prev2.shape[1] // LANES, step, 0, unroll=4)
+def group_start(here, by, blk, count):
+    start = here + by * blk
+    return jnp.where(start >= count, start - count, jnp.where(start < 0, start + count, start))
 
 
 def image_kernel(
-    col, base, cols, st, up1, down1, up2, down2, values, before, after, ritz,
+    count, col, cols, st, swap, near, relay, far, values, before, after, ritz,
     image_high, image_low, stiff, stiff_terms, mass, mass_terms,
     part_own, part_after, part_opp, part_before, stiff_sum, mass_sum, turned
 ):
@@ -88,6 +91,11 @@
     left_half = low_half((width, LANES))
     flip = lambda x: pltpu.roll(x, BLOCK, 1)
     images, owns = [], []
+    blk = cols.shape[1]
+    here = cols[0, 0]
+    even = here // blk % 2 == 0
+    starts = [group_start(here, by, blk, count) for by in (1, 2, -1, -2)]
+    sources = ((swap, near), (relay, far), (near, swap), (far, relay))
 
     @pl.when(m == 0)
     def _():
@@ -106,20 +114,21 @@
         own = st[:, pl.ds(pl.multiple_of(tile * LANES, LANES), LANES)]
         owns.append(own)
         left, right = [], []
-        for q, (far1, far2, at) in enumerate(((up1, up2, 1), (down1, down2, 2))):
+        for q in range(2):
             row = 2 * tile + q
-            near = block_at(st, cols[1, row] - base[0], 1 - q)
-            first = jnp.where(left_half, own, near) if q == 0 else jnp.where(left_half, near, own)
-            side = h % 2
-            other = block_at(far1, cols[2, row] - base[at], 1 - side)
-            second = far2[:, h // 2 * LANES : (h // 2 + 1) * LANES]
-            second = jnp.where(left_half, second, other) if side == 0 else jnp.where(left_half, other, second)
-            left.append(jnp.concatenate([first, second], axis=1))
+            index = cols[1, row] - here
+            close = in_half(tile_at(st, index), index, 1 - q)
+            first = jnp.where(left_half, own, close) if q == 0 else jnp.where(left_half, close, own)
+            beyond = []
+            for slot in range(2):
+                index = cols[2 + slot, row] - starts[2 * q + slot]
+                one, two = (tile_at(ref, index) for ref in sources[2 * q + slot])
+                beyond.append(in_half(jnp.where(even, one, two), index, slot))
+            left.append(jnp.concatenate([first, jnp.where(left_half, *beyond)], axis=1))
             coef = values[(2 * h + q) * BLOCK : (2 * h + q + 1) * BLOCK, :]
-            one, two = coef[:, :LANES], coef[:, LANES:]
-            one = one if q == 0 else flip(one)
-            two = flip(two) if side == 0 else two
-            right.append(jnp.concatenate([one, two], axis=1))
+            if q:
+                coef = jnp.concatenate([flip(coef[:, :LANES]), coef[:, LANES:]], axis=1)
+            right.append(coef)
         part = dot4(split(jnp.concatenate(left, axis=0)), split(jnp.concatenate(right, axis=0)))
         images.append(split(4.0 * own + jnp.where(left_half, part[:width], part[width:])))
         if h % 2:
@@ -250,23 +259,17 @@
     modes = ritz.shape[1] // 4
     half = width // 2
     c = lax.axis_index("col")
-    w = lax.axis_index(WIRE)
     groups = lax.axis_size(WIRE)
     col = jnp.reshape(c, (1,)).astype(jnp.int32)
-    base = (jnp.stack([w, (w + 1) % groups, (w + groups - 1) % groups]) * blk).astype(jnp.int32)
     st = search.T
     cols = block_cols.T
 
     before = shifted(st, "col", 1)
     after = shifted(st, "col", -1)
-    prev2 = shifted(cols, WIRE, 2)
-    next2 = shifted(cols, WIRE, -2)
-    up1 = shifted(st, WIRE, -1)
-    down1 = shifted(st, WIRE, 1)
-
-    packed = call(pack_kernel, [(width, rows // 2)] * 2, [SMEM] * 3 + [VMEM])(base, prev2, next2, st)
-    up2 = shifted(packed[0], WIRE, -2)
-    down2 = shifted(packed[1], WIRE, 2)
+    near = to_sides(st, 1)
+    far = to_sides(st, 2)
+    swap = shifted(st, "core", 1)
+    relay = shifted(near, "core", 1)
 
     opp_a = shifted(before[:half], "col", 1)
     opp_b = shifted(after[half:], "col", -1)
@@ -277,11 +280,10 @@
     grams = [(3, width, width), (1, LANES)] * 2
     gram_specs = [pl.BlockSpec((3, width, width), lambda m: (0, 0, 0)), pl.BlockSpec((1, LANES), lambda m: (0, 0))] * 2
     made = call(
-        image_kernel,
+        functools.partial(image_kernel, blk * groups),
         [(width, rows)] * 2 + grams + [(modes, rows)] * 4,
-        [SMEM] * 3
-        + [whole] * 3
-        + [tile(step_lanes // 2)] * 2
+        [SMEM] * 2
+        + [whole] * 5
         + [pl.BlockSpec((step_lanes, values.shape[1]), lambda m: (m, 0))]
         + [tile(step_lanes)] * 2
         + [VMEM],
@@ -291,7 +293,7 @@
         + [pl.BlockSpec((modes, step_lanes), lambda m: (0, m))] * 4,
         grid=(rows // step_lanes,),
         scratch_shapes=[pltpu.VMEM((3 * width, LANES), F32)] * 2 + [pltpu.VMEM((4 * modes, width), F32)],
-    )(col, base, cols, st, up1, down1, up2, down2, values, before, after, ritz)
+    )(col, cols, st, swap, near, relay, far, values, before, after, ritz)
     image, grams, (part_own, part_after, part_opp, part_before) = made[:2], made[2:6], made[6:]
 
     payload, terms = call(

time: 131 us -> 123 us (0.939)
  waiting for transfers between devices: 40.3 us -> 25.9 us
  starting transfers between devices: 44.2 us -> 51.7 us
  blocking collectives: 12 us -> 14.3 us
  Pallas kernels: 26.3 us -> 24.1 us
    ppermute x16 -> x12, waiting for transfers between devices: 38.7 us -> 19.9 us  [shifted(): lax.ppermute(array, axis, [(i, (i + by) % length) for i in range(length)])]
    ppermute x0 -> x2, waiting for transfers between devices: none -> 5.91 us  [to_sides(): return lax.ppermute(array, WIRE, pairs)]
    ppermute x16 -> x12, starting transfers between devices: 31.8 us -> 35.4 us  [shifted(): lax.ppermute(array, axis, [(i, (i + by) % length) for i in range(length)])]
    ppermute x0 -> x2, starting transfers between devices: none -> 3.22 us  [to_sides(): return lax.ppermute(array, WIRE, pairs)]
    all_to_all x1, blocking collectives: 12 us -> 14.3 us  [shards(): part = lax.all_to_all(part, 'zh', 0, 0, tiled=True)]
    pallas_call x2 -> x1, Pallas kernels: 15.3 us -> 13.2 us  [shards(): call(functools.partial(image_kernel, blk * groups), [(width, rows)] * 2 +...]
    all_to_all x1, starting transfers between devices: 7 us -> 8.6 us  [shards(): parts = lax.all_to_all(spread_out(part), RING, 0, 0, tiled=True)]
    all_to_all x1, waiting for transfers between devices: 1.54 us -> 0.16 us  [shards(): got = lax.all_to_all(payload, RING, 0, 0, tiled=True)]
  transfers between devices with their start and end apart: 18 -> 16, of which waited for: 9 -> 7; matrix products, arithmetic and copies ran while one was open for 2% -> 2% of each run, Pallas kernels for 15% -> 15%
where the time goes in v6:
time: 123 us
  starting transfers between devices  51.7 us (42%)
  waiting for transfers between devices  25.9 us (21%)
  Pallas kernels  24.1 us (20%)
  blocking collectives  14.3 us (12%)
  local copies, waits for them, and re-layouts  5.15 us (4%)
    ppermute x12, starting transfers between devices, shifted(): lax.ppermute(array, axis, [(i, (i + by) % length) for i in range(length)])  35.4 us
    ppermute x12, waiting for transfers between devices, shifted(): lax.ppermute(array, axis, [(i, (i + by) % length) for i in range(length)])  19.9 us
    all_to_all x1, blocking collectives, shards(): part = lax.all_to_all(part, 'zh', 0, 0, tiled=True)  14.3 us
    pallas_call x1, Pallas kernels, shards(): call(functools.partial(image_kernel, blk * groups), [(width, rows)] * 2 +...  13.2 us
    all_to_all x1, starting transfers between devices, shards(): parts = lax.all_to_all(spread_out(part), RING, 0, 0, tiled=True)  8.6 us
    ppermute x2, waiting for transfers between devices, to_sides(): return lax.ppermute(array, WIRE, pairs)  5.91 us
    pallas_call x1, Pallas kernels, shards(): call(modes_kernel, [(modes, rows)] * 2, [SMEM] + [VMEM] * 10, scratch_sha...  4.75 us
    all_to_all x1, starting transfers between devices, shards(): got = lax.all_to_all(payload, RING, 0, 0, tiled=True)  4.49 us
  transfers between devices with their start and end apart: 16, of which 7 were waited for; matrix products, arithmetic and copies ran while one was open for 2% of the time, Pallas kernels for 15%

profile of v6, /device:TPU:1, one launch (start us, length us, event | category | flops | bytes accessed | tf_op | source)
XLA Modules:
  0.0 122.7 jit_solution(2669548272807337434)
XLA Ops:
  0.6 2.8 %collective-permute-start.5 = (f32[96,3072]{1,0:T(8,128)}, f32[96,3072]{1,0:T(8,128)}, u32[]{:S(2)}, u32[]{:S(2)}) collective-permute-start(f32[96,3072]{1,0:T(8,128)} %bitcast.8), channel_id=1, source_target_pairs={{252,0},{8,4},{4,8},{16,12},{12,16},{24,20},{20,24},{32,28},{28,32... | collective-permute-start | bytes 3538952 | tf_op jit(solution)/shard_map/ppermute | solution.py:33
  3.4 1.2 collective-permute-start
  4.6 1.5 %collective-permute-start.1 = (f32[96,3072]{1,0:T(8,128)}, f32[96,3072]{1,0:T(8,128)S(1)}, u32[]{:S(2)}, u32[]{:S(2)}) collective-permute-start(f32[96,3072]{1,0:T(8,128)} %bitcast.10), channel_id=1, source_target_pairs={{0,3},{1,0},{2,1},{3,2},{4,7},{5,4},{6,5},{7,6},{8,11},{9,8},{10,9... | collective-permute-start | bytes 3538952 | tf_op jit(solution)/shard_map/ppermute | solution.py:27
  6.1 7.1 %collective-permute-start.4 = (f32[96,3072]{1,0:T(8,128)}, f32[96,3072]{1,0:T(8,128)}, u32[]{:S(2)}, u32[]{:S(2)}) collective-permute-start(f32[96,3072]{1,0:T(8,128)} %bitcast.11), channel_id=1, source_target_pairs={{0,4},{4,0},{1,5},{5,1},{2,6},{6,2},{3,7},{7,3},{8,12},{12,8},{9,1... | collective-permute-start | bytes 3538952 | tf_op jit(solution)/shard_map/ppermute | solution.py:27
  13.7 5.9 %collective-permute-done.5.near = f32[96,3072]{1,0:T(8,128)} collective-permute-done((f32[96,3072]{1,0:T(8,128)}, f32[96,3072]{1,0:T(8,128)}, u32[]{:S(2)}, u32[]{:S(2)}) %collective-permute-start.5) | collective-permute-done | bytes 1179680 | tf_op jit(solution)/shard_map/ppermute | solution.py:33
  19.6 13.5 %collective-permute-start.6 = (f32[96,3072]{1,0:T(8,128)}, f32[96,3072]{1,0:T(8,128)}, u32[]{:S(2)}, u32[]{:S(2)}) collective-permute-start(f32[96,3072]{1,0:T(8,128)} %collective-permute-done.5.near), channel_id=1, source_target_pairs={{0,4},{4,0},{1,5},{5,1},{2,6},{6,2},{3,7},{7,3},{8,12},{12,8},{9,1... | collective-permute-start | bytes 3538952 | tf_op jit(solution)/shard_map/ppermute | solution.py:27
  33.1 1.0 slice.8
  34.1 2.4 %collective-permute-start.2 = (f32[48,3072]{1,0:T(8,128)}, f32[48,3072]{1,0:T(8,128)S(1)}, u32[]{:S(2)}, u32[]{:S(2)}) collective-permute-start(f32[48,3072]{1,0:T(8,128)} %slice.8), channel_id=1, source_target_pairs={{0,1},{1,2},{2,3},{3,0},{4,5},{5,6},{6,7},{7,4},{8,9},{9,10},{10,1... | collective-permute-start | bytes 1769480 | tf_op jit(solution)/shard_map/ppermute | solution.py:27
  36.5 0.9 slice.9
  37.4 1.3 %collective-permute-start.3 = (f32[48,3072]{1,0:T(8,128)}, f32[48,3072]{1,0:T(8,128)S(1)}, u32[]{:S(2)}, u32[]{:S(2)}) collective-permute-start(f32[48,3072]{1,0:T(8,128)} %slice.9), channel_id=1, source_target_pairs={{0,3},{1,0},{2,1},{3,2},{4,7},{5,4},{6,5},{7,6},{8,11},{9,8},{10,9... | collective-permute-start | bytes 1769480 | tf_op jit(solution)/shard_map/ppermute | solution.py:27
  38.7 13.2 %shard_map.83 = (bf16[96,3072]{1,0:T(8,128)(2,1)}, bf16[96,3072]{1,0:T(8,128)(2,1)}, f32[3,96,96]{2,1,0:T(8,128)}, f32[1,128]{1,0:T(1,128)}, f32[3,96,96]{2,1,0:...) custom-call(s32[1]{0:T(128)} %bitcast.col, ...), custom_call_target="tpu_custom_call" | custom-call | tf_op jit(solution)/shard_map/pallas_call | solution.py:282
  52.2 0.6 copy-done.2
  53.1 4.0 %shard_map.85 = (f32[16,40,128]{2,1,0:T(8,128)}, f32[8,128]{1,0:T(8,128)}) custom-call(s32[1]{0:T(128)} %bitcast.col, f32[3,96,96]{2,1,0:T(8,128)} %get-tuple-element.28.stiff3, f32[1,128]{1,0:T(1,128)} %get-tuple-element.29.stiff_terms, f32[3,96,96]{2,1,0:T(8,128)} %get-tuple-element.30.mass3, f32[1,128]{1,0:T(1,128)} %get-tuple-element.31.mass_terms, ...), custom_call_target="tpu_custom_call" | custom-call | tf_op jit(solution)/shard_map/pallas_call | solution.py:299
  57.1 4.5 %all-to-all-start = ((f32[16,40,128]{2,1,0:T(8,128)}), f32[16,40,128]{2,1,0:T(8,128)S(1)}, u32[]{:S(2)}, u32[]{:S(2)}) async-start(f32[16,40,128]{2,1,0:T(8,128)} %get-tuple-element.34), calls=%async_computation | async-start | bytes 655360 | tf_op jit(solution)/shard_map/all_to_all | solution.py:306
  61.6 1.3 %collective-permute-start.11 = (f32[8,128]{1,0:T(8,128)}, f32[8,128]{1,0:T(8,128)S(1)}, u32[]{:S(2)}, u32[]{:S(2)}) collective-permute-start(f32[8,128]{1,0:T(8,128)} %get-tuple-element.35), channel_id=1, source_target_pairs={{0,1},{1,2},{2,3},{3,0},{4,5},{5,6},{6,7},{7,4},{8,9},{9,10},{10,1... | collective-permute-start | bytes 12296 | tf_op jit(solution)/shard_map/ppermute | solution.py:27
  62.9 2.7 %collective-permute-start.12 = (f32[8,128]{1,0:T(8,128)}, f32[8,128]{1,0:T(8,128)S(1)}, u32[]{:S(2)}, u32[]{:S(2)}) collective-permute-start(f32[8,128]{1,0:T(8,128)} %get-tuple-element.35), channel_id=1, source_target_pairs={{0,2},{1,3},{2,0},{3,1},{4,6},{5,7},{6,4},{7,5},{8,10},{9,11},{10,... | collective-permute-start | bytes 12296 | tf_op jit(solution)/shard_map/ppermute | solution.py:27
  65.6 0.6 collective-permute-start.13
  66.2 1.2 collective-permute-done.12
  67.4 1.1 collective-permute-done.13
  68.5 0.7 add_add_fusion
  69.4 14.3 %all_to_all.15 = f32[4,48,128]{2,1,0:T(8,128)S(1)} all-to-all(f32[4,48,128]{2,1,0:T(8,128)S(1)} %broadcast_in_dim.4), channel_id=1, replica_groups=mesh['zh'=4,'zl'=2,'y'=4,'core'=2,'col'=4] {'zh'}, dimensions={0} | all-to-all | bytes 196608 | tf_op jit(solution)/shard_map/all_to_all | solution.py:322
  83.7 0.8 broadcast_in_dim.5
  84.5 8.6 %all-to-all-start.2 = ((f32[16,48,128]{2,1,0:T(8,128)}), f32[16,48,128]{2,1,0:T(8,128)S(1)}, u32[]{:S(2)}, u32[]{:S(2)}) async-start(f32[16,48,128]{2,1,0:T(8,128)} %broadcast_in_dim.5), calls=%async_computation.2 | async-start | bytes 786432 | tf_op jit(solution)/shard_map/all_to_all | solution.py:324
  93.1 1.1 collective-permute-start.10
  94.2 0.6 collective-permute-start.8
  94.7 2.1 %collective-permute-start.9 = (f32[32,3072]{1,0:T(8,128)S(1)}, f32[32,3072]{1,0:T(8,128)S(1)}, u32[]{:S(2)}, u32[]{:S(2)}) collective-permute-start(f32[32,3072]{1,0:T(8,128)S(1)} %copy-done.8), channel_id=1, source_target_pairs={{0,3},{1,0},{2,1},{3,2},{4,7},{5,4},{6,5},{7,6},{8,11},{9,8},{10,9... | collective-permute-start | bytes 1179656 | tf_op jit(solution)/shard_map/ppermute | solution.py:27
  96.8 8.5 %collective-permute-done.10.from_opp = f32[32,3072]{1,0:T(8,128)S(1)} collective-permute-done((f32[32,3072]{1,0:T(8,128)S(1)}, f32[32,3072]{1,0:T(8,128)S(1)}, u32[]{:S(2)}, u32[]{:S(2)}) %collective-permute-start.10) | collective-permute-done | bytes 393248 | tf_op jit(solution)/shard_map/ppermute | solution.py:27
  105.3 8.9 %collective-permute-done.8.from_prev = f32[32,3072]{1,0:T(8,128)S(1)} collective-permute-done((f32[32,3072]{1,0:T(8,128)S(1)}, f32[32,3072]{1,0:T(8,128)S(1)}, u32[]{:S(2)}, u32[]{:S(2)}) %collective-permute-start.8) | collective-permute-done | bytes 393248 | tf_op jit(solution)/shard_map/ppermute | solution.py:27
  114.2 0.7 copy-done.6
  115.0 4.7 %shard_map.84 = (f32[32,3072]{1,0:T(8,128)}, f32[32,3072]{1,0:T(8,128)}) custom-call(s32[1]{0:T(128)} %bitcast.col, f32[96,3072]{1,0:T(8,128)} %bitcast.15, f32[96,3072]{1,0:T(8,128)} %copy-done, f32[96,3072]{1,0:T(8,128)} %copy-done.1, f32[48,3072]{1,0:T(8,128)} %copy-done.2, f32[48,3072]{1,0:T(8,128)} %copy-done.3, f32[384,128]{1,0:T(8,128)} %ritz.5, ...), custom_call_target="tpu_custom_call" | custom-call | tf_op jit(solution)/shard_map/pallas_call | solution.py:311
  119.8 0.7 copy-done.4
  120.5 2.1 %shard_map.86 = (f32[96,384]{1,0:T(8,128)}, f32[96,384]{1,0:T(8,128)}, f32[1,32]{1,0:T(1,128)}, f32[32,3072]{1,0:T(8,128)}) custom-call(s32[1]{0:T(128)} %bitcast.col, f32[16,48,128]{2,1,0:T(8,128)} %copy-done.4, f32[32,3072]{1,0:T(8,128)} %get-tuple-element.27.modes, f32[32,3072]{1,0:T(8,128)} %get-tuple-element.36.image), custom_call_target="tpu_custom_call" | custom-call | tf_op jit(solution)/shard_map/pallas_call | solution.py:326
  (35 shorter events, 1.3 us)
Async XLA Ops:
  0.6 18.9 %collective-permute-start.5 = (f32[96,3072]{1,0:T(8,128)}, f32[96,3072]{1,0:T(8,128)}, u32[]{:S(2)}, u32[]{:S(2)}) collective-permute-start(f32[96,3072]{1,0:T(8,128)} %bitcast.8), channel_id=1, source_target_pairs={{252,0},{8,4},{4,8},{16,12},{12,16},{24,20},{20,24},{32,28},{28,32... | collective-permute-start | bytes 3538952 | tf_op jit(solution)/shard_map/ppermute | solution.py:33
  3.4 29.7 %collective-permute-start = (f32[96,3072]{1,0:T(8,128)}, f32[96,3072]{1,0:T(8,128)S(1)}, u32[]{:S(2)}, u32[]{:S(2)}) collective-permute-start(f32[96,3072]{1,0:T(8,128)} %bitcast.9), channel_id=1, source_target_pairs={{0,1},{1,2},{2,3},{3,0},{4,5},{5,6},{6,7},{7,4},{8,9},{9,10},{10,1... | collective-permute-start | bytes 3538952 | tf_op jit(solution)/shard_map/ppermute | solution.py:27
  4.6 31.9 %collective-permute-start.1 = (f32[96,3072]{1,0:T(8,128)}, f32[96,3072]{1,0:T(8,128)S(1)}, u32[]{:S(2)}, u32[]{:S(2)}) collective-permute-start(f32[96,3072]{1,0:T(8,128)} %bitcast.10), channel_id=1, source_target_pairs={{0,3},{1,0},{2,1},{3,2},{4,7},{5,4},{6,5},{7,6},{8,11},{9,8},{10,9... | collective-permute-start | bytes 3538952 | tf_op jit(solution)/shard_map/ppermute | solution.py:27
  6.1 32.7 %collective-permute-start.4 = (f32[96,3072]{1,0:T(8,128)}, f32[96,3072]{1,0:T(8,128)}, u32[]{:S(2)}, u32[]{:S(2)}) collective-permute-start(f32[96,3072]{1,0:T(8,128)} %bitcast.11), channel_id=1, source_target_pairs={{0,4},{4,0},{1,5},{5,1},{2,6},{6,2},{3,7},{7,3},{8,12},{12,8},{9,1... | collective-permute-start | bytes 3538952 | tf_op jit(solution)/shard_map/ppermute | solution.py:27
  13.2 25.5 %collective-permute-start.7 = (f32[96,3072]{1,0:T(8,128)}, f32[96,3072]{1,0:T(8,128)}, u32[]{:S(2)}, u32[]{:S(2)}) collective-permute-start(f32[96,3072]{1,0:T(8,128)} %bitcast.12), channel_id=1, source_target_pairs={{248,0},{12,4},{0,8},{20,12},{8,16},{28,20},{16,24},{36,28},{24,32... | collective-permute-start | bytes 3538952 | tf_op jit(solution)/shard_map/ppermute | solution.py:33
  19.6 19.2 %collective-permute-start.6 = (f32[96,3072]{1,0:T(8,128)}, f32[96,3072]{1,0:T(8,128)}, u32[]{:S(2)}, u32[]{:S(2)}) collective-permute-start(f32[96,3072]{1,0:T(8,128)} %collective-permute-done.5.near), channel_id=1, source_target_pairs={{0,4},{4,0},{1,5},{5,1},{2,6},{6,2},{3,7},{7,3},{8,12},{12,8},{9,1... | collective-permute-start | bytes 3538952 | tf_op jit(solution)/shard_map/ppermute | solution.py:27
  33.1 4.3 %copy-start = (f32[96,3072]{1,0:T(8,128)}, f32[96,3072]{1,0:T(8,128)S(1)}, u32[]{:S(2)}) copy-start(f32[96,3072]{1,0:T(8,128)S(1)} %collective-permute-done.before) | copy-start | bytes 3538948
  34.1 17.9 %collective-permute-start.2 = (f32[48,3072]{1,0:T(8,128)}, f32[48,3072]{1,0:T(8,128)S(1)}, u32[]{:S(2)}, u32[]{:S(2)}) collective-permute-start(f32[48,3072]{1,0:T(8,128)} %slice.8), channel_id=1, source_target_pairs={{0,1},{1,2},{2,3},{3,0},{4,5},{5,6},{6,7},{7,4},{8,9},{9,10},{10,1... | collective-permute-start | bytes 1769480 | tf_op jit(solution)/shard_map/ppermute | solution.py:27
  36.5 2.2 %copy-start.1 = (f32[96,3072]{1,0:T(8,128)}, f32[96,3072]{1,0:T(8,128)S(1)}, u32[]{:S(2)}) copy-start(f32[96,3072]{1,0:T(8,128)S(1)} %collective-permute-done.1.after) | copy-start | bytes 3538948
  37.4 14.8 %collective-permute-start.3 = (f32[48,3072]{1,0:T(8,128)}, f32[48,3072]{1,0:T(8,128)S(1)}, u32[]{:S(2)}, u32[]{:S(2)}) collective-permute-start(f32[48,3072]{1,0:T(8,128)} %slice.9), channel_id=1, source_target_pairs={{0,3},{1,0},{2,1},{3,2},{4,7},{5,4},{6,5},{7,6},{8,11},{9,8},{10,9... | collective-permute-start | bytes 1769480 | tf_op jit(solution)/shard_map/ppermute | solution.py:27
  52.0 0.8 copy-start.2
  52.2 0.8 copy-start.3
  57.1 12.2 %all-to-all-start = ((f32[16,40,128]{2,1,0:T(8,128)}), f32[16,40,128]{2,1,0:T(8,128)S(1)}, u32[]{:S(2)}, u32[]{:S(2)}) async-start(f32[16,40,128]{2,1,0:T(8,128)} %get-tuple-element.34), calls=%async_computation | async-start | bytes 655360 | tf_op jit(solution)/shard_map/all_to_all | solution.py:306
  61.6 31.5 %copy-start.10 = (f32[32,3072]{1,0:T(8,128)S(1)}, f32[32,3072]{1,0:T(8,128)}, u32[]{:S(2)}) copy-start(f32[32,3072]{1,0:T(8,128)} %get-tuple-element.26) | copy-start | bytes 1179652
  61.6 32.6 %copy-start.9 = (f32[32,3072]{1,0:T(8,128)S(1)}, f32[32,3072]{1,0:T(8,128)}, u32[]{:S(2)}) copy-start(f32[32,3072]{1,0:T(8,128)} %get-tuple-element.24) | copy-start | bytes 1179652
  61.6 33.1 %copy-start.8 = (f32[32,3072]{1,0:T(8,128)S(1)}, f32[32,3072]{1,0:T(8,128)}, u32[]{:S(2)}) copy-start(f32[32,3072]{1,0:T(8,128)} %get-tuple-element.25) | copy-start | bytes 1179652
  61.6 4.6 %collective-permute-start.11 = (f32[8,128]{1,0:T(8,128)}, f32[8,128]{1,0:T(8,128)S(1)}, u32[]{:S(2)}, u32[]{:S(2)}) collective-permute-start(f32[8,128]{1,0:T(8,128)} %get-tuple-element.35), channel_id=1, source_target_pairs={{0,1},{1,2},{2,3},{3,0},{4,5},{5,6},{6,7},{7,4},{8,9},{9,10},{10,1... | collective-permute-start | bytes 12296 | tf_op jit(solution)/shard_map/ppermute | solution.py:27
  62.9 4.5 %collective-permute-start.12 = (f32[8,128]{1,0:T(8,128)}, f32[8,128]{1,0:T(8,128)S(1)}, u32[]{:S(2)}, u32[]{:S(2)}) collective-permute-start(f32[8,128]{1,0:T(8,128)} %get-tuple-element.35), channel_id=1, source_target_pairs={{0,2},{1,3},{2,0},{3,1},{4,6},{5,7},{6,4},{7,5},{8,10},{9,11},{10,... | collective-permute-start | bytes 12296 | tf_op jit(solution)/shard_map/ppermute | solution.py:27
  65.6 2.9 %collective-permute-start.13 = (f32[8,128]{1,0:T(8,128)}, f32[8,128]{1,0:T(8,128)S(1)}, u32[]{:S(2)}, u32[]{:S(2)}) collective-permute-start(f32[8,128]{1,0:T(8,128)} %get-tuple-element.35), channel_id=1, source_target_pairs={{0,3},{1,0},{2,1},{3,2},{4,7},{5,4},{6,5},{7,6},{8,11},{9,8},{10,9... | collective-permute-start | bytes 12296 | tf_op jit(solution)/shard_map/ppermute | solution.py:27
  84.5 35.3 %all-to-all-start.2 = ((f32[16,48,128]{2,1,0:T(8,128)}), f32[16,48,128]{2,1,0:T(8,128)S(1)}, u32[]{:S(2)}, u32[]{:S(2)}) async-start(f32[16,48,128]{2,1,0:T(8,128)} %broadcast_in_dim.5), calls=%async_computation.2 | async-start | bytes 786432 | tf_op jit(solution)/shard_map/all_to_all | solution.py:324
  93.1 12.2 %collective-permute-start.10 = (f32[32,3072]{1,0:T(8,128)S(1)}, f32[32,3072]{1,0:T(8,128)S(1)}, u32[]{:S(2)}, u32[]{:S(2)}) collective-permute-start(f32[32,3072]{1,0:T(8,128)S(1)} %copy-done.10), channel_id=1, source_target_pairs={{0,2},{1,3},{2,0},{3,1},{4,6},{5,7},{6,4},{7,5},{8,10},{9,11},{10,... | collective-permute-start | bytes 1179656 | tf_op jit(solution)/shard_map/ppermute | solution.py:27
  94.2 20.0 %collective-permute-start.8 = (f32[32,3072]{1,0:T(8,128)S(1)}, f32[32,3072]{1,0:T(8,128)S(1)}, u32[]{:S(2)}, u32[]{:S(2)}) collective-permute-start(f32[32,3072]{1,0:T(8,128)S(1)} %copy-done.9), channel_id=1, source_target_pairs={{0,1},{1,2},{2,3},{3,0},{4,5},{5,6},{6,7},{7,4},{8,9},{9,10},{10,1... | collective-permute-start | bytes 1179656 | tf_op jit(solution)/shard_map/ppermute | solution.py:27
  94.7 19.4 %collective-permute-start.9 = (f32[32,3072]{1,0:T(8,128)S(1)}, f32[32,3072]{1,0:T(8,128)S(1)}, u32[]{:S(2)}, u32[]{:S(2)}) collective-permute-start(f32[32,3072]{1,0:T(8,128)S(1)} %copy-done.8), channel_id=1, source_target_pairs={{0,3},{1,0},{2,1},{3,2},{4,7},{5,4},{6,5},{7,6},{8,11},{9,8},{10,9... | collective-permute-start | bytes 1179656 | tf_op jit(solution)/shard_map/ppermute | solution.py:27
  105.3 8.9 %copy-start.5 = (f32[32,3072]{1,0:T(8,128)}, f32[32,3072]{1,0:T(8,128)S(1)}, u32[]{:S(2)}) copy-start(f32[32,3072]{1,0:T(8,128)S(1)} %collective-permute-done.10.from_opp) | copy-start | bytes 1179652
  114.2 0.8 copy-start.6
  114.2 0.9 copy-start.7
  119.8 0.7 copy-start.4

commit v7 on v6

--- a/solution.py
+++ b/solution.py
@@ -20,6 +20,7 @@
 NT = (((1,), (1,)), ((), ()))
 VMEM = pl.BlockSpec(memory_space=pltpu.VMEM)
 SMEM = pl.BlockSpec(memory_space=pltpu.SMEM)
+HBM = pl.BlockSpec(memory_space=pltpu.HBM)
 
 
 def shifted(array, axis, by):
@@ -83,7 +84,7 @@
 def image_kernel(
     count, col, cols, st, swap, near, relay, far, values, before, after, ritz,
     image_high, image_low, stiff, stiff_terms, mass, mass_terms,
-    part_own, part_after, part_opp, part_before, stiff_sum, mass_sum, turned
+    part_own, part_after, part_opp, part_before, stiff_sum, mass_sum, turned, beside, sems
 ):
     m = pl.program_id(0)
     width = st.shape[0]
@@ -93,14 +94,23 @@
     images, owns = [], []
     blk = cols.shape[1]
     here = cols[0, 0]
-    even = here // blk % 2 == 0
     starts = [group_start(here, by, blk, count) for by in (1, 2, -1, -2)]
-    sources = ((swap, near), (relay, far), (near, swap), (far, relay))
 
     @pl.when(m == 0)
     def _():
         stiff_sum[...] = jnp.zeros_like(stiff_sum)
         mass_sum[...] = jnp.zeros_like(mass_sum)
+        odd = here // blk % 2
+        copies = [
+            pltpu.make_async_copy(source, beside.at[slot], sems.at[i])
+            for i, (source, slot) in enumerate(
+                ((swap, 2 * odd), (near, 2 - 2 * odd), (relay, 1 + 2 * odd), (far, 3 - 2 * odd))
+            )
+        ]
+        for copy in copies:
+            copy.start()
+        for copy in copies:
+            copy.wait()
         turned[...] = ritz[pl.ds(pl.multiple_of(col[0] * width, 8), width), :].T
 
     modes = part_own.shape[0]
@@ -122,8 +132,7 @@
             beyond = []
             for slot in range(2):
                 index = cols[2 + slot, row] - starts[2 * q + slot]
-                one, two = (tile_at(ref, index) for ref in sources[2 * q + slot])
-                beyond.append(in_half(jnp.where(even, one, two), index, slot))
+                beyond.append(in_half(tile_at(beside.at[2 * q + slot], index), index, slot))
             left.append(jnp.concatenate([first, jnp.where(left_half, *beyond)], axis=1))
             coef = values[(2 * h + q) * BLOCK : (2 * h + q + 1) * BLOCK, :]
             if q:
@@ -283,7 +292,8 @@
         functools.partial(image_kernel, blk * groups),
         [(width, rows)] * 2 + grams + [(modes, rows)] * 4,
         [SMEM] * 2
-        + [whole] * 5
+        + [whole]
+        + [HBM] * 4
         + [pl.BlockSpec((step_lanes, values.shape[1]), lambda m: (m, 0))]
         + [tile(step_lanes)] * 2
         + [VMEM],
@@ -292,7 +302,12 @@
         + gram_specs
         + [pl.BlockSpec((modes, step_lanes), lambda m: (0, m))] * 4,
         grid=(rows // step_lanes,),
-        scratch_shapes=[pltpu.VMEM((3 * width, LANES), F32)] * 2 + [pltpu.VMEM((4 * modes, width), F32)],
+        scratch_shapes=[pltpu.VMEM((3 * width, LANES), F32)] * 2
+        + [
+            pltpu.VMEM((4 * modes, width), F32),
+            pltpu.VMEM((4, width, rows), F32),
+            pltpu.SemaphoreType.DMA((4,)),
+        ],
     )(col, cols, st, swap, near, relay, far, values, before, after, ritz)
     image, grams, (part_own, part_after, part_opp, part_before) = made[:2], made[2:6], made[6:]
 

time: 123 us -> 123 us (level)
  no operation moved by 1% of the time
where the time goes in v7:
time: 123 us
  starting transfers between devices  50.6 us (41%)
  waiting for transfers between devices  26.2 us (21%)
  Pallas kernels  24.8 us (20%)
  blocking collectives  14.3 us (12%)
  local copies, waits for them, and re-layouts  5.32 us (4%)
    ppermute x12, starting transfers between devices, shifted(): lax.ppermute(array, axis, [(i, (i + by) % length) for i in range(length)])  34.8 us
    ppermute x12, waiting for transfers between devices, shifted(): lax.ppermute(array, axis, [(i, (i + by) % length) for i in range(length)])  19.7 us
    all_to_all x1, blocking collectives, shards(): part = lax.all_to_all(part, 'zh', 0, 0, tiled=True)  14.3 us
    pallas_call x1, Pallas kernels, shards(): call(functools.partial(image_kernel, blk * groups), [(width, rows)] * 2 +...  13.9 us
    all_to_all x1, starting transfers between devices, shards(): parts = lax.all_to_all(spread_out(part), RING, 0, 0, tiled=True)  8.1 us
    ppermute x2, waiting for transfers between devices, to_sides(): return lax.ppermute(array, WIRE, pairs)  5.91 us
    pallas_call x1, Pallas kernels, shards(): call(modes_kernel, [(modes, rows)] * 2, [SMEM] + [VMEM] * 10, scratch_sha...  4.75 us
    all_to_all x1, starting transfers between devices, shards(): got = lax.all_to_all(payload, RING, 0, 0, tiled=True)  4.48 us
  transfers between devices with their start and end apart: 16, of which 7 were waited for; matrix products, arithmetic and copies ran while one was open for 2% of the time, Pallas kernels for 15%

profile of v7, /device:TPU:1, one launch (start us, length us, event | category | flops | bytes accessed | tf_op | source)
XLA Modules:
  0.0 122.7 jit_solution(1041697330297842777)
XLA Ops:
  0.6 2.8 %collective-permute-start.5 = (f32[96,3072]{1,0:T(8,128)}, f32[96,3072]{1,0:T(8,128)}, u32[]{:S(2)}, u32[]{:S(2)}) collective-permute-start(f32[96,3072]{1,0:T(8,128)} %bitcast.8), channel_id=1, source_target_pairs={{252,0},{8,4},{4,8},{16,12},{12,16},{24,20},{20,24},{32,28},{28,32... | collective-permute-start | bytes 3538952 | tf_op jit(solution)/shard_map/ppermute | solution.py:34
  3.4 1.2 collective-permute-start
  4.6 1.5 %collective-permute-start.1 = (f32[96,3072]{1,0:T(8,128)}, f32[96,3072]{1,0:T(8,128)S(1)}, u32[]{:S(2)}, u32[]{:S(2)}) collective-permute-start(f32[96,3072]{1,0:T(8,128)} %bitcast.10), channel_id=1, source_target_pairs={{0,3},{1,0},{2,1},{3,2},{4,7},{5,4},{6,5},{7,6},{8,11},{9,8},{10,9... | collective-permute-start | bytes 3538952 | tf_op jit(solution)/shard_map/ppermute | solution.py:28
  6.1 7.1 %collective-permute-start.4 = (f32[96,3072]{1,0:T(8,128)}, f32[96,3072]{1,0:T(8,128)}, u32[]{:S(2)}, u32[]{:S(2)}) collective-permute-start(f32[96,3072]{1,0:T(8,128)} %bitcast.11), channel_id=1, source_target_pairs={{0,4},{4,0},{1,5},{5,1},{2,6},{6,2},{3,7},{7,3},{8,12},{12,8},{9,1... | collective-permute-start | bytes 3538952 | tf_op jit(solution)/shard_map/ppermute | solution.py:28
  13.7 5.9 %collective-permute-done.5.near = f32[96,3072]{1,0:T(8,128)} collective-permute-done((f32[96,3072]{1,0:T(8,128)}, f32[96,3072]{1,0:T(8,128)}, u32[]{:S(2)}, u32[]{:S(2)}) %collective-permute-start.5) | collective-permute-done | bytes 1179680 | tf_op jit(solution)/shard_map/ppermute | solution.py:34
  19.6 13.5 %collective-permute-start.6 = (f32[96,3072]{1,0:T(8,128)}, f32[96,3072]{1,0:T(8,128)}, u32[]{:S(2)}, u32[]{:S(2)}) collective-permute-start(f32[96,3072]{1,0:T(8,128)} %collective-permute-done.5.near), channel_id=1, source_target_pairs={{0,4},{4,0},{1,5},{5,1},{2,6},{6,2},{3,7},{7,3},{8,12},{12,8},{9,1... | collective-permute-start | bytes 3538952 | tf_op jit(solution)/shard_map/ppermute | solution.py:28
  33.1 1.0 slice.8
  34.1 2.4 %collective-permute-start.2 = (f32[48,3072]{1,0:T(8,128)}, f32[48,3072]{1,0:T(8,128)S(1)}, u32[]{:S(2)}, u32[]{:S(2)}) collective-permute-start(f32[48,3072]{1,0:T(8,128)} %slice.8), channel_id=1, source_target_pairs={{0,1},{1,2},{2,3},{3,0},{4,5},{5,6},{6,7},{7,4},{8,9},{9,10},{10,1... | collective-permute-start | bytes 1769480 | tf_op jit(solution)/shard_map/ppermute | solution.py:28
  36.5 0.9 slice.9
  37.4 1.3 %collective-permute-start.3 = (f32[48,3072]{1,0:T(8,128)}, f32[48,3072]{1,0:T(8,128)S(1)}, u32[]{:S(2)}, u32[]{:S(2)}) collective-permute-start(f32[48,3072]{1,0:T(8,128)} %slice.9), channel_id=1, source_target_pairs={{0,3},{1,0},{2,1},{3,2},{4,7},{5,4},{6,5},{7,6},{8,11},{9,8},{10,9... | collective-permute-start | bytes 1769480 | tf_op jit(solution)/shard_map/ppermute | solution.py:28
  38.7 13.9 %shard_map.83 = (bf16[96,3072]{1,0:T(8,128)(2,1)}, bf16[96,3072]{1,0:T(8,128)(2,1)}, f32[3,96,96]{2,1,0:T(8,128)}, f32[1,128]{1,0:T(1,128)}, f32[3,96,96]{2,1,0:...) custom-call(s32[1]{0:T(128)} %bitcast.col, ...), custom_call_target="tpu_custom_call" | custom-call | tf_op jit(solution)/shard_map/pallas_call | solution.py:291
  52.7 0.8 copy-done.2
  53.7 4.0 %shard_map.85 = (f32[16,40,128]{2,1,0:T(8,128)}, f32[8,128]{1,0:T(8,128)}) custom-call(s32[1]{0:T(128)} %bitcast.col, f32[3,96,96]{2,1,0:T(8,128)} %get-tuple-element.28.stiff3, f32[1,128]{1,0:T(1,128)} %get-tuple-element.29.stiff_terms, f32[3,96,96]{2,1,0:T(8,128)} %get-tuple-element.30.mass3, f32[1,128]{1,0:T(1,128)} %get-tuple-element.31.mass_terms, ...), custom_call_target="tpu_custom_call" | custom-call | tf_op jit(solution)/shard_map/pallas_call | solution.py:314
  57.7 4.5 %all-to-all-start = ((f32[16,40,128]{2,1,0:T(8,128)}), f32[16,40,128]{2,1,0:T(8,128)S(1)}, u32[]{:S(2)}, u32[]{:S(2)}) async-start(f32[16,40,128]{2,1,0:T(8,128)} %get-tuple-element.34), calls=%async_computation | async-start | bytes 655360 | tf_op jit(solution)/shard_map/all_to_all | solution.py:321
  62.2 0.7 collective-permute-start.11
  62.9 2.7 %collective-permute-start.12 = (f32[8,128]{1,0:T(8,128)}, f32[8,128]{1,0:T(8,128)S(1)}, u32[]{:S(2)}, u32[]{:S(2)}) collective-permute-start(f32[8,128]{1,0:T(8,128)} %get-tuple-element.35), channel_id=1, source_target_pairs={{0,2},{1,3},{2,0},{3,1},{4,6},{5,7},{6,4},{7,5},{8,10},{9,11},{10,... | collective-permute-start | bytes 12296 | tf_op jit(solution)/shard_map/ppermute | solution.py:28
  65.6 0.6 collective-permute-start.13
  66.5 0.9 collective-permute-done.12
  67.4 1.2 collective-permute-done.13
  68.6 0.7 add_add_fusion
  69.2 0.6 all-to-all-done
  69.9 14.3 %all_to_all.15 = f32[4,48,128]{2,1,0:T(8,128)S(1)} all-to-all(f32[4,48,128]{2,1,0:T(8,128)S(1)} %broadcast_in_dim.4), channel_id=1, replica_groups=mesh['zh'=4,'zl'=2,'y'=4,'core'=2,'col'=4] {'zh'}, dimensions={0} | all-to-all | bytes 196608 | tf_op jit(solution)/shard_map/all_to_all | solution.py:337
  84.2 0.8 broadcast_in_dim.5
  85.0 8.1 %all-to-all-start.2 = ((f32[16,48,128]{2,1,0:T(8,128)}), f32[16,48,128]{2,1,0:T(8,128)S(1)}, u32[]{:S(2)}, u32[]{:S(2)}) async-start(f32[16,48,128]{2,1,0:T(8,128)} %broadcast_in_dim.5), calls=%async_computation.2 | async-start | bytes 786432 | tf_op jit(solution)/shard_map/all_to_all | solution.py:339
  93.1 1.1 collective-permute-start.10
  94.5 2.4 %collective-permute-start.9 = (f32[32,3072]{1,0:T(8,128)S(1)}, f32[32,3072]{1,0:T(8,128)S(1)}, u32[]{:S(2)}, u32[]{:S(2)}) collective-permute-start(f32[32,3072]{1,0:T(8,128)S(1)} %copy-done.8), channel_id=1, source_target_pairs={{0,3},{1,0},{2,1},{3,2},{4,7},{5,4},{6,5},{7,6},{8,11},{9,8},{10,9... | collective-permute-start | bytes 1179656 | tf_op jit(solution)/shard_map/ppermute | solution.py:28
  96.8 8.5 %collective-permute-done.10.from_opp = f32[32,3072]{1,0:T(8,128)S(1)} collective-permute-done((f32[32,3072]{1,0:T(8,128)S(1)}, f32[32,3072]{1,0:T(8,128)S(1)}, u32[]{:S(2)}, u32[]{:S(2)}) %collective-permute-start.10) | collective-permute-done | bytes 393248 | tf_op jit(solution)/shard_map/ppermute | solution.py:28
  105.3 8.9 %collective-permute-done.8.from_prev = f32[32,3072]{1,0:T(8,128)S(1)} collective-permute-done((f32[32,3072]{1,0:T(8,128)S(1)}, f32[32,3072]{1,0:T(8,128)S(1)}, u32[]{:S(2)}, u32[]{:S(2)}) %collective-permute-start.8) | collective-permute-done | bytes 393248 | tf_op jit(solution)/shard_map/ppermute | solution.py:28
  114.2 0.7 copy-done.6
  115.0 4.7 %shard_map.84 = (f32[32,3072]{1,0:T(8,128)}, f32[32,3072]{1,0:T(8,128)}) custom-call(s32[1]{0:T(128)} %bitcast.col, f32[96,3072]{1,0:T(8,128)} %bitcast.15, f32[96,3072]{1,0:T(8,128)} %copy-done, f32[96,3072]{1,0:T(8,128)} %copy-done.1, f32[48,3072]{1,0:T(8,128)} %copy-done.2, f32[48,3072]{1,0:T(8,128)} %copy-done.3, f32[384,128]{1,0:T(8,128)} %ritz.5, ...), custom_call_target="tpu_custom_call" | custom-call | tf_op jit(solution)/shard_map/pallas_call | solution.py:326
  119.8 0.7 copy-done.4
  120.5 2.1 %shard_map.86 = (f32[96,384]{1,0:T(8,128)}, f32[96,384]{1,0:T(8,128)}, f32[1,32]{1,0:T(1,128)}, f32[32,3072]{1,0:T(8,128)}) custom-call(s32[1]{0:T(128)} %bitcast.col, f32[16,48,128]{2,1,0:T(8,128)} %copy-done.4, f32[32,3072]{1,0:T(8,128)} %get-tuple-element.27.modes, f32[32,3072]{1,0:T(8,128)} %get-tuple-element.36.image), custom_call_target="tpu_custom_call" | custom-call | tf_op jit(solution)/shard_map/pallas_call | solution.py:341
  (35 shorter events, 1.4 us)
Async XLA Ops:
  0.6 18.9 %collective-permute-start.5 = (f32[96,3072]{1,0:T(8,128)}, f32[96,3072]{1,0:T(8,128)}, u32[]{:S(2)}, u32[]{:S(2)}) collective-permute-start(f32[96,3072]{1,0:T(8,128)} %bitcast.8), channel_id=1, source_target_pairs={{252,0},{8,4},{4,8},{16,12},{12,16},{24,20},{20,24},{32,28},{28,32... | collective-permute-start | bytes 3538952 | tf_op jit(solution)/shard_map/ppermute | solution.py:34
  3.4 29.7 %collective-permute-start = (f32[96,3072]{1,0:T(8,128)}, f32[96,3072]{1,0:T(8,128)S(1)}, u32[]{:S(2)}, u32[]{:S(2)}) collective-permute-start(f32[96,3072]{1,0:T(8,128)} %bitcast.9), channel_id=1, source_target_pairs={{0,1},{1,2},{2,3},{3,0},{4,5},{5,6},{6,7},{7,4},{8,9},{9,10},{10,1... | collective-permute-start | bytes 3538952 | tf_op jit(solution)/shard_map/ppermute | solution.py:28
  4.6 31.9 %collective-permute-start.1 = (f32[96,3072]{1,0:T(8,128)}, f32[96,3072]{1,0:T(8,128)S(1)}, u32[]{:S(2)}, u32[]{:S(2)}) collective-permute-start(f32[96,3072]{1,0:T(8,128)} %bitcast.10), channel_id=1, source_target_pairs={{0,3},{1,0},{2,1},{3,2},{4,7},{5,4},{6,5},{7,6},{8,11},{9,8},{10,9... | collective-permute-start | bytes 3538952 | tf_op jit(solution)/shard_map/ppermute | solution.py:28
  6.1 32.7 %collective-permute-start.4 = (f32[96,3072]{1,0:T(8,128)}, f32[96,3072]{1,0:T(8,128)}, u32[]{:S(2)}, u32[]{:S(2)}) collective-permute-start(f32[96,3072]{1,0:T(8,128)} %bitcast.11), channel_id=1, source_target_pairs={{0,4},{4,0},{1,5},{5,1},{2,6},{6,2},{3,7},{7,3},{8,12},{12,8},{9,1... | collective-permute-start | bytes 3538952 | tf_op jit(solution)/shard_map/ppermute | solution.py:28
  13.2 25.5 %collective-permute-start.7 = (f32[96,3072]{1,0:T(8,128)}, f32[96,3072]{1,0:T(8,128)}, u32[]{:S(2)}, u32[]{:S(2)}) collective-permute-start(f32[96,3072]{1,0:T(8,128)} %bitcast.12), channel_id=1, source_target_pairs={{248,0},{12,4},{0,8},{20,12},{8,16},{28,20},{16,24},{36,28},{24,32... | collective-permute-start | bytes 3538952 | tf_op jit(solution)/shard_map/ppermute | solution.py:34
  19.6 19.2 %collective-permute-start.6 = (f32[96,3072]{1,0:T(8,128)}, f32[96,3072]{1,0:T(8,128)}, u32[]{:S(2)}, u32[]{:S(2)}) collective-permute-start(f32[96,3072]{1,0:T(8,128)} %collective-permute-done.5.near), channel_id=1, source_target_pairs={{0,4},{4,0},{1,5},{5,1},{2,6},{6,2},{3,7},{7,3},{8,12},{12,8},{9,1... | collective-permute-start | bytes 3538952 | tf_op jit(solution)/shard_map/ppermute | solution.py:28
  33.1 4.3 %copy-start = (f32[96,3072]{1,0:T(8,128)}, f32[96,3072]{1,0:T(8,128)S(1)}, u32[]{:S(2)}) copy-start(f32[96,3072]{1,0:T(8,128)S(1)} %collective-permute-done.before) | copy-start | bytes 3538948
  34.1 18.6 %collective-permute-start.2 = (f32[48,3072]{1,0:T(8,128)}, f32[48,3072]{1,0:T(8,128)S(1)}, u32[]{:S(2)}, u32[]{:S(2)}) collective-permute-start(f32[48,3072]{1,0:T(8,128)} %slice.8), channel_id=1, source_target_pairs={{0,1},{1,2},{2,3},{3,0},{4,5},{5,6},{6,7},{7,4},{8,9},{9,10},{10,1... | collective-permute-start | bytes 1769480 | tf_op jit(solution)/shard_map/ppermute | solution.py:28
  36.5 2.2 %copy-start.1 = (f32[96,3072]{1,0:T(8,128)}, f32[96,3072]{1,0:T(8,128)S(1)}, u32[]{:S(2)}) copy-start(f32[96,3072]{1,0:T(8,128)S(1)} %collective-permute-done.1.after) | copy-start | bytes 3538948
  37.4 15.2 %collective-permute-start.3 = (f32[48,3072]{1,0:T(8,128)}, f32[48,3072]{1,0:T(8,128)S(1)}, u32[]{:S(2)}, u32[]{:S(2)}) collective-permute-start(f32[48,3072]{1,0:T(8,128)} %slice.9), channel_id=1, source_target_pairs={{0,3},{1,0},{2,1},{3,2},{4,7},{5,4},{6,5},{7,6},{8,11},{9,8},{10,9... | collective-permute-start | bytes 1769480 | tf_op jit(solution)/shard_map/ppermute | solution.py:28
  52.6 0.8 copy-start.2
  52.7 1.0 copy-start.3
  57.7 12.2 %all-to-all-start = ((f32[16,40,128]{2,1,0:T(8,128)}), f32[16,40,128]{2,1,0:T(8,128)S(1)}, u32[]{:S(2)}, u32[]{:S(2)}) async-start(f32[16,40,128]{2,1,0:T(8,128)} %get-tuple-element.34), calls=%async_computation | async-start | bytes 655360 | tf_op jit(solution)/shard_map/all_to_all | solution.py:321
  62.2 30.9 %copy-start.10 = (f32[32,3072]{1,0:T(8,128)S(1)}, f32[32,3072]{1,0:T(8,128)}, u32[]{:S(2)}) copy-start(f32[32,3072]{1,0:T(8,128)} %get-tuple-element.26) | copy-start | bytes 1179652
  62.2 32.0 %copy-start.9 = (f32[32,3072]{1,0:T(8,128)S(1)}, f32[32,3072]{1,0:T(8,128)}, u32[]{:S(2)}) copy-start(f32[32,3072]{1,0:T(8,128)} %get-tuple-element.24) | copy-start | bytes 1179652
  62.2 32.3 %copy-start.8 = (f32[32,3072]{1,0:T(8,128)S(1)}, f32[32,3072]{1,0:T(8,128)}, u32[]{:S(2)}) copy-start(f32[32,3072]{1,0:T(8,128)} %get-tuple-element.25) | copy-start | bytes 1179652
  62.2 4.3 %collective-permute-start.11 = (f32[8,128]{1,0:T(8,128)}, f32[8,128]{1,0:T(8,128)S(1)}, u32[]{:S(2)}, u32[]{:S(2)}) collective-permute-start(f32[8,128]{1,0:T(8,128)} %get-tuple-element.35), channel_id=1, source_target_pairs={{0,1},{1,2},{2,3},{3,0},{4,5},{5,6},{6,7},{7,4},{8,9},{9,10},{10,1... | collective-permute-start | bytes 12296 | tf_op jit(solution)/shard_map/ppermute | solution.py:28
  62.9 4.5 %collective-permute-start.12 = (f32[8,128]{1,0:T(8,128)}, f32[8,128]{1,0:T(8,128)S(1)}, u32[]{:S(2)}, u32[]{:S(2)}) collective-permute-start(f32[8,128]{1,0:T(8,128)} %get-tuple-element.35), channel_id=1, source_target_pairs={{0,2},{1,3},{2,0},{3,1},{4,6},{5,7},{6,4},{7,5},{8,10},{9,11},{10,... | collective-permute-start | bytes 12296 | tf_op jit(solution)/shard_map/ppermute | solution.py:28
  65.6 3.0 %collective-permute-start.13 = (f32[8,128]{1,0:T(8,128)}, f32[8,128]{1,0:T(8,128)S(1)}, u32[]{:S(2)}, u32[]{:S(2)}) collective-permute-start(f32[8,128]{1,0:T(8,128)} %get-tuple-element.35), channel_id=1, source_target_pairs={{0,3},{1,0},{2,1},{3,2},{4,7},{5,4},{6,5},{7,6},{8,11},{9,8},{10,9... | collective-permute-start | bytes 12296 | tf_op jit(solution)/shard_map/ppermute | solution.py:28
  85.0 34.8 %all-to-all-start.2 = ((f32[16,48,128]{2,1,0:T(8,128)}), f32[16,48,128]{2,1,0:T(8,128)S(1)}, u32[]{:S(2)}, u32[]{:S(2)}) async-start(f32[16,48,128]{2,1,0:T(8,128)} %broadcast_in_dim.5), calls=%async_computation.2 | async-start | bytes 786432 | tf_op jit(solution)/shard_map/all_to_all | solution.py:339
  93.1 12.2 %collective-permute-start.10 = (f32[32,3072]{1,0:T(8,128)S(1)}, f32[32,3072]{1,0:T(8,128)S(1)}, u32[]{:S(2)}, u32[]{:S(2)}) collective-permute-start(f32[32,3072]{1,0:T(8,128)S(1)} %copy-done.10), channel_id=1, source_target_pairs={{0,2},{1,3},{2,0},{3,1},{4,6},{5,7},{6,4},{7,5},{8,10},{9,11},{10,... | collective-permute-start | bytes 1179656 | tf_op jit(solution)/shard_map/ppermute | solution.py:28
  94.2 20.0 %collective-permute-start.8 = (f32[32,3072]{1,0:T(8,128)S(1)}, f32[32,3072]{1,0:T(8,128)S(1)}, u32[]{:S(2)}, u32[]{:S(2)}) collective-permute-start(f32[32,3072]{1,0:T(8,128)S(1)} %copy-done.9), channel_id=1, source_target_pairs={{0,1},{1,2},{2,3},{3,0},{4,5},{5,6},{6,7},{7,4},{8,9},{9,10},{10,1... | collective-permute-start | bytes 1179656 | tf_op jit(solution)/shard_map/ppermute | solution.py:28
  94.5 19.7 %collective-permute-start.9 = (f32[32,3072]{1,0:T(8,128)S(1)}, f32[32,3072]{1,0:T(8,128)S(1)}, u32[]{:S(2)}, u32[]{:S(2)}) collective-permute-start(f32[32,3072]{1,0:T(8,128)S(1)} %copy-done.8), channel_id=1, source_target_pairs={{0,3},{1,0},{2,1},{3,2},{4,7},{5,4},{6,5},{7,6},{8,11},{9,8},{10,9... | collective-permute-start | bytes 1179656 | tf_op jit(solution)/shard_map/ppermute | solution.py:28
  105.3 8.9 %copy-start.5 = (f32[32,3072]{1,0:T(8,128)}, f32[32,3072]{1,0:T(8,128)S(1)}, u32[]{:S(2)}) copy-start(f32[32,3072]{1,0:T(8,128)S(1)} %collective-permute-done.10.from_opp) | copy-start | bytes 1179652
  114.2 0.8 copy-start.6
  114.2 0.9 copy-start.7
  119.8 0.7 copy-start.4

commit v8 on v6

--- a/solution.py
+++ b/solution.py
@@ -27,10 +27,10 @@
     return lax.ppermute(array, axis, [(i, (i + by) % length) for i in range(length)])
 
 
-def to_sides(array, distance):
+def to_sides(array, distance, back=False):
     length = lax.axis_size(WIRE)
     pairs = [((i - distance if i % 2 == 0 else i + distance) % length, i) for i in range(length)]
-    return lax.ppermute(array, WIRE, pairs)
+    return lax.ppermute(array, WIRE, [pair[::-1] for pair in pairs] if back else pairs)
 
 
 def split(x):
@@ -78,6 +78,22 @@
 def group_start(here, by, blk, count):
     start = here + by * blk
     return jnp.where(start >= count, start - count, jnp.where(start < 0, start + count, start))
+
+
+def pack_kernel(cols, asked, st, packed):
+    low = low_half((st.shape[0], LANES))
+    here = cols[0, 0]
+    parity = 1 - here // cols.shape[1] % 2
+
+    def step(m, carry):
+        first = asked[3, 4 * m + parity] - here
+        second = asked[3, 4 * m + 2 + parity] - here
+        packed[:, pl.ds(pl.multiple_of(m * LANES, LANES), LANES)] = jnp.where(
+            low, in_half(tile_at(st, first), first, 0), in_half(tile_at(st, second), second, 1)
+        )
+        return carry
+
+    lax.fori_loop(0, packed.shape[1] // LANES, step, 0, unroll=4)
 
 
 def image_kernel(
@@ -95,7 +111,7 @@
     here = cols[0, 0]
     even = here // blk % 2 == 0
     starts = [group_start(here, by, blk, count) for by in (1, 2, -1, -2)]
-    sources = ((swap, near), (relay, far), (near, swap), (far, relay))
+    beside = ((swap, near), (near, swap))
 
     @pl.when(m == 0)
     def _():
@@ -119,11 +135,14 @@
             index = cols[1, row] - here
             close = in_half(tile_at(st, index), index, 1 - q)
             first = jnp.where(left_half, own, close) if q == 0 else jnp.where(left_half, close, own)
-            beyond = []
-            for slot in range(2):
-                index = cols[2 + slot, row] - starts[2 * q + slot]
-                one, two = (tile_at(ref, index) for ref in sources[2 * q + slot])
-                beyond.append(in_half(jnp.where(even, one, two), index, slot))
+            index = cols[2, row] - starts[2 * q]
+            one, two = (tile_at(ref, index) for ref in beside[q])
+            third = in_half(jnp.where(even, one, two), index, 0)
+            whole = even if q == 0 else jnp.logical_not(even)
+            index = jnp.where(whole, cols[3, row] - starts[2 * q + 1], row // 2)
+            last = tile_at(far, row // 2)
+            last = jnp.where(whole, tile_at(relay, jnp.where(whole, index, 0)), last)
+            beyond = (third, in_half(last, index, 1))
             left.append(jnp.concatenate([first, jnp.where(left_half, *beyond)], axis=1))
             coef = values[(2 * h + q) * BLOCK : (2 * h + q + 1) * BLOCK, :]
             if q:
@@ -266,9 +285,11 @@
 
     before = shifted(st, "col", 1)
     after = shifted(st, "col", -1)
+    asked = to_sides(cols, 2, back=True)
     near = to_sides(st, 1)
-    far = to_sides(st, 2)
     swap = shifted(st, "core", 1)
+    packed = call(pack_kernel, [(width, rows // 2)], [SMEM] * 2 + [VMEM])(cols, asked, st)[0]
+    far = to_sides(packed, 2)
     relay = shifted(near, "core", 1)
 
     opp_a = shifted(before[:half], "col", 1)
@@ -283,7 +304,8 @@
         functools.partial(image_kernel, blk * groups),
         [(width, rows)] * 2 + grams + [(modes, rows)] * 4,
         [SMEM] * 2
-        + [whole] * 5
+        + [whole] * 4
+        + [pl.BlockSpec((width, rows // 2), lambda m: (0, 0))]
         + [pl.BlockSpec((step_lanes, values.shape[1]), lambda m: (m, 0))]
         + [tile(step_lanes)] * 2
         + [VMEM],

time: 123 us -> 128 us (1.041)
  waiting for transfers between devices: 25.9 us -> 35.7 us
  blocking collectives: 14.3 us -> 9.54 us
  starting transfers between devices: 51.7 us -> 48.4 us
  Pallas kernels: 24.1 us -> 26.8 us
    ppermute x12, starting transfers between devices: 35.4 us -> 27.2 us  [shifted(): lax.ppermute(array, axis, [(i, (i + by) % length) for i in range(length)])]
    ppermute x2 -> x3, waiting for transfers between devices: 5.91 us -> 13.7 us  [to_sides(): lax.ppermute(array, WIRE, [pair[::-1] for pair in pairs] if back else pairs)]
    all_to_all x1, blocking collectives: 14.3 us -> 9.54 us  [shards(): part = lax.all_to_all(part, 'zh', 0, 0, tiled=True)]
    all_to_all x1, starting transfers between devices: 4.49 us -> 8.79 us  [shards(): got = lax.all_to_all(payload, RING, 0, 0, tiled=True)]
    pallas_call x0 -> x1, Pallas kernels: none -> 2.66 us  [shards(): call(pack_kernel, [(width, rows // 2)], [SMEM] * 2 + [VMEM])]
    ppermute x12, waiting for transfers between devices: 19.9 us -> 21.7 us  [shifted(): lax.ppermute(array, axis, [(i, (i + by) % length) for i in range(length)])]
    ppermute x2 -> x3, starting transfers between devices: 3.22 us -> 4.4 us  [to_sides(): lax.ppermute(array, WIRE, [pair[::-1] for pair in pairs] if back else pairs)]
    unnamed x22 -> x24, local copies, waits for them, and re-layouts: 2.47 us -> 3.1 us
  transfers between devices with their start and end apart: 16 -> 17, of which waited for: 7 -> 8; matrix products, arithmetic and copies ran while one was open for 2% -> 2% of each run, Pallas kernels for 15% -> 16%
where the time goes in v8:
time: 128 us
  starting transfers between devices  48.4 us (38%)
  waiting for transfers between devices  35.7 us (28%)
  Pallas kernels  26.8 us (21%)
  blocking collectives  9.54 us (7%)
  local copies, waits for them, and re-layouts  5.82 us (5%)
    ppermute x12, starting transfers between devices, shifted(): lax.ppermute(array, axis, [(i, (i + by) % length) for i in range(length)])  27.2 us
    ppermute x12, waiting for transfers between devices, shifted(): lax.ppermute(array, axis, [(i, (i + by) % length) for i in range(length)])  21.7 us
    ppermute x3, waiting for transfers between devices, to_sides(): lax.ppermute(array, WIRE, [pair[::-1] for pair in pairs] if back else pairs)  13.7 us
    pallas_call x1, Pallas kernels, shards(): call(functools.partial(image_kernel, blk * groups), [(width, rows)] * 2 +...  13.2 us
    all_to_all x1, blocking collectives, shards(): part = lax.all_to_all(part, 'zh', 0, 0, tiled=True)  9.54 us
    all_to_all x1, starting transfers between devices, shards(): got = lax.all_to_all(payload, RING, 0, 0, tiled=True)  8.79 us
    all_to_all x1, starting transfers between devices, shards(): parts = lax.all_to_all(spread_out(part), RING, 0, 0, tiled=True)  8.05 us
    pallas_call x1, Pallas kernels, shards(): call(modes_kernel, [(modes, rows)] * 2, [SMEM] + [VMEM] * 10, scratch_sha...  4.77 us
  transfers between devices with their start and end apart: 17, of which 8 were waited for; matrix products, arithmetic and copies ran while one was open for 2% of the time, Pallas kernels for 16%

profile of v8, /device:TPU:1, one launch (start us, length us, event | category | flops | bytes accessed | tf_op | source)
XLA Modules:
  0.0 127.8 jit_solution(1902186213833902197)
XLA Ops:
  0.6 2.8 %collective-permute-start.5 = (f32[96,3072]{1,0:T(8,128)}, f32[96,3072]{1,0:T(8,128)}, u32[]{:S(2)}, u32[]{:S(2)}) collective-permute-start(f32[96,3072]{1,0:T(8,128)} %bitcast.8), channel_id=1, source_target_pairs={{252,0},{8,4},{4,8},{16,12},{12,16},{24,20},{20,24},{32,28},{28,32... | collective-permute-start | bytes 3538952 | tf_op jit(solution)/shard_map/ppermute | solution.py:33
  3.4 1.2 collective-permute-start
  4.6 1.5 %collective-permute-start.1 = (f32[96,3072]{1,0:T(8,128)}, f32[96,3072]{1,0:T(8,128)S(1)}, u32[]{:S(2)}, u32[]{:S(2)}) collective-permute-start(f32[96,3072]{1,0:T(8,128)} %bitcast.10), channel_id=1, source_target_pairs={{0,3},{1,0},{2,1},{3,2},{4,7},{5,4},{6,5},{7,6},{8,11},{9,8},{10,9... | collective-permute-start | bytes 3538952 | tf_op jit(solution)/shard_map/ppermute | solution.py:27
  6.1 7.1 %collective-permute-start.4 = (f32[96,3072]{1,0:T(8,128)}, f32[96,3072]{1,0:T(8,128)}, u32[]{:S(2)}, u32[]{:S(2)}) collective-permute-start(f32[96,3072]{1,0:T(8,128)} %bitcast.11), channel_id=1, source_target_pairs={{0,4},{4,0},{1,5},{5,1},{2,6},{6,2},{3,7},{7,3},{8,12},{12,8},{9,1... | collective-permute-start | bytes 3538952 | tf_op jit(solution)/shard_map/ppermute | solution.py:27
  13.2 4.7 %collective-permute-done.5.near = f32[96,3072]{1,0:T(8,128)} collective-permute-done((f32[96,3072]{1,0:T(8,128)}, f32[96,3072]{1,0:T(8,128)}, u32[]{:S(2)}, u32[]{:S(2)}) %collective-permute-start.5) | collective-permute-done | bytes 1179680 | tf_op jit(solution)/shard_map/ppermute | solution.py:33
  17.9 6.3 %collective-permute-start.6 = (f32[96,3072]{1,0:T(8,128)}, f32[96,3072]{1,0:T(8,128)}, u32[]{:S(2)}, u32[]{:S(2)}) collective-permute-start(f32[96,3072]{1,0:T(8,128)} %collective-permute-done.5.near), channel_id=1, source_target_pairs={{0,4},{4,0},{1,5},{5,1},{2,6},{6,2},{3,7},{7,3},{8,12},{12,8},{9,1... | collective-permute-start | bytes 3538952 | tf_op jit(solution)/shard_map/ppermute | solution.py:27
  24.2 6.0 %collective-permute-done.7.asked = s32[4,48]{1,0:T(4,128)S(1)} collective-permute-done((s32[4,48]{1,0:T(4,128)}, s32[4,48]{1,0:T(4,128)S(1)}, u32[]{:S(2)}, u32[]{:S(2)}) %collective-permute-start.7) | collective-permute-done | bytes 800 | tf_op jit(solution)/shard_map/ppermute | solution.py:33
  30.7 2.7 %shard_map.83 = f32[96,1536]{1,0:T(8,128)} custom-call(s32[4,48]{1,0:T(4,128)} %bitcast.18, s32[4,48]{1,0:T(4,128)} %copy-done.8, f32[96,3072]{1,0:T(8,128)} %bitcast.12), custom_call_target="tpu_custom_call" | custom-call | tf_op jit(solution)/shard_map/pallas_call | solution.py:291
  33.4 1.6 %collective-permute-start.8 = (f32[96,1536]{1,0:T(8,128)}, f32[96,1536]{1,0:T(8,128)}, u32[]{:S(2)}, u32[]{:S(2)}) collective-permute-start(f32[96,1536]{1,0:T(8,128)} %shard_map.83), channel_id=1, source_target_pairs={{248,0},{12,4},{0,8},{20,12},{8,16},{28,20},{16,24},{36,28},{24,32... | collective-permute-start | bytes 1769480 | tf_op jit(solution)/shard_map/ppermute | solution.py:33
  35.0 1.0 slice.8
  36.0 1.2 collective-permute-start.2
  37.2 1.0 slice.9
  38.2 1.5 %collective-permute-start.3 = (f32[48,3072]{1,0:T(8,128)}, f32[48,3072]{1,0:T(8,128)S(1)}, u32[]{:S(2)}, u32[]{:S(2)}) collective-permute-start(f32[48,3072]{1,0:T(8,128)} %slice.9), channel_id=1, source_target_pairs={{0,3},{1,0},{2,1},{3,2},{4,7},{5,4},{6,5},{7,6},{8,11},{9,8},{10,9... | collective-permute-start | bytes 1769480 | tf_op jit(solution)/shard_map/ppermute | solution.py:27
  39.6 3.1 %collective-permute-done.8.far = f32[96,1536]{1,0:T(8,128)} collective-permute-done((f32[96,1536]{1,0:T(8,128)}, f32[96,1536]{1,0:T(8,128)}, u32[]{:S(2)}, u32[]{:S(2)}) %collective-permute-start.8) | collective-permute-done | bytes 589856 | tf_op jit(solution)/shard_map/ppermute | solution.py:33
  42.7 13.2 %shard_map.84 = (bf16[96,3072]{1,0:T(8,128)(2,1)}, bf16[96,3072]{1,0:T(8,128)(2,1)}, f32[3,96,96]{2,1,0:T(8,128)}, f32[1,128]{1,0:T(1,128)}, f32[3,96,96]{2,1,0:...) custom-call(s32[1]{0:T(128)} %bitcast.col, ...), custom_call_target="tpu_custom_call" | custom-call | tf_op jit(solution)/shard_map/pallas_call | solution.py:303
  55.9 0.8 copy-done.2
  56.9 4.1 %shard_map.86 = (f32[16,40,128]{2,1,0:T(8,128)}, f32[8,128]{1,0:T(8,128)}) custom-call(s32[1]{0:T(128)} %bitcast.col, f32[3,96,96]{2,1,0:T(8,128)} %get-tuple-element.28.stiff3, f32[1,128]{1,0:T(1,128)} %get-tuple-element.29.stiff_terms, f32[3,96,96]{2,1,0:T(8,128)} %get-tuple-element.30.mass3, f32[1,128]{1,0:T(1,128)} %get-tuple-element.31.mass_terms, ...), custom_call_target="tpu_custom_call" | custom-call | tf_op jit(solution)/shard_map/pallas_call | solution.py:321
  61.0 8.8 %all-to-all-start = ((f32[16,40,128]{2,1,0:T(8,128)}), f32[16,40,128]{2,1,0:T(8,128)S(1)}, u32[]{:S(2)}, u32[]{:S(2)}) async-start(f32[16,40,128]{2,1,0:T(8,128)} %get-tuple-element.34), calls=%async_computation | async-start | bytes 655360 | tf_op jit(solution)/shard_map/all_to_all | solution.py:328
  69.8 1.3 %collective-permute-start.12 = (f32[8,128]{1,0:T(8,128)}, f32[8,128]{1,0:T(8,128)S(1)}, u32[]{:S(2)}, u32[]{:S(2)}) collective-permute-start(f32[8,128]{1,0:T(8,128)} %get-tuple-element.35), channel_id=1, source_target_pairs={{0,1},{1,2},{2,3},{3,0},{4,5},{5,6},{6,7},{7,4},{8,9},{9,10},{10,1... | collective-permute-start | bytes 12296 | tf_op jit(solution)/shard_map/ppermute | solution.py:27
  71.1 2.4 %collective-permute-start.13 = (f32[8,128]{1,0:T(8,128)}, f32[8,128]{1,0:T(8,128)S(1)}, u32[]{:S(2)}, u32[]{:S(2)}) collective-permute-start(f32[8,128]{1,0:T(8,128)} %get-tuple-element.35), channel_id=1, source_target_pairs={{0,2},{1,3},{2,0},{3,1},{4,6},{5,7},{6,4},{7,5},{8,10},{9,11},{10,... | collective-permute-start | bytes 12296 | tf_op jit(solution)/shard_map/ppermute | solution.py:27
  73.5 1.2 collective-permute-start.14
  74.7 0.9 collective-permute-done.13
  75.6 0.9 collective-permute-done.14
  77.6 9.5 %all_to_all.15 = f32[4,48,128]{2,1,0:T(8,128)S(1)} all-to-all(f32[4,48,128]{2,1,0:T(8,128)S(1)} %broadcast_in_dim.4), channel_id=1, replica_groups=mesh['zh'=4,'zl'=2,'y'=4,'core'=2,'col'=4] {'zh'}, dimensions={0} | all-to-all | bytes 196608 | tf_op jit(solution)/shard_map/all_to_all | solution.py:344
  87.1 0.8 broadcast_in_dim.5
  87.9 8.1 %all-to-all-start.2 = ((f32[16,48,128]{2,1,0:T(8,128)}), f32[16,48,128]{2,1,0:T(8,128)S(1)}, u32[]{:S(2)}, u32[]{:S(2)}) async-start(f32[16,48,128]{2,1,0:T(8,128)} %broadcast_in_dim.5), calls=%async_computation.2 | async-start | bytes 786432 | tf_op jit(solution)/shard_map/all_to_all | solution.py:346
  96.0 2.9 %collective-permute-start.10 = (f32[32,3072]{1,0:T(8,128)S(1)}, f32[32,3072]{1,0:T(8,128)S(1)}, u32[]{:S(2)}, u32[]{:S(2)}) collective-permute-start(f32[32,3072]{1,0:T(8,128)S(1)} %copy-done.11), channel_id=1, source_target_pairs={{0,3},{1,0},{2,1},{3,2},{4,7},{5,4},{6,5},{7,6},{8,11},{9,8},{10,9... | collective-permute-start | bytes 1179656 | tf_op jit(solution)/shard_map/ppermute | solution.py:27
  99.5 16.0 %collective-permute-done.10.from_next = f32[32,3072]{1,0:T(8,128)S(1)} collective-permute-done((f32[32,3072]{1,0:T(8,128)S(1)}, f32[32,3072]{1,0:T(8,128)S(1)}, u32[]{:S(2)}, u32[]{:S(2)}) %collective-permute-start.10) | collective-permute-done | bytes 393248 | tf_op jit(solution)/shard_map/ppermute | solution.py:27
  115.5 3.9 %collective-permute-done.9.from_prev = f32[32,3072]{1,0:T(8,128)S(1)} collective-permute-done((f32[32,3072]{1,0:T(8,128)S(1)}, f32[32,3072]{1,0:T(8,128)S(1)}, u32[]{:S(2)}, u32[]{:S(2)}) %collective-permute-start.9) | collective-permute-done | bytes 393248 | tf_op jit(solution)/shard_map/ppermute | solution.py:27
  119.4 0.8 copy-done.7
  120.2 4.8 %shard_map.85 = (f32[32,3072]{1,0:T(8,128)}, f32[32,3072]{1,0:T(8,128)}) custom-call(s32[1]{0:T(128)} %bitcast.col, f32[96,3072]{1,0:T(8,128)} %bitcast.15, f32[96,3072]{1,0:T(8,128)} %copy-done, f32[96,3072]{1,0:T(8,128)} %copy-done.1, f32[48,3072]{1,0:T(8,128)} %copy-done.2, f32[48,3072]{1,0:T(8,128)} %copy-done.3, f32[384,128]{1,0:T(8,128)} %ritz.5, ...), custom_call_target="tpu_custom_call" | custom-call | tf_op jit(solution)/shard_map/pallas_call | solution.py:333
  125.7 2.1 %shard_map.87 = (f32[96,384]{1,0:T(8,128)}, f32[96,384]{1,0:T(8,128)}, f32[1,32]{1,0:T(1,128)}, f32[32,3072]{1,0:T(8,128)}) custom-call(s32[1]{0:T(128)} %bitcast.col, f32[16,48,128]{2,1,0:T(8,128)} %copy-done.4, f32[32,3072]{1,0:T(8,128)} %get-tuple-element.27.modes, f32[32,3072]{1,0:T(8,128)} %get-tuple-element.36.image), custom_call_target="tpu_custom_call" | custom-call | tf_op jit(solution)/shard_map/pallas_call | solution.py:348
  (40 shorter events, 3.3 us)
Async XLA Ops:
  0.6 17.3 %collective-permute-start.5 = (f32[96,3072]{1,0:T(8,128)}, f32[96,3072]{1,0:T(8,128)}, u32[]{:S(2)}, u32[]{:S(2)}) collective-permute-start(f32[96,3072]{1,0:T(8,128)} %bitcast.8), channel_id=1, source_target_pairs={{252,0},{8,4},{4,8},{16,12},{12,16},{24,20},{20,24},{32,28},{28,32... | collective-permute-start | bytes 3538952 | tf_op jit(solution)/shard_map/ppermute | solution.py:33
  3.4 31.6 %collective-permute-start = (f32[96,3072]{1,0:T(8,128)}, f32[96,3072]{1,0:T(8,128)S(1)}, u32[]{:S(2)}, u32[]{:S(2)}) collective-permute-start(f32[96,3072]{1,0:T(8,128)} %bitcast.9), channel_id=1, source_target_pairs={{0,1},{1,2},{2,3},{3,0},{4,5},{5,6},{6,7},{7,4},{8,9},{9,10},{10,1... | collective-permute-start | bytes 3538952 | tf_op jit(solution)/shard_map/ppermute | solution.py:27
  4.6 32.6 %collective-permute-start.1 = (f32[96,3072]{1,0:T(8,128)}, f32[96,3072]{1,0:T(8,128)S(1)}, u32[]{:S(2)}, u32[]{:S(2)}) collective-permute-start(f32[96,3072]{1,0:T(8,128)} %bitcast.10), channel_id=1, source_target_pairs={{0,3},{1,0},{2,1},{3,2},{4,7},{5,4},{6,5},{7,6},{8,11},{9,8},{10,9... | collective-permute-start | bytes 3538952 | tf_op jit(solution)/shard_map/ppermute | solution.py:27
  6.1 36.6 %collective-permute-start.4 = (f32[96,3072]{1,0:T(8,128)}, f32[96,3072]{1,0:T(8,128)}, u32[]{:S(2)}, u32[]{:S(2)}) collective-permute-start(f32[96,3072]{1,0:T(8,128)} %bitcast.11), channel_id=1, source_target_pairs={{0,4},{4,0},{1,5},{5,1},{2,6},{6,2},{3,7},{7,3},{8,12},{12,8},{9,1... | collective-permute-start | bytes 3538952 | tf_op jit(solution)/shard_map/ppermute | solution.py:27
  17.9 24.8 %collective-permute-start.6 = (f32[96,3072]{1,0:T(8,128)}, f32[96,3072]{1,0:T(8,128)}, u32[]{:S(2)}, u32[]{:S(2)}) collective-permute-start(f32[96,3072]{1,0:T(8,128)} %collective-permute-done.5.near), channel_id=1, source_target_pairs={{0,4},{4,0},{1,5},{5,1},{2,6},{6,2},{3,7},{7,3},{8,12},{12,8},{9,1... | collective-permute-start | bytes 3538952 | tf_op jit(solution)/shard_map/ppermute | solution.py:27
  24.2 6.0 %collective-permute-start.7 = (s32[4,48]{1,0:T(4,128)}, s32[4,48]{1,0:T(4,128)S(1)}, u32[]{:S(2)}, u32[]{:S(2)}) collective-permute-start(s32[4,48]{1,0:T(4,128)} %bitcast.17), channel_id=1, source_target_pairs={{0,248},{4,12},{8,0},{12,20},{16,8},{20,28},{24,16},{28,36},{32,24... | collective-permute-start | bytes 2312 | tf_op jit(solution)/shard_map/ppermute | solution.py:33
  30.1 0.6 copy-start.8
  33.4 9.3 %collective-permute-start.8 = (f32[96,1536]{1,0:T(8,128)}, f32[96,1536]{1,0:T(8,128)}, u32[]{:S(2)}, u32[]{:S(2)}) collective-permute-start(f32[96,1536]{1,0:T(8,128)} %shard_map.83), channel_id=1, source_target_pairs={{248,0},{12,4},{0,8},{20,12},{8,16},{28,20},{16,24},{36,28},{24,32... | collective-permute-start | bytes 1769480 | tf_op jit(solution)/shard_map/ppermute | solution.py:33
  35.0 3.2 %copy-start = (f32[96,3072]{1,0:T(8,128)}, f32[96,3072]{1,0:T(8,128)S(1)}, u32[]{:S(2)}) copy-start(f32[96,3072]{1,0:T(8,128)S(1)} %collective-permute-done.before) | copy-start | bytes 3538948
  36.0 19.9 %collective-permute-start.2 = (f32[48,3072]{1,0:T(8,128)}, f32[48,3072]{1,0:T(8,128)S(1)}, u32[]{:S(2)}, u32[]{:S(2)}) collective-permute-start(f32[48,3072]{1,0:T(8,128)} %slice.8), channel_id=1, source_target_pairs={{0,1},{1,2},{2,3},{3,0},{4,5},{5,6},{6,7},{7,4},{8,9},{9,10},{10,1... | collective-permute-start | bytes 1769480 | tf_op jit(solution)/shard_map/ppermute | solution.py:27
  37.2 5.5 %copy-start.1 = (f32[96,3072]{1,0:T(8,128)}, f32[96,3072]{1,0:T(8,128)S(1)}, u32[]{:S(2)}) copy-start(f32[96,3072]{1,0:T(8,128)S(1)} %collective-permute-done.1.after) | copy-start | bytes 3538948
  38.2 17.7 %collective-permute-start.3 = (f32[48,3072]{1,0:T(8,128)}, f32[48,3072]{1,0:T(8,128)S(1)}, u32[]{:S(2)}, u32[]{:S(2)}) collective-permute-start(f32[48,3072]{1,0:T(8,128)} %slice.9), channel_id=1, source_target_pairs={{0,3},{1,0},{2,1},{3,2},{4,7},{5,4},{6,5},{7,6},{8,11},{9,8},{10,9... | collective-permute-start | bytes 1769480 | tf_op jit(solution)/shard_map/ppermute | solution.py:27
  55.9 0.8 copy-start.2
  55.9 1.0 copy-start.3
  61.0 16.5 %all-to-all-start = ((f32[16,40,128]{2,1,0:T(8,128)}), f32[16,40,128]{2,1,0:T(8,128)S(1)}, u32[]{:S(2)}, u32[]{:S(2)}) async-start(f32[16,40,128]{2,1,0:T(8,128)} %get-tuple-element.34), calls=%async_computation | async-start | bytes 655360 | tf_op jit(solution)/shard_map/all_to_all | solution.py:328
  69.8 26.2 %copy-start.11 = (f32[32,3072]{1,0:T(8,128)S(1)}, f32[32,3072]{1,0:T(8,128)}, u32[]{:S(2)}) copy-start(f32[32,3072]{1,0:T(8,128)} %get-tuple-element.25) | copy-start | bytes 1179652
  69.8 29.1 %copy-start.10 = (f32[32,3072]{1,0:T(8,128)S(1)}, f32[32,3072]{1,0:T(8,128)}, u32[]{:S(2)}) copy-start(f32[32,3072]{1,0:T(8,128)} %get-tuple-element.26) | copy-start | bytes 1179652
  69.8 29.1 %copy-start.9 = (f32[32,3072]{1,0:T(8,128)S(1)}, f32[32,3072]{1,0:T(8,128)}, u32[]{:S(2)}) copy-start(f32[32,3072]{1,0:T(8,128)} %get-tuple-element.24) | copy-start | bytes 1179652
  69.8 4.9 %collective-permute-start.12 = (f32[8,128]{1,0:T(8,128)}, f32[8,128]{1,0:T(8,128)S(1)}, u32[]{:S(2)}, u32[]{:S(2)}) collective-permute-start(f32[8,128]{1,0:T(8,128)} %get-tuple-element.35), channel_id=1, source_target_pairs={{0,1},{1,2},{2,3},{3,0},{4,5},{5,6},{6,7},{7,4},{8,9},{9,10},{10,1... | collective-permute-start | bytes 12296 | tf_op jit(solution)/shard_map/ppermute | solution.py:27
  71.1 4.5 %collective-permute-start.13 = (f32[8,128]{1,0:T(8,128)}, f32[8,128]{1,0:T(8,128)S(1)}, u32[]{:S(2)}, u32[]{:S(2)}) collective-permute-start(f32[8,128]{1,0:T(8,128)} %get-tuple-element.35), channel_id=1, source_target_pairs={{0,2},{1,3},{2,0},{3,1},{4,6},{5,7},{6,4},{7,5},{8,10},{9,11},{10,... | collective-permute-start | bytes 12296 | tf_op jit(solution)/shard_map/ppermute | solution.py:27
  73.5 3.0 %collective-permute-start.14 = (f32[8,128]{1,0:T(8,128)}, f32[8,128]{1,0:T(8,128)S(1)}, u32[]{:S(2)}, u32[]{:S(2)}) collective-permute-start(f32[8,128]{1,0:T(8,128)} %get-tuple-element.35), channel_id=1, source_target_pairs={{0,3},{1,0},{2,1},{3,2},{4,7},{5,4},{6,5},{7,6},{8,11},{9,8},{10,9... | collective-permute-start | bytes 12296 | tf_op jit(solution)/shard_map/ppermute | solution.py:27
  87.9 37.0 %all-to-all-start.2 = ((f32[16,48,128]{2,1,0:T(8,128)}), f32[16,48,128]{2,1,0:T(8,128)S(1)}, u32[]{:S(2)}, u32[]{:S(2)}) async-start(f32[16,48,128]{2,1,0:T(8,128)} %broadcast_in_dim.5), calls=%async_computation.2 | async-start | bytes 786432 | tf_op jit(solution)/shard_map/all_to_all | solution.py:346
  96.0 19.5 %collective-permute-start.10 = (f32[32,3072]{1,0:T(8,128)S(1)}, f32[32,3072]{1,0:T(8,128)S(1)}, u32[]{:S(2)}, u32[]{:S(2)}) collective-permute-start(f32[32,3072]{1,0:T(8,128)S(1)} %copy-done.11), channel_id=1, source_target_pairs={{0,3},{1,0},{2,1},{3,2},{4,7},{5,4},{6,5},{7,6},{8,11},{9,8},{10,9... | collective-permute-start | bytes 1179656 | tf_op jit(solution)/shard_map/ppermute | solution.py:27
  98.8 16.7 %collective-permute-start.11 = (f32[32,3072]{1,0:T(8,128)S(1)}, f32[32,3072]{1,0:T(8,128)S(1)}, u32[]{:S(2)}, u32[]{:S(2)}) collective-permute-start(f32[32,3072]{1,0:T(8,128)S(1)} %copy-done.10), channel_id=1, source_target_pairs={{0,2},{1,3},{2,0},{3,1},{4,6},{5,7},{6,4},{7,5},{8,10},{9,11},{10,... | collective-permute-start | bytes 1179656 | tf_op jit(solution)/shard_map/ppermute | solution.py:27
  98.8 20.5 %collective-permute-start.9 = (f32[32,3072]{1,0:T(8,128)S(1)}, f32[32,3072]{1,0:T(8,128)S(1)}, u32[]{:S(2)}, u32[]{:S(2)}) collective-permute-start(f32[32,3072]{1,0:T(8,128)S(1)} %copy-done.9), channel_id=1, source_target_pairs={{0,1},{1,2},{2,3},{3,0},{4,5},{5,6},{6,7},{7,4},{8,9},{9,10},{10,1... | collective-permute-start | bytes 1179656 | tf_op jit(solution)/shard_map/ppermute | solution.py:27
  115.5 3.9 %copy-start.5 = (f32[32,3072]{1,0:T(8,128)}, f32[32,3072]{1,0:T(8,128)S(1)}, u32[]{:S(2)}) copy-start(f32[32,3072]{1,0:T(8,128)S(1)} %collective-permute-done.10.from_next) | copy-start | bytes 1179652
  115.5 3.9 %copy-start.6 = (f32[32,3072]{1,0:T(8,128)}, f32[32,3072]{1,0:T(8,128)S(1)}, u32[]{:S(2)}) copy-start(f32[32,3072]{1,0:T(8,128)S(1)} %collective-permute-done.11.from_opp) | copy-start | bytes 1179652
  119.4 0.8 copy-start.7
  124.9 0.8 copy-start.4

commit v9 on v8

--- a/solution.py
+++ b/solution.py
@@ -96,16 +96,23 @@
     lax.fori_loop(0, packed.shape[1] // LANES, step, 0, unroll=4)
 
 
+def coef_kernel(values, high, low):
+    for at in range(0, values.shape[0], BLOCK):
+        coef = values[at : at + BLOCK, :]
+        if at // BLOCK % 2:
+            coef = jnp.concatenate([pltpu.roll(coef[:, :LANES], BLOCK, 1), coef[:, LANES:]], axis=1)
+        high[at : at + BLOCK, :], low[at : at + BLOCK, :] = split(coef)
+
+
 def image_kernel(
-    count, col, cols, st, swap, near, relay, far, values, before, after, ritz,
+    count, col, cols, st, swap, near, relay, far, values_high, values_low, before, after, ritz,
     image_high, image_low, stiff, stiff_terms, mass, mass_terms,
     part_own, part_after, part_opp, part_before, stiff_sum, mass_sum, turned
 ):
     m = pl.program_id(0)
     width = st.shape[0]
-    pairs = values.shape[0] // LANES
+    pairs = values_high.shape[0] // LANES
     left_half = low_half((width, LANES))
-    flip = lambda x: pltpu.roll(x, BLOCK, 1)
     images, owns = [], []
     blk = cols.shape[1]
     here = cols[0, 0]
@@ -129,7 +136,7 @@
         tile = m * pairs + h
         own = st[:, pl.ds(pl.multiple_of(tile * LANES, LANES), LANES)]
         owns.append(own)
-        left, right = [], []
+        left = []
         for q in range(2):
             row = 2 * tile + q
             index = cols[1, row] - here
@@ -144,11 +151,10 @@
             last = jnp.where(whole, tile_at(relay, jnp.where(whole, index, 0)), last)
             beyond = (third, in_half(last, index, 1))
             left.append(jnp.concatenate([first, jnp.where(left_half, *beyond)], axis=1))
-            coef = values[(2 * h + q) * BLOCK : (2 * h + q + 1) * BLOCK, :]
-            if q:
-                coef = jnp.concatenate([flip(coef[:, :LANES]), coef[:, LANES:]], axis=1)
-            right.append(coef)
-        part = dot4(split(jnp.concatenate(left, axis=0)), split(jnp.concatenate(right, axis=0)))
+        rows = slice(h * LANES, (h + 1) * LANES)
+        part = dot4(
+            split(jnp.concatenate(left, axis=0)), (values_high[rows, :], values_low[rows, :])
+        )
         images.append(split(4.0 * own + jnp.where(left_half, part[:width], part[width:])))
         if h % 2:
             span = slice((h - 1) * LANES, (h + 1) * LANES)
@@ -292,12 +298,23 @@
     far = to_sides(packed, 2)
     relay = shifted(near, "core", 1)
 
+    step_lanes = PAIRS * LANES
+    depth = values.shape[1]
+    coef_spec = pl.BlockSpec((step_lanes, depth), lambda m: (m, 0))
+    coefs = call(
+        coef_kernel,
+        [(rows, depth)] * 2,
+        [coef_spec],
+        [jnp.bfloat16] * 2,
+        out_specs=[coef_spec] * 2,
+        grid=(rows // step_lanes,),
+    )(values)
+
     opp_a = shifted(before[:half], "col", 1)
     opp_b = shifted(after[half:], "col", -1)
 
     tile = lambda n: pl.BlockSpec((width, n), lambda m: (0, m))
     whole = pl.BlockSpec((width, rows), lambda m: (0, 0))
-    step_lanes = PAIRS * LANES
     grams = [(3, width, width), (1, LANES)] * 2
     gram_specs = [pl.BlockSpec((3, width, width), lambda m: (0, 0, 0)), pl.BlockSpec((1, LANES), lambda m: (0, 0))] * 2
     made = call(
@@ -306,7 +323,7 @@
         [SMEM] * 2
         + [whole] * 4
         + [pl.BlockSpec((width, rows // 2), lambda m: (0, 0))]
-        + [pl.BlockSpec((step_lanes, values.shape[1]), lambda m: (m, 0))]
+        + [coef_spec] * 2
         + [tile(step_lanes)] * 2
         + [VMEM],
         [jnp.bfloat16] * 2 + [F32] * 8,
@@ -315,7 +332,7 @@
         + [pl.BlockSpec((modes, step_lanes), lambda m: (0, m))] * 4,
         grid=(rows // step_lanes,),
         scratch_shapes=[pltpu.VMEM((3 * width, LANES), F32)] * 2 + [pltpu.VMEM((4 * modes, width), F32)],
-    )(col, cols, st, swap, near, relay, far, values, before, after, ritz)
+    )(col, cols, st, swap, near, relay, far, *coefs, before, after, ritz)
     image, grams, (part_own, part_after, part_opp, part_before) = made[:2], made[2:6], made[6:]
 
     payload, terms = call(

time: 128 us -> 129 us (level)
  Pallas kernels: 26.8 us -> 32.1 us
  starting transfers between devices: 48.4 us -> 44.9 us
  waiting for transfers between devices: 35.7 us -> 33.1 us
  blocking collectives: 9.54 us -> 11.4 us
    pallas_call x0 -> x1, Pallas kernels: none -> 5.47 us  [shards(): call(coef_kernel, [(rows, depth)] * 2, [coef_spec], [jnp.bfloat16] * 2, o...]
    ppermute x3, waiting for transfers between devices: 13.7 us -> 10.7 us  [to_sides(): lax.ppermute(array, WIRE, [pair[::-1] for pair in pairs] if back else pairs)]
    all_to_all x1, starting transfers between devices: 8.79 us -> 6.45 us  [shards(): got = lax.all_to_all(payload, RING, 0, 0, tiled=True)]
    all_to_all x1, blocking collectives: 9.54 us -> 11.4 us  [shards(): part = lax.all_to_all(part, 'zh', 0, 0, tiled=True)]
  transfers between devices with their start and end apart: 17 -> 17, of which waited for: 8 -> 7; matrix products, arithmetic and copies ran while one was open for 2% -> 2% of each run, Pallas kernels for 16% -> 20%
where the time goes in v9:
time: 129 us
  starting transfers between devices  44.9 us (35%)
  waiting for transfers between devices  33.1 us (26%)
  Pallas kernels  32.1 us (25%)
  blocking collectives  11.4 us (9%)
  local copies, waits for them, and re-layouts  5.73 us (4%)
    ppermute x12, starting transfers between devices, shifted(): lax.ppermute(array, axis, [(i, (i + by) % length) for i in range(length)])  27.2 us
    ppermute x12, waiting for transfers between devices, shifted(): lax.ppermute(array, axis, [(i, (i + by) % length) for i in range(length)])  22.1 us
    pallas_call x1, Pallas kernels, shards(): call(functools.partial(image_kernel, blk * groups), [(width, rows)] * 2 +...  13 us
    all_to_all x1, blocking collectives, shards(): part = lax.all_to_all(part, 'zh', 0, 0, tiled=True)  11.4 us
    ppermute x3, waiting for transfers between devices, to_sides(): lax.ppermute(array, WIRE, [pair[::-1] for pair in pairs] if back else pairs)  10.7 us
    all_to_all x1, starting transfers between devices, shards(): parts = lax.all_to_all(spread_out(part), RING, 0, 0, tiled=True)  6.81 us
    all_to_all x1, starting transfers between devices, shards(): got = lax.all_to_all(payload, RING, 0, 0, tiled=True)  6.45 us
    pallas_call x1, Pallas kernels, shards(): call(coef_kernel, [(rows, depth)] * 2, [coef_spec], [jnp.bfloat16] * 2, o...  5.47 us
  transfers between devices with their start and end apart: 17, of which 7 were waited for; matrix products, arithmetic and copies ran while one was open for 2% of the time, Pallas kernels for 20%

profile of v9, /device:TPU:1, one launch (start us, length us, event | category | flops | bytes accessed | tf_op | source)
XLA Modules:
  0.0 128.6 jit_solution(9950946225965360937)
XLA Ops:
  0.6 2.8 %collective-permute-start.5 = (f32[96,3072]{1,0:T(8,128)}, f32[96,3072]{1,0:T(8,128)}, u32[]{:S(2)}, u32[]{:S(2)}) collective-permute-start(f32[96,3072]{1,0:T(8,128)} %bitcast.8), channel_id=1, source_target_pairs={{252,0},{8,4},{4,8},{16,12},{12,16},{24,20},{20,24},{32,28},{28,32... | collective-permute-start | bytes 3538952 | tf_op jit(solution)/shard_map/ppermute | solution.py:33
  3.4 1.2 collective-permute-start
  4.6 1.5 %collective-permute-start.1 = (f32[96,3072]{1,0:T(8,128)}, f32[96,3072]{1,0:T(8,128)S(1)}, u32[]{:S(2)}, u32[]{:S(2)}) collective-permute-start(f32[96,3072]{1,0:T(8,128)} %bitcast.10), channel_id=1, source_target_pairs={{0,3},{1,0},{2,1},{3,2},{4,7},{5,4},{6,5},{7,6},{8,11},{9,8},{10,9... | collective-permute-start | bytes 3538952 | tf_op jit(solution)/shard_map/ppermute | solution.py:27
  6.1 7.1 %collective-permute-start.4 = (f32[96,3072]{1,0:T(8,128)}, f32[96,3072]{1,0:T(8,128)}, u32[]{:S(2)}, u32[]{:S(2)}) collective-permute-start(f32[96,3072]{1,0:T(8,128)} %bitcast.11), channel_id=1, source_target_pairs={{0,4},{4,0},{1,5},{5,1},{2,6},{6,2},{3,7},{7,3},{8,12},{12,8},{9,1... | collective-permute-start | bytes 3538952 | tf_op jit(solution)/shard_map/ppermute | solution.py:27
  13.2 4.7 %collective-permute-done.5.near = f32[96,3072]{1,0:T(8,128)} collective-permute-done((f32[96,3072]{1,0:T(8,128)}, f32[96,3072]{1,0:T(8,128)}, u32[]{:S(2)}, u32[]{:S(2)}) %collective-permute-start.5) | collective-permute-done | bytes 1179680 | tf_op jit(solution)/shard_map/ppermute | solution.py:33
  17.9 6.3 %collective-permute-start.6 = (f32[96,3072]{1,0:T(8,128)}, f32[96,3072]{1,0:T(8,128)}, u32[]{:S(2)}, u32[]{:S(2)}) collective-permute-start(f32[96,3072]{1,0:T(8,128)} %collective-permute-done.5.near), channel_id=1, source_target_pairs={{0,4},{4,0},{1,5},{5,1},{2,6},{6,2},{3,7},{7,3},{8,12},{12,8},{9,1... | collective-permute-start | bytes 3538952 | tf_op jit(solution)/shard_map/ppermute | solution.py:27
  24.2 6.0 %collective-permute-done.7.asked = s32[4,48]{1,0:T(4,128)S(1)} collective-permute-done((s32[4,48]{1,0:T(4,128)}, s32[4,48]{1,0:T(4,128)S(1)}, u32[]{:S(2)}, u32[]{:S(2)}) %collective-permute-start.7) | collective-permute-done | bytes 800 | tf_op jit(solution)/shard_map/ppermute | solution.py:33
  30.7 2.7 %shard_map.83 = f32[96,1536]{1,0:T(8,128)} custom-call(s32[4,48]{1,0:T(4,128)} %bitcast.18, s32[4,48]{1,0:T(4,128)} %copy-done.8, f32[96,3072]{1,0:T(8,128)} %bitcast.12), custom_call_target="tpu_custom_call" | custom-call | tf_op jit(solution)/shard_map/pallas_call | solution.py:297
  33.4 1.6 %collective-permute-start.8 = (f32[96,1536]{1,0:T(8,128)}, f32[96,1536]{1,0:T(8,128)}, u32[]{:S(2)}, u32[]{:S(2)}) collective-permute-start(f32[96,1536]{1,0:T(8,128)} %shard_map.83), channel_id=1, source_target_pairs={{248,0},{12,4},{0,8},{20,12},{8,16},{28,20},{16,24},{36,28},{24,32... | collective-permute-start | bytes 1769480 | tf_op jit(solution)/shard_map/ppermute | solution.py:33
  35.0 0.9 slice.8
  35.9 1.2 collective-permute-start.2
  37.2 0.9 slice.9
  38.1 1.5 %collective-permute-start.3 = (f32[48,3072]{1,0:T(8,128)}, f32[48,3072]{1,0:T(8,128)S(1)}, u32[]{:S(2)}, u32[]{:S(2)}) collective-permute-start(f32[48,3072]{1,0:T(8,128)} %slice.9), channel_id=1, source_target_pairs={{0,3},{1,0},{2,1},{3,2},{4,7},{5,4},{6,5},{7,6},{8,11},{9,8},{10,9... | collective-permute-start | bytes 1769480 | tf_op jit(solution)/shard_map/ppermute | solution.py:27
  39.5 5.5 %shard_map.84 = (bf16[3072,256]{1,0:T(8,128)(2,1)}, bf16[3072,256]{1,0:T(8,128)(2,1)}) custom-call(f32[3072,256]{1,0:T(8,128)} %values.1), custom_call_target="tpu_custom_call" | custom-call | tf_op jit(solution)/shard_map/pallas_call | solution.py:304
  45.0 13.0 %shard_map.85 = (bf16[96,3072]{1,0:T(8,128)(2,1)}, bf16[96,3072]{1,0:T(8,128)(2,1)}, f32[3,96,96]{2,1,0:T(8,128)}, f32[1,128]{1,0:T(1,128)}, f32[3,96,96]{2,1,0:...) custom-call(s32[1]{0:T(128)} %bitcast.col, ...), custom_call_target="tpu_custom_call" | custom-call | tf_op jit(solution)/shard_map/pallas_call | solution.py:320
  58.1 0.8 copy-done.2
  59.1 4.0 %shard_map.87 = (f32[16,40,128]{2,1,0:T(8,128)}, f32[8,128]{1,0:T(8,128)}) custom-call(s32[1]{0:T(128)} %bitcast.col, f32[3,96,96]{2,1,0:T(8,128)} %get-tuple-element.32.stiff3, f32[1,128]{1,0:T(1,128)} %get-tuple-element.33.stiff_terms, f32[3,96,96]{2,1,0:T(8,128)} %get-tuple-element.34.mass3, f32[1,128]{1,0:T(1,128)} %get-tuple-element.35.mass_terms, ...), custom_call_target="tpu_custom_call" | custom-call | tf_op jit(solution)/shard_map/pallas_call | solution.py:338
  63.1 6.5 %all-to-all-start = ((f32[16,40,128]{2,1,0:T(8,128)}), f32[16,40,128]{2,1,0:T(8,128)S(1)}, u32[]{:S(2)}, u32[]{:S(2)}) async-start(f32[16,40,128]{2,1,0:T(8,128)} %get-tuple-element.38), calls=%async_computation | async-start | bytes 655360 | tf_op jit(solution)/shard_map/all_to_all | solution.py:345
  69.6 1.3 %collective-permute-start.12 = (f32[8,128]{1,0:T(8,128)}, f32[8,128]{1,0:T(8,128)S(1)}, u32[]{:S(2)}, u32[]{:S(2)}) collective-permute-start(f32[8,128]{1,0:T(8,128)} %get-tuple-element.39), channel_id=1, source_target_pairs={{0,1},{1,2},{2,3},{3,0},{4,5},{5,6},{6,7},{7,4},{8,9},{9,10},{10,1... | collective-permute-start | bytes 12296 | tf_op jit(solution)/shard_map/ppermute | solution.py:27
  70.9 2.4 %collective-permute-start.13 = (f32[8,128]{1,0:T(8,128)}, f32[8,128]{1,0:T(8,128)S(1)}, u32[]{:S(2)}, u32[]{:S(2)}) collective-permute-start(f32[8,128]{1,0:T(8,128)} %get-tuple-element.39), channel_id=1, source_target_pairs={{0,2},{1,3},{2,0},{3,1},{4,6},{5,7},{6,4},{7,5},{8,10},{9,11},{10,... | collective-permute-start | bytes 12296 | tf_op jit(solution)/shard_map/ppermute | solution.py:27
  73.3 1.2 collective-permute-start.14
  74.5 0.9 collective-permute-done.13
  75.4 0.9 collective-permute-done.14
  77.4 11.4 %all_to_all.15 = f32[4,48,128]{2,1,0:T(8,128)S(1)} all-to-all(f32[4,48,128]{2,1,0:T(8,128)S(1)} %broadcast_in_dim.4), channel_id=1, replica_groups=mesh['zh'=4,'zl'=2,'y'=4,'core'=2,'col'=4] {'zh'}, dimensions={0} | all-to-all | bytes 196608 | tf_op jit(solution)/shard_map/all_to_all | solution.py:361
  88.7 0.8 broadcast_in_dim.5
  89.5 6.8 %all-to-all-start.2 = ((f32[16,48,128]{2,1,0:T(8,128)}), f32[16,48,128]{2,1,0:T(8,128)S(1)}, u32[]{:S(2)}, u32[]{:S(2)}) async-start(f32[16,48,128]{2,1,0:T(8,128)} %broadcast_in_dim.5), calls=%async_computation.2 | async-start | bytes 786432 | tf_op jit(solution)/shard_map/all_to_all | solution.py:363
  96.3 2.9 %collective-permute-start.10 = (f32[32,3072]{1,0:T(8,128)S(1)}, f32[32,3072]{1,0:T(8,128)S(1)}, u32[]{:S(2)}, u32[]{:S(2)}) collective-permute-start(f32[32,3072]{1,0:T(8,128)S(1)} %copy-done.11), channel_id=1, source_target_pairs={{0,3},{1,0},{2,1},{3,2},{4,7},{5,4},{6,5},{7,6},{8,11},{9,8},{10,9... | collective-permute-start | bytes 1179656 | tf_op jit(solution)/shard_map/ppermute | solution.py:27
  99.9 16.0 %collective-permute-done.10.from_next = f32[32,3072]{1,0:T(8,128)S(1)} collective-permute-done((f32[32,3072]{1,0:T(8,128)S(1)}, f32[32,3072]{1,0:T(8,128)S(1)}, u32[]{:S(2)}, u32[]{:S(2)}) %collective-permute-start.10) | collective-permute-done | bytes 393248 | tf_op jit(solution)/shard_map/ppermute | solution.py:27
  115.9 4.3 %collective-permute-done.9.from_prev = f32[32,3072]{1,0:T(8,128)S(1)} collective-permute-done((f32[32,3072]{1,0:T(8,128)S(1)}, f32[32,3072]{1,0:T(8,128)S(1)}, u32[]{:S(2)}, u32[]{:S(2)}) %collective-permute-start.9) | collective-permute-done | bytes 393248 | tf_op jit(solution)/shard_map/ppermute | solution.py:27
  120.9 4.8 %shard_map.86 = (f32[32,3072]{1,0:T(8,128)}, f32[32,3072]{1,0:T(8,128)}) custom-call(s32[1]{0:T(128)} %bitcast.col, f32[96,3072]{1,0:T(8,128)} %bitcast.15, f32[96,3072]{1,0:T(8,128)} %copy-done, f32[96,3072]{1,0:T(8,128)} %copy-done.1, f32[48,3072]{1,0:T(8,128)} %copy-done.2, f32[48,3072]{1,0:T(8,128)} %copy-done.3, f32[384,128]{1,0:T(8,128)} %ritz.5, ...), custom_call_target="tpu_custom_call" | custom-call | tf_op jit(solution)/shard_map/pallas_call | solution.py:350
  125.7 0.8 copy-done.4
  126.5 2.1 %shard_map.88 = (f32[96,384]{1,0:T(8,128)}, f32[96,384]{1,0:T(8,128)}, f32[1,32]{1,0:T(1,128)}, f32[32,3072]{1,0:T(8,128)}) custom-call(s32[1]{0:T(128)} %bitcast.col, f32[16,48,128]{2,1,0:T(8,128)} %copy-done.4, f32[32,3072]{1,0:T(8,128)} %get-tuple-element.31.modes, f32[32,3072]{1,0:T(8,128)} %get-tuple-element.40.image), custom_call_target="tpu_custom_call" | custom-call | tf_op jit(solution)/shard_map/pallas_call | solution.py:365
  (41 shorter events, 3.3 us)
Async XLA Ops:
  0.6 17.3 %collective-permute-start.5 = (f32[96,3072]{1,0:T(8,128)}, f32[96,3072]{1,0:T(8,128)}, u32[]{:S(2)}, u32[]{:S(2)}) collective-permute-start(f32[96,3072]{1,0:T(8,128)} %bitcast.8), channel_id=1, source_target_pairs={{252,0},{8,4},{4,8},{16,12},{12,16},{24,20},{20,24},{32,28},{28,32... | collective-permute-start | bytes 3538952 | tf_op jit(solution)/shard_map/ppermute | solution.py:33
  3.4 31.6 %collective-permute-start = (f32[96,3072]{1,0:T(8,128)}, f32[96,3072]{1,0:T(8,128)S(1)}, u32[]{:S(2)}, u32[]{:S(2)}) collective-permute-start(f32[96,3072]{1,0:T(8,128)} %bitcast.9), channel_id=1, source_target_pairs={{0,1},{1,2},{2,3},{3,0},{4,5},{5,6},{6,7},{7,4},{8,9},{9,10},{10,1... | collective-permute-start | bytes 3538952 | tf_op jit(solution)/shard_map/ppermute | solution.py:27
  4.6 32.5 %collective-permute-start.1 = (f32[96,3072]{1,0:T(8,128)}, f32[96,3072]{1,0:T(8,128)S(1)}, u32[]{:S(2)}, u32[]{:S(2)}) collective-permute-start(f32[96,3072]{1,0:T(8,128)} %bitcast.10), channel_id=1, source_target_pairs={{0,3},{1,0},{2,1},{3,2},{4,7},{5,4},{6,5},{7,6},{8,11},{9,8},{10,9... | collective-permute-start | bytes 3538952 | tf_op jit(solution)/shard_map/ppermute | solution.py:27
  6.1 38.9 %collective-permute-start.4 = (f32[96,3072]{1,0:T(8,128)}, f32[96,3072]{1,0:T(8,128)}, u32[]{:S(2)}, u32[]{:S(2)}) collective-permute-start(f32[96,3072]{1,0:T(8,128)} %bitcast.11), channel_id=1, source_target_pairs={{0,4},{4,0},{1,5},{5,1},{2,6},{6,2},{3,7},{7,3},{8,12},{12,8},{9,1... | collective-permute-start | bytes 3538952 | tf_op jit(solution)/shard_map/ppermute | solution.py:27
  17.9 27.1 %collective-permute-start.6 = (f32[96,3072]{1,0:T(8,128)}, f32[96,3072]{1,0:T(8,128)}, u32[]{:S(2)}, u32[]{:S(2)}) collective-permute-start(f32[96,3072]{1,0:T(8,128)} %collective-permute-done.5.near), channel_id=1, source_target_pairs={{0,4},{4,0},{1,5},{5,1},{2,6},{6,2},{3,7},{7,3},{8,12},{12,8},{9,1... | collective-permute-start | bytes 3538952 | tf_op jit(solution)/shard_map/ppermute | solution.py:27
  24.2 6.0 %collective-permute-start.7 = (s32[4,48]{1,0:T(4,128)}, s32[4,48]{1,0:T(4,128)S(1)}, u32[]{:S(2)}, u32[]{:S(2)}) collective-permute-start(s32[4,48]{1,0:T(4,128)} %bitcast.17), channel_id=1, source_target_pairs={{0,248},{4,12},{8,0},{12,20},{16,8},{20,28},{24,16},{28,36},{32,24... | collective-permute-start | bytes 2312 | tf_op jit(solution)/shard_map/ppermute | solution.py:33
  30.1 0.6 copy-start.8
  33.4 11.6 %collective-permute-start.8 = (f32[96,1536]{1,0:T(8,128)}, f32[96,1536]{1,0:T(8,128)}, u32[]{:S(2)}, u32[]{:S(2)}) collective-permute-start(f32[96,1536]{1,0:T(8,128)} %shard_map.83), channel_id=1, source_target_pairs={{248,0},{12,4},{0,8},{20,12},{8,16},{28,20},{16,24},{36,28},{24,32... | collective-permute-start | bytes 1769480 | tf_op jit(solution)/shard_map/ppermute | solution.py:33
  35.0 3.0 %copy-start = (f32[96,3072]{1,0:T(8,128)}, f32[96,3072]{1,0:T(8,128)S(1)}, u32[]{:S(2)}) copy-start(f32[96,3072]{1,0:T(8,128)S(1)} %collective-permute-done.before) | copy-start | bytes 3538948
  35.9 22.1 %collective-permute-start.2 = (f32[48,3072]{1,0:T(8,128)}, f32[48,3072]{1,0:T(8,128)S(1)}, u32[]{:S(2)}, u32[]{:S(2)}) collective-permute-start(f32[48,3072]{1,0:T(8,128)} %slice.8), channel_id=1, source_target_pairs={{0,1},{1,2},{2,3},{3,0},{4,5},{5,6},{6,7},{7,4},{8,9},{9,10},{10,1... | collective-permute-start | bytes 1769480 | tf_op jit(solution)/shard_map/ppermute | solution.py:27
  37.2 7.8 %copy-start.1 = (f32[96,3072]{1,0:T(8,128)}, f32[96,3072]{1,0:T(8,128)S(1)}, u32[]{:S(2)}) copy-start(f32[96,3072]{1,0:T(8,128)S(1)} %collective-permute-done.1.after) | copy-start | bytes 3538948
  38.1 20.0 %collective-permute-start.3 = (f32[48,3072]{1,0:T(8,128)}, f32[48,3072]{1,0:T(8,128)S(1)}, u32[]{:S(2)}, u32[]{:S(2)}) collective-permute-start(f32[48,3072]{1,0:T(8,128)} %slice.9), channel_id=1, source_target_pairs={{0,3},{1,0},{2,1},{3,2},{4,7},{5,4},{6,5},{7,6},{8,11},{9,8},{10,9... | collective-permute-start | bytes 1769480 | tf_op jit(solution)/shard_map/ppermute | solution.py:27
  58.1 0.8 copy-start.2
  58.1 1.0 copy-start.3
  63.1 14.2 %all-to-all-start = ((f32[16,40,128]{2,1,0:T(8,128)}), f32[16,40,128]{2,1,0:T(8,128)S(1)}, u32[]{:S(2)}, u32[]{:S(2)}) async-start(f32[16,40,128]{2,1,0:T(8,128)} %get-tuple-element.38), calls=%async_computation | async-start | bytes 655360 | tf_op jit(solution)/shard_map/all_to_all | solution.py:345
  69.6 26.8 %copy-start.11 = (f32[32,3072]{1,0:T(8,128)S(1)}, f32[32,3072]{1,0:T(8,128)}, u32[]{:S(2)}) copy-start(f32[32,3072]{1,0:T(8,128)} %get-tuple-element.29) | copy-start | bytes 1179652
  69.6 29.6 %copy-start.10 = (f32[32,3072]{1,0:T(8,128)S(1)}, f32[32,3072]{1,0:T(8,128)}, u32[]{:S(2)}) copy-start(f32[32,3072]{1,0:T(8,128)} %get-tuple-element.30) | copy-start | bytes 1179652
  69.6 30.1 %copy-start.9 = (f32[32,3072]{1,0:T(8,128)S(1)}, f32[32,3072]{1,0:T(8,128)}, u32[]{:S(2)}) copy-start(f32[32,3072]{1,0:T(8,128)} %get-tuple-element.28) | copy-start | bytes 1179652
  69.6 4.9 %collective-permute-start.12 = (f32[8,128]{1,0:T(8,128)}, f32[8,128]{1,0:T(8,128)S(1)}, u32[]{:S(2)}, u32[]{:S(2)}) collective-permute-start(f32[8,128]{1,0:T(8,128)} %get-tuple-element.39), channel_id=1, source_target_pairs={{0,1},{1,2},{2,3},{3,0},{4,5},{5,6},{6,7},{7,4},{8,9},{9,10},{10,1... | collective-permute-start | bytes 12296 | tf_op jit(solution)/shard_map/ppermute | solution.py:27
  70.9 4.5 %collective-permute-start.13 = (f32[8,128]{1,0:T(8,128)}, f32[8,128]{1,0:T(8,128)S(1)}, u32[]{:S(2)}, u32[]{:S(2)}) collective-permute-start(f32[8,128]{1,0:T(8,128)} %get-tuple-element.39), channel_id=1, source_target_pairs={{0,2},{1,3},{2,0},{3,1},{4,6},{5,7},{6,4},{7,5},{8,10},{9,11},{10,... | collective-permute-start | bytes 12296 | tf_op jit(solution)/shard_map/ppermute | solution.py:27
  73.3 3.0 %collective-permute-start.14 = (f32[8,128]{1,0:T(8,128)}, f32[8,128]{1,0:T(8,128)S(1)}, u32[]{:S(2)}, u32[]{:S(2)}) collective-permute-start(f32[8,128]{1,0:T(8,128)} %get-tuple-element.39), channel_id=1, source_target_pairs={{0,3},{1,0},{2,1},{3,2},{4,7},{5,4},{6,5},{7,6},{8,11},{9,8},{10,9... | collective-permute-start | bytes 12296 | tf_op jit(solution)/shard_map/ppermute | solution.py:27
  89.5 36.2 %all-to-all-start.2 = ((f32[16,48,128]{2,1,0:T(8,128)}), f32[16,48,128]{2,1,0:T(8,128)S(1)}, u32[]{:S(2)}, u32[]{:S(2)}) async-start(f32[16,48,128]{2,1,0:T(8,128)} %broadcast_in_dim.5), calls=%async_computation.2 | async-start | bytes 786432 | tf_op jit(solution)/shard_map/all_to_all | solution.py:363
  96.3 19.5 %collective-permute-start.10 = (f32[32,3072]{1,0:T(8,128)S(1)}, f32[32,3072]{1,0:T(8,128)S(1)}, u32[]{:S(2)}, u32[]{:S(2)}) collective-permute-start(f32[32,3072]{1,0:T(8,128)S(1)} %copy-done.11), channel_id=1, source_target_pairs={{0,3},{1,0},{2,1},{3,2},{4,7},{5,4},{6,5},{7,6},{8,11},{9,8},{10,9... | collective-permute-start | bytes 1179656 | tf_op jit(solution)/shard_map/ppermute | solution.py:27
  99.2 16.7 %collective-permute-start.11 = (f32[32,3072]{1,0:T(8,128)S(1)}, f32[32,3072]{1,0:T(8,128)S(1)}, u32[]{:S(2)}, u32[]{:S(2)}) collective-permute-start(f32[32,3072]{1,0:T(8,128)S(1)} %copy-done.10), channel_id=1, source_target_pairs={{0,2},{1,3},{2,0},{3,1},{4,6},{5,7},{6,4},{7,5},{8,10},{9,11},{10,... | collective-permute-start | bytes 1179656 | tf_op jit(solution)/shard_map/ppermute | solution.py:27
  99.6 20.5 %collective-permute-start.9 = (f32[32,3072]{1,0:T(8,128)S(1)}, f32[32,3072]{1,0:T(8,128)S(1)}, u32[]{:S(2)}, u32[]{:S(2)}) collective-permute-start(f32[32,3072]{1,0:T(8,128)S(1)} %copy-done.9), channel_id=1, source_target_pairs={{0,1},{1,2},{2,3},{3,0},{4,5},{5,6},{6,7},{7,4},{8,9},{9,10},{10,1... | collective-permute-start | bytes 1179656 | tf_op jit(solution)/shard_map/ppermute | solution.py:27
  115.9 4.3 %copy-start.5 = (f32[32,3072]{1,0:T(8,128)}, f32[32,3072]{1,0:T(8,128)S(1)}, u32[]{:S(2)}) copy-start(f32[32,3072]{1,0:T(8,128)S(1)} %collective-permute-done.10.from_next) | copy-start | bytes 1179652
  115.9 4.3 %copy-start.6 = (f32[32,3072]{1,0:T(8,128)}, f32[32,3072]{1,0:T(8,128)S(1)}, u32[]{:S(2)}) copy-start(f32[32,3072]{1,0:T(8,128)S(1)} %collective-permute-done.11.from_opp) | copy-start | bytes 1179652
  120.2 0.7 copy-start.7
  125.7 0.8 copy-start.4

commit v10 on v9

--- a/solution.py
+++ b/solution.py
@@ -222,6 +222,16 @@
             payload[k, to : to + 8, :] = jnp.zeros((8, LANES), F32)
 
 
+def join_kernel(got, own, next_one, next_two, next_three, out):
+    total = got[0]
+    for k in range(1, got.shape[0]):
+        total = total + got[k]
+    terms = own[...] + next_one[...] + next_two[...] + next_three[...]
+    for k in range(out.shape[0]):
+        out[k, : total.shape[0], :] = total
+        out[k, total.shape[0] :, :] = terms
+
+
 def modes_kernel(
     col, st, before, after, opp_a, opp_b, ritz, own, from_prev, from_next, from_opp, modes, image, turned
 ):
@@ -354,10 +364,7 @@
         scratch_shapes=[pltpu.VMEM((4 * modes, width), F32)],
     )(col, st, before, after, opp_a, opp_b, ritz, part_own, from_prev, from_next, from_opp)
 
-    part = jnp.concatenate(
-        [jnp.sum(got, axis=0), terms + around[0] + around[1] + around[2]], axis=0
-    )
-    part = jnp.broadcast_to(part[None], (4,) + part.shape)
+    part = call(join_kernel, [(4, 8 * TILES + 8, LANES)], [VMEM] * 5)(got, terms, *around)[0]
     part = lax.all_to_all(part, "zh", 0, 0, tiled=True)
     part = jnp.sum(part, axis=0)
     parts = lax.all_to_all(spread_out(part), RING, 0, 0, tiled=True)

time: 129 us -> 131 us (1.016)
  Pallas kernels: 32.1 us -> 33.7 us
    pallas_call x0 -> x1, Pallas kernels: none -> 1.65 us  [shards(): call(join_kernel, [(4, 8 * TILES + 8, LANES)], [VMEM] * 5)]
    unnamed x24 -> x32, local copies, waits for them, and re-layouts: 3.1 us -> 3.83 us
  transfers between devices with their start and end apart: 17 -> 17, of which waited for: 7 -> 8; matrix products, arithmetic and copies ran while one was open for 2% -> 1% of each run, Pallas kernels for 20% -> 20%
where the time goes in v10:
time: 131 us
  starting transfers between devices  44.4 us (34%)
  waiting for transfers between devices  33.9 us (26%)
  Pallas kernels  33.7 us (26%)
  blocking collectives  11.6 us (9%)
  local copies, waits for them, and re-layouts  6.45 us (5%)
    ppermute x12, starting transfers between devices, shifted(): lax.ppermute(array, axis, [(i, (i + by) % length) for i in range(length)])  26.6 us
    ppermute x12, waiting for transfers between devices, shifted(): lax.ppermute(array, axis, [(i, (i + by) % length) for i in range(length)])  22.1 us
    pallas_call x1, Pallas kernels, shards(): call(functools.partial(image_kernel, blk * groups), [(width, rows)] * 2 +...  13 us
    all_to_all x1, blocking collectives, shards(): part = lax.all_to_all(part, 'zh', 0, 0, tiled=True)  11.6 us
    ppermute x3, waiting for transfers between devices, to_sides(): lax.ppermute(array, WIRE, [pair[::-1] for pair in pairs] if back else pairs)  10.7 us
    all_to_all x1, starting transfers between devices, shards(): parts = lax.all_to_all(spread_out(part), RING, 0, 0, tiled=True)  6.83 us
    all_to_all x1, starting transfers between devices, shards(): got = lax.all_to_all(payload, RING, 0, 0, tiled=True)  6.57 us
    pallas_call x1, Pallas kernels, shards(): call(coef_kernel, [(rows, depth)] * 2, [coef_spec], [jnp.bfloat16] * 2, o...  5.46 us
  transfers between devices with their start and end apart: 17, of which 8 were waited for; matrix products, arithmetic and copies ran while one was open for 1% of the time, Pallas kernels for 20%

profile of v10, /device:TPU:1, one launch (start us, length us, event | category | flops | bytes accessed | tf_op | source)
XLA Modules:
  0.0 130.8 jit_solution(9042568676420056387)
XLA Ops:
  0.6 2.8 %collective-permute-start.5 = (f32[96,3072]{1,0:T(8,128)}, f32[96,3072]{1,0:T(8,128)}, u32[]{:S(2)}, u32[]{:S(2)}) collective-permute-start(f32[96,3072]{1,0:T(8,128)} %bitcast.8), channel_id=1, source_target_pairs={{252,0},{8,4},{4,8},{16,12},{12,16},{24,20},{20,24},{32,28},{28,32... | collective-permute-start | bytes 3538952 | tf_op jit(solution)/shard_map/ppermute | solution.py:33
  3.4 1.2 collective-permute-start
  4.6 1.5 %collective-permute-start.1 = (f32[96,3072]{1,0:T(8,128)}, f32[96,3072]{1,0:T(8,128)S(1)}, u32[]{:S(2)}, u32[]{:S(2)}) collective-permute-start(f32[96,3072]{1,0:T(8,128)} %bitcast.10), channel_id=1, source_target_pairs={{0,3},{1,0},{2,1},{3,2},{4,7},{5,4},{6,5},{7,6},{8,11},{9,8},{10,9... | collective-permute-start | bytes 3538952 | tf_op jit(solution)/shard_map/ppermute | solution.py:27
  6.1 7.1 %collective-permute-start.4 = (f32[96,3072]{1,0:T(8,128)}, f32[96,3072]{1,0:T(8,128)}, u32[]{:S(2)}, u32[]{:S(2)}) collective-permute-start(f32[96,3072]{1,0:T(8,128)} %bitcast.11), channel_id=1, source_target_pairs={{0,4},{4,0},{1,5},{5,1},{2,6},{6,2},{3,7},{7,3},{8,12},{12,8},{9,1... | collective-permute-start | bytes 3538952 | tf_op jit(solution)/shard_map/ppermute | solution.py:27
  13.2 4.7 %collective-permute-done.5.near = f32[96,3072]{1,0:T(8,128)} collective-permute-done((f32[96,3072]{1,0:T(8,128)}, f32[96,3072]{1,0:T(8,128)}, u32[]{:S(2)}, u32[]{:S(2)}) %collective-permute-start.5) | collective-permute-done | bytes 1179680 | tf_op jit(solution)/shard_map/ppermute | solution.py:33
  17.9 6.3 %collective-permute-start.6 = (f32[96,3072]{1,0:T(8,128)}, f32[96,3072]{1,0:T(8,128)}, u32[]{:S(2)}, u32[]{:S(2)}) collective-permute-start(f32[96,3072]{1,0:T(8,128)} %collective-permute-done.5.near), channel_id=1, source_target_pairs={{0,4},{4,0},{1,5},{5,1},{2,6},{6,2},{3,7},{7,3},{8,12},{12,8},{9,1... | collective-permute-start | bytes 3538952 | tf_op jit(solution)/shard_map/ppermute | solution.py:27
  24.2 6.0 %collective-permute-done.7.asked = s32[4,48]{1,0:T(4,128)S(1)} collective-permute-done((s32[4,48]{1,0:T(4,128)}, s32[4,48]{1,0:T(4,128)S(1)}, u32[]{:S(2)}, u32[]{:S(2)}) %collective-permute-start.7) | collective-permute-done | bytes 800 | tf_op jit(solution)/shard_map/ppermute | solution.py:33
  30.7 2.6 %shard_map.83 = f32[96,1536]{1,0:T(8,128)} custom-call(s32[4,48]{1,0:T(4,128)} %bitcast.18, s32[4,48]{1,0:T(4,128)} %copy-done.12, f32[96,3072]{1,0:T(8,128)} %bitcast.12), custom_call_target="tpu_custom_call" | custom-call | tf_op jit(solution)/shard_map/pallas_call | solution.py:307
  33.4 1.6 %collective-permute-start.8 = (f32[96,1536]{1,0:T(8,128)}, f32[96,1536]{1,0:T(8,128)}, u32[]{:S(2)}, u32[]{:S(2)}) collective-permute-start(f32[96,1536]{1,0:T(8,128)} %shard_map.83), channel_id=1, source_target_pairs={{248,0},{12,4},{0,8},{20,12},{8,16},{28,20},{16,24},{36,28},{24,32... | collective-permute-start | bytes 1769480 | tf_op jit(solution)/shard_map/ppermute | solution.py:33
  35.0 0.9 slice.8
  35.9 1.2 collective-permute-start.2
  37.1 0.9 slice.9
  38.1 1.5 %collective-permute-start.3 = (f32[48,3072]{1,0:T(8,128)}, f32[48,3072]{1,0:T(8,128)S(1)}, u32[]{:S(2)}, u32[]{:S(2)}) collective-permute-start(f32[48,3072]{1,0:T(8,128)} %slice.9), channel_id=1, source_target_pairs={{0,3},{1,0},{2,1},{3,2},{4,7},{5,4},{6,5},{7,6},{8,11},{9,8},{10,9... | collective-permute-start | bytes 1769480 | tf_op jit(solution)/shard_map/ppermute | solution.py:27
  39.5 5.5 %shard_map.84 = (bf16[3072,256]{1,0:T(8,128)(2,1)}, bf16[3072,256]{1,0:T(8,128)(2,1)}) custom-call(f32[3072,256]{1,0:T(8,128)} %values.1), custom_call_target="tpu_custom_call" | custom-call | tf_op jit(solution)/shard_map/pallas_call | solution.py:314
  45.0 13.0 %shard_map.85 = (bf16[96,3072]{1,0:T(8,128)(2,1)}, bf16[96,3072]{1,0:T(8,128)(2,1)}, f32[3,96,96]{2,1,0:T(8,128)}, f32[1,128]{1,0:T(1,128)}, f32[3,96,96]{2,1,0:...) custom-call(s32[1]{0:T(128)} %bitcast.col, ...), custom_call_target="tpu_custom_call" | custom-call | tf_op jit(solution)/shard_map/pallas_call | solution.py:330
  58.1 0.8 copy-done.2
  59.1 4.0 %shard_map.87 = (f32[16,40,128]{2,1,0:T(8,128)}, f32[8,128]{1,0:T(8,128)}) custom-call(s32[1]{0:T(128)} %bitcast.col, f32[3,96,96]{2,1,0:T(8,128)} %get-tuple-element.32.stiff3, f32[1,128]{1,0:T(1,128)} %get-tuple-element.33.stiff_terms, f32[3,96,96]{2,1,0:T(8,128)} %get-tuple-element.34.mass3, f32[1,128]{1,0:T(1,128)} %get-tuple-element.35.mass_terms, ...), custom_call_target="tpu_custom_call" | custom-call | tf_op jit(solution)/shard_map/pallas_call | solution.py:348
  63.2 6.6 %all-to-all-start = ((f32[16,40,128]{2,1,0:T(8,128)}), f32[16,40,128]{2,1,0:T(8,128)S(1)}, u32[]{:S(2)}, u32[]{:S(2)}) async-start(f32[16,40,128]{2,1,0:T(8,128)} %get-tuple-element.38), calls=%async_computation | async-start | bytes 655360 | tf_op jit(solution)/shard_map/all_to_all | solution.py:355
  69.7 1.2 collective-permute-start.12
  70.9 2.5 %collective-permute-start.13 = (f32[8,128]{1,0:T(8,128)}, f32[8,128]{1,0:T(8,128)S(1)}, u32[]{:S(2)}, u32[]{:S(2)}) collective-permute-start(f32[8,128]{1,0:T(8,128)} %get-tuple-element.39.own), channel_id=1, source_target_pairs={{0,2},{1,3},{2,0},{3,1},{4,6},{5,7},{6,4},{7,5},{8,10},{9,11},{10,... | collective-permute-start | bytes 12296 | tf_op jit(solution)/shard_map/ppermute | solution.py:27
  73.4 1.1 collective-permute-start.14
  75.1 1.3 collective-permute-done.14.next_three
  76.4 1.1 all-to-all-done.got
  78.2 1.6 %shard_map.88 = f32[4,48,128]{2,1,0:T(8,128)} custom-call(f32[16,40,128]{2,1,0:T(8,128)} %copy-done.5, f32[8,128]{1,0:T(8,128)} %get-tuple-element.39.own, f32[8,128]{1,0:T(8,128)} %copy-done.9, f32[8,128]{1,0:T(8,128)} %copy-done.10, f32[8,128]{1,0:T(8,128)} %copy-done.11), custom_call_target="tpu_custom_call" | custom-call | tf_op jit(solution)/shard_map/pallas_call | solution.py:367
  79.9 11.6 %all_to_all.15 = f32[4,48,128]{2,1,0:T(8,128)S(1)} all-to-all(f32[4,48,128]{2,1,0:T(8,128)} %shard_map.88), channel_id=1, replica_groups=mesh['zh'=4,'zl'=2,'y'=4,'core'=2,'col'=4] {'zh'}, dimensions={0} | all-to-all | bytes 196608 | tf_op jit(solution)/shard_map/all_to_all | solution.py:368
  92.2 6.8 %all-to-all-start.2 = ((f32[16,48,128]{2,1,0:T(8,128)}), f32[16,48,128]{2,1,0:T(8,128)S(1)}, u32[]{:S(2)}, u32[]{:S(2)}) async-start(f32[16,48,128]{2,1,0:T(8,128)} %broadcast_in_dim.2), calls=%async_computation.2 | async-start | bytes 786432 | tf_op jit(solution)/shard_map/all_to_all | solution.py:370
  99.1 2.4 %collective-permute-start.10 = (f32[32,3072]{1,0:T(8,128)S(1)}, f32[32,3072]{1,0:T(8,128)S(1)}, u32[]{:S(2)}, u32[]{:S(2)}) collective-permute-start(f32[32,3072]{1,0:T(8,128)S(1)} %copy-done.15), channel_id=1, source_target_pairs={{0,3},{1,0},{2,1},{3,2},{4,7},{5,4},{6,5},{7,6},{8,11},{9,8},{10,9... | collective-permute-start | bytes 1179656 | tf_op jit(solution)/shard_map/ppermute | solution.py:27
  102.1 8.1 %collective-permute-done.10.from_next = f32[32,3072]{1,0:T(8,128)S(1)} collective-permute-done((f32[32,3072]{1,0:T(8,128)S(1)}, f32[32,3072]{1,0:T(8,128)S(1)}, u32[]{:S(2)}, u32[]{:S(2)}) %collective-permute-start.10) | collective-permute-done | bytes 393248 | tf_op jit(solution)/shard_map/ppermute | solution.py:27
  110.2 3.0 %collective-permute-done.11.from_opp = f32[32,3072]{1,0:T(8,128)S(1)} collective-permute-done((f32[32,3072]{1,0:T(8,128)S(1)}, f32[32,3072]{1,0:T(8,128)S(1)}, u32[]{:S(2)}, u32[]{:S(2)}) %collective-permute-start.11) | collective-permute-done | bytes 393248 | tf_op jit(solution)/shard_map/ppermute | solution.py:27
  113.3 9.1 %collective-permute-done.9.from_prev = f32[32,3072]{1,0:T(8,128)S(1)} collective-permute-done((f32[32,3072]{1,0:T(8,128)S(1)}, f32[32,3072]{1,0:T(8,128)S(1)}, u32[]{:S(2)}, u32[]{:S(2)}) %collective-permute-start.9) | collective-permute-done | bytes 393248 | tf_op jit(solution)/shard_map/ppermute | solution.py:27
  123.2 4.7 %shard_map.86 = (f32[32,3072]{1,0:T(8,128)}, f32[32,3072]{1,0:T(8,128)}) custom-call(s32[1]{0:T(128)} %bitcast.col, f32[96,3072]{1,0:T(8,128)} %bitcast.15, f32[96,3072]{1,0:T(8,128)} %copy-done, f32[96,3072]{1,0:T(8,128)} %copy-done.1, f32[48,3072]{1,0:T(8,128)} %copy-done.2, f32[48,3072]{1,0:T(8,128)} %copy-done.3, f32[384,128]{1,0:T(8,128)} %ritz.5, ...), custom_call_target="tpu_custom_call" | custom-call | tf_op jit(solution)/shard_map/pallas_call | solution.py:360
  128.7 2.1 %shard_map.89 = (f32[96,384]{1,0:T(8,128)}, f32[96,384]{1,0:T(8,128)}, f32[1,32]{1,0:T(1,128)}, f32[32,3072]{1,0:T(8,128)}) custom-call(s32[1]{0:T(128)} %bitcast.col, f32[16,48,128]{2,1,0:T(8,128)} %copy-done.4, f32[32,3072]{1,0:T(8,128)} %get-tuple-element.31.modes, f32[32,3072]{1,0:T(8,128)} %get-tuple-element.40.image), custom_call_target="tpu_custom_call" | custom-call | tf_op jit(solution)/shard_map/pallas_call | solution.py:372
  (46 shorter events, 5.1 us)
Async XLA Ops:
  0.6 17.3 %collective-permute-start.5 = (f32[96,3072]{1,0:T(8,128)}, f32[96,3072]{1,0:T(8,128)}, u32[]{:S(2)}, u32[]{:S(2)}) collective-permute-start(f32[96,3072]{1,0:T(8,128)} %bitcast.8), channel_id=1, source_target_pairs={{252,0},{8,4},{4,8},{16,12},{12,16},{24,20},{20,24},{32,28},{28,32... | collective-permute-start | bytes 3538952 | tf_op jit(solution)/shard_map/ppermute | solution.py:33
  3.4 31.6 %collective-permute-start = (f32[96,3072]{1,0:T(8,128)}, f32[96,3072]{1,0:T(8,128)S(1)}, u32[]{:S(2)}, u32[]{:S(2)}) collective-permute-start(f32[96,3072]{1,0:T(8,128)} %bitcast.9), channel_id=1, source_target_pairs={{0,1},{1,2},{2,3},{3,0},{4,5},{5,6},{6,7},{7,4},{8,9},{9,10},{10,1... | collective-permute-start | bytes 3538952 | tf_op jit(solution)/shard_map/ppermute | solution.py:27
  4.6 32.5 %collective-permute-start.1 = (f32[96,3072]{1,0:T(8,128)}, f32[96,3072]{1,0:T(8,128)S(1)}, u32[]{:S(2)}, u32[]{:S(2)}) collective-permute-start(f32[96,3072]{1,0:T(8,128)} %bitcast.10), channel_id=1, source_target_pairs={{0,3},{1,0},{2,1},{3,2},{4,7},{5,4},{6,5},{7,6},{8,11},{9,8},{10,9... | collective-permute-start | bytes 3538952 | tf_op jit(solution)/shard_map/ppermute | solution.py:27
  6.1 38.9 %collective-permute-start.4 = (f32[96,3072]{1,0:T(8,128)}, f32[96,3072]{1,0:T(8,128)}, u32[]{:S(2)}, u32[]{:S(2)}) collective-permute-start(f32[96,3072]{1,0:T(8,128)} %bitcast.11), channel_id=1, source_target_pairs={{0,4},{4,0},{1,5},{5,1},{2,6},{6,2},{3,7},{7,3},{8,12},{12,8},{9,1... | collective-permute-start | bytes 3538952 | tf_op jit(solution)/shard_map/ppermute | solution.py:27
  17.9 27.1 %collective-permute-start.6 = (f32[96,3072]{1,0:T(8,128)}, f32[96,3072]{1,0:T(8,128)}, u32[]{:S(2)}, u32[]{:S(2)}) collective-permute-start(f32[96,3072]{1,0:T(8,128)} %collective-permute-done.5.near), channel_id=1, source_target_pairs={{0,4},{4,0},{1,5},{5,1},{2,6},{6,2},{3,7},{7,3},{8,12},{12,8},{9,1... | collective-permute-start | bytes 3538952 | tf_op jit(solution)/shard_map/ppermute | solution.py:27
  24.2 6.0 %collective-permute-start.7 = (s32[4,48]{1,0:T(4,128)}, s32[4,48]{1,0:T(4,128)S(1)}, u32[]{:S(2)}, u32[]{:S(2)}) collective-permute-start(s32[4,48]{1,0:T(4,128)} %bitcast.17), channel_id=1, source_target_pairs={{0,248},{4,12},{8,0},{12,20},{16,8},{20,28},{24,16},{28,36},{32,24... | collective-permute-start | bytes 2312 | tf_op jit(solution)/shard_map/ppermute | solution.py:33
  33.4 11.6 %collective-permute-start.8 = (f32[96,1536]{1,0:T(8,128)}, f32[96,1536]{1,0:T(8,128)}, u32[]{:S(2)}, u32[]{:S(2)}) collective-permute-start(f32[96,1536]{1,0:T(8,128)} %shard_map.83), channel_id=1, source_target_pairs={{248,0},{12,4},{0,8},{20,12},{8,16},{28,20},{16,24},{36,28},{24,32... | collective-permute-start | bytes 1769480 | tf_op jit(solution)/shard_map/ppermute | solution.py:33
  35.0 3.1 %copy-start = (f32[96,3072]{1,0:T(8,128)}, f32[96,3072]{1,0:T(8,128)S(1)}, u32[]{:S(2)}) copy-start(f32[96,3072]{1,0:T(8,128)S(1)} %collective-permute-done.before) | copy-start | bytes 3538948
  35.9 22.1 %collective-permute-start.2 = (f32[48,3072]{1,0:T(8,128)}, f32[48,3072]{1,0:T(8,128)S(1)}, u32[]{:S(2)}, u32[]{:S(2)}) collective-permute-start(f32[48,3072]{1,0:T(8,128)} %slice.8), channel_id=1, source_target_pairs={{0,1},{1,2},{2,3},{3,0},{4,5},{5,6},{6,7},{7,4},{8,9},{9,10},{10,1... | collective-permute-start | bytes 1769480 | tf_op jit(solution)/shard_map/ppermute | solution.py:27
  37.1 7.9 %copy-start.1 = (f32[96,3072]{1,0:T(8,128)}, f32[96,3072]{1,0:T(8,128)S(1)}, u32[]{:S(2)}) copy-start(f32[96,3072]{1,0:T(8,128)S(1)} %collective-permute-done.1.after) | copy-start | bytes 3538948
  38.1 20.0 %collective-permute-start.3 = (f32[48,3072]{1,0:T(8,128)}, f32[48,3072]{1,0:T(8,128)S(1)}, u32[]{:S(2)}, u32[]{:S(2)}) collective-permute-start(f32[48,3072]{1,0:T(8,128)} %slice.9), channel_id=1, source_target_pairs={{0,3},{1,0},{2,1},{3,2},{4,7},{5,4},{6,5},{7,6},{8,11},{9,8},{10,9... | collective-permute-start | bytes 1769480 | tf_op jit(solution)/shard_map/ppermute | solution.py:27
  58.1 0.8 copy-start.2
  58.1 1.0 copy-start.3
  63.1 35.9 %copy-start.15 = (f32[32,3072]{1,0:T(8,128)S(1)}, f32[32,3072]{1,0:T(8,128)}, u32[]{:S(2)}) copy-start(f32[32,3072]{1,0:T(8,128)} %get-tuple-element.29) | copy-start | bytes 1179652
  63.1 38.3 %copy-start.14 = (f32[32,3072]{1,0:T(8,128)S(1)}, f32[32,3072]{1,0:T(8,128)}, u32[]{:S(2)}) copy-start(f32[32,3072]{1,0:T(8,128)} %get-tuple-element.30) | copy-start | bytes 1179652
  63.2 39.0 %copy-start.13 = (f32[32,3072]{1,0:T(8,128)S(1)}, f32[32,3072]{1,0:T(8,128)}, u32[]{:S(2)}) copy-start(f32[32,3072]{1,0:T(8,128)} %get-tuple-element.28) | copy-start | bytes 1179652
  63.2 14.3 %all-to-all-start = ((f32[16,40,128]{2,1,0:T(8,128)}), f32[16,40,128]{2,1,0:T(8,128)S(1)}, u32[]{:S(2)}, u32[]{:S(2)}) async-start(f32[16,40,128]{2,1,0:T(8,128)} %get-tuple-element.38), calls=%async_computation | async-start | bytes 655360 | tf_op jit(solution)/shard_map/all_to_all | solution.py:355
  69.7 4.8 %collective-permute-start.12 = (f32[8,128]{1,0:T(8,128)}, f32[8,128]{1,0:T(8,128)S(1)}, u32[]{:S(2)}, u32[]{:S(2)}) collective-permute-start(f32[8,128]{1,0:T(8,128)} %get-tuple-element.39.own), channel_id=1, source_target_pairs={{0,1},{1,2},{2,3},{3,0},{4,5},{5,6},{6,7},{7,4},{8,9},{9,10},{10,1... | collective-permute-start | bytes 12296 | tf_op jit(solution)/shard_map/ppermute | solution.py:27
  70.9 4.2 %collective-permute-start.13 = (f32[8,128]{1,0:T(8,128)}, f32[8,128]{1,0:T(8,128)S(1)}, u32[]{:S(2)}, u32[]{:S(2)}) collective-permute-start(f32[8,128]{1,0:T(8,128)} %get-tuple-element.39.own), channel_id=1, source_target_pairs={{0,2},{1,3},{2,0},{3,1},{4,6},{5,7},{6,4},{7,5},{8,10},{9,11},{10,... | collective-permute-start | bytes 12296 | tf_op jit(solution)/shard_map/ppermute | solution.py:27
  73.4 3.0 %collective-permute-start.14 = (f32[8,128]{1,0:T(8,128)}, f32[8,128]{1,0:T(8,128)S(1)}, u32[]{:S(2)}, u32[]{:S(2)}) collective-permute-start(f32[8,128]{1,0:T(8,128)} %get-tuple-element.39.own), channel_id=1, source_target_pairs={{0,3},{1,0},{2,1},{3,2},{4,7},{5,4},{6,5},{7,6},{8,11},{9,8},{10,9... | collective-permute-start | bytes 12296 | tf_op jit(solution)/shard_map/ppermute | solution.py:27
  74.6 2.9 %copy-start.9 = (f32[8,128]{1,0:T(8,128)}, f32[8,128]{1,0:T(8,128)S(1)}, u32[]{:S(2)}) copy-start(f32[8,128]{1,0:T(8,128)S(1)} %collective-permute-done.12.next_one) | copy-start | bytes 12292
  75.1 2.4 %copy-start.10 = (f32[8,128]{1,0:T(8,128)}, f32[8,128]{1,0:T(8,128)S(1)}, u32[]{:S(2)}) copy-start(f32[8,128]{1,0:T(8,128)S(1)} %collective-permute-done.13.next_two) | copy-start | bytes 12292
  76.4 1.1 copy-start.11
  77.5 0.7 copy-start.5
  92.2 35.7 %all-to-all-start.2 = ((f32[16,48,128]{2,1,0:T(8,128)}), f32[16,48,128]{2,1,0:T(8,128)S(1)}, u32[]{:S(2)}, u32[]{:S(2)}) async-start(f32[16,48,128]{2,1,0:T(8,128)} %broadcast_in_dim.2), calls=%async_computation.2 | async-start | bytes 786432 | tf_op jit(solution)/shard_map/all_to_all | solution.py:370
  99.1 11.2 %collective-permute-start.10 = (f32[32,3072]{1,0:T(8,128)S(1)}, f32[32,3072]{1,0:T(8,128)S(1)}, u32[]{:S(2)}, u32[]{:S(2)}) collective-permute-start(f32[32,3072]{1,0:T(8,128)S(1)} %copy-done.15), channel_id=1, source_target_pairs={{0,3},{1,0},{2,1},{3,2},{4,7},{5,4},{6,5},{7,6},{8,11},{9,8},{10,9... | collective-permute-start | bytes 1179656 | tf_op jit(solution)/shard_map/ppermute | solution.py:27
  101.5 11.8 %collective-permute-start.11 = (f32[32,3072]{1,0:T(8,128)S(1)}, f32[32,3072]{1,0:T(8,128)S(1)}, u32[]{:S(2)}, u32[]{:S(2)}) collective-permute-start(f32[32,3072]{1,0:T(8,128)S(1)} %copy-done.14), channel_id=1, source_target_pairs={{0,2},{1,3},{2,0},{3,1},{4,6},{5,7},{6,4},{7,5},{8,10},{9,11},{10,... | collective-permute-start | bytes 1179656 | tf_op jit(solution)/shard_map/ppermute | solution.py:27
  102.1 20.3 %collective-permute-start.9 = (f32[32,3072]{1,0:T(8,128)S(1)}, f32[32,3072]{1,0:T(8,128)S(1)}, u32[]{:S(2)}, u32[]{:S(2)}) collective-permute-start(f32[32,3072]{1,0:T(8,128)S(1)} %copy-done.13), channel_id=1, source_target_pairs={{0,1},{1,2},{2,3},{3,0},{4,5},{5,6},{6,7},{7,4},{8,9},{9,10},{10,1... | collective-permute-start | bytes 1179656 | tf_op jit(solution)/shard_map/ppermute | solution.py:27
  110.2 12.2 %copy-start.6 = (f32[32,3072]{1,0:T(8,128)}, f32[32,3072]{1,0:T(8,128)S(1)}, u32[]{:S(2)}) copy-start(f32[32,3072]{1,0:T(8,128)S(1)} %collective-permute-done.10.from_next) | copy-start | bytes 1179652
  113.3 9.1 %copy-start.7 = (f32[32,3072]{1,0:T(8,128)}, f32[32,3072]{1,0:T(8,128)S(1)}, u32[]{:S(2)}) copy-start(f32[32,3072]{1,0:T(8,128)S(1)} %collective-permute-done.11.from_opp) | copy-start | bytes 1179652
  122.4 0.7 copy-start.8
  127.9 0.7 copy-start.4
  (1 other events, 0.6 us)
